TPU v7x, 32 devices: a whole 2x2x4 slice. The times are simulated.
32 devices in a mesh: groups: 2 (over x), seq: 16 (over z, y, core).
Axes of the slice: x: 2, y: 2, z: 4, core: 2. Of those that a mesh axis runs over, the one named last changes fastest.
Arguments:
- prefill_q: bfloat16 [32, 8192], P(('groups', 'seq')), parts along dimension 0, may hold values from -48 to 48
- cache_k: bfloat16 [16384, 1024], P(('groups', 'seq')), parts along dimension 0, may hold values from -4.5 to 4.5
- cache_v: bfloat16 [16384, 1024], P(('groups', 'seq')), parts along dimension 0, may hold values from -4.5 to 4.5
- page_counts: int32 [32], P('groups'), parts along dimension 0, may hold values from 1 to 64, 768 in all
- page_owner: int32 [2048, 1], P(('groups', 'seq')), parts along dimension 0, may hold values from 0 to 15; in each aligned block of 64 rows (0 to 63, 64 to 127, ...) at most 8 rows name the same one
- decode_q: bfloat16 [32, 2, 8192], P(('groups', 'seq')), parts along dimension 0, may hold values from -48 to 48
- decode_k: bfloat16 [32, 2, 1024], P(('groups', 'seq')), parts along dimension 0, may hold values from -12 to 12
- decode_v: bfloat16 [32, 2, 1024], P(('groups', 'seq')), parts along dimension 0, may hold values from -4.5 to 4.5
- context_len: int32 [32], P(('groups', 'seq')), parts along dimension 0, may hold values from 768 to 6144
Outputs:
- prefill_out: bfloat16 [32, 8192], P(('groups', 'seq')), parts along dimension 0
- decode_out: bfloat16 [32, 2, 8192], P(('groups', 'seq')), parts along dimension 0
- store_k: bfloat16 [32768, 1024], P(('groups', 'seq')), parts along dimension 0
- store_v: bfloat16 [32768, 1024], P(('groups', 'seq')), parts along dimension 0
- store_page: int32 [4096], P(('groups', 'seq')), parts along dimension 0
There are 2 independent parts, one for each index of `groups`. A program takes and returns all parts, laid end to end along the dimension named above; each array names one. Nothing has to cross between parts.
Inputs may be any that keep to these rules, and one draw needn't show every extreme that they name: `page_counts`: the counts sum to 768 and the largest equals 64. `page_owner`: within the 64 page slots of one shard each owner is named at most 8 times, and exactly 8 times in some shards.
All inputs are finite; a program needn't handle non-finite values.
Results may differ from a plain program's by a relative error of at most 0.014.
Values may be sent and summed in bfloat16 or wider, within the bound.
No kernel may reach another device: no remote copies, remote signals or barrier semaphores. Data moves between devices by JAX's collectives and lax.ppermute only.
A program may use at most 128 MiB of HBM per device.

v0:
```python
import jax
import jax.numpy as jnp
from jax import lax
from jax.sharding import PartitionSpec as P

HQ = 64
KVH = 8
HD = 128
PAGE = 8
STEPS = 2
KVD = 1024


MASKED = -1e30


def partial_attend(queries, key_block, value_block, allowed):
    height = queries.shape[0]
    grouping = HQ // KVH
    scaling = HD ** (-0.5)
    start_state = (
        jnp.zeros((height, HQ * HD), jnp.float32),
        jnp.zeros((height, HQ), jnp.float32),
        jnp.zeros((height, HQ), jnp.float32),
    )

    def one_group(member, state):
        weighted, highs, totals = state
        query_group = lax.dynamic_slice_in_dim(
            queries, member * grouping * HD, grouping * HD, 1
        ).reshape(height, grouping, HD)
        key_group = lax.dynamic_slice_in_dim(key_block, member * HD, HD, 1)
        value_group = lax.dynamic_slice_in_dim(value_block, member * HD, HD, 1)
        scores = (
            jnp.einsum("qhd,kd->qhk", query_group, key_group, preferred_element_type=jnp.float32)
            * scaling
        )
        scores = jnp.where(allowed[:, None, :], scores, MASKED)
        highest = jnp.max(scores, axis=2)
        weights = jnp.where(allowed[:, None, :], jnp.exp(scores - highest[:, :, None]), 0.0)
        summed = jnp.sum(weights, axis=2)
        product = jnp.einsum(
            "qhk,kd->qhd",
            weights.astype(jnp.bfloat16),
            value_group,
            preferred_element_type=jnp.float32,
        )
        weighted = lax.dynamic_update_slice_in_dim(
            weighted, product.reshape(height, grouping * HD), member * grouping * HD, 1
        )
        highs = lax.dynamic_update_slice_in_dim(highs, highest, member * grouping, 1)
        totals = lax.dynamic_update_slice_in_dim(totals, summed, member * grouping, 1)
        return (weighted, highs, totals)

    return lax.fori_loop(0, KVH, one_group, start_state)


def combine_parts(pieces):
    weighted, highs, totals = pieces
    sources = highs.shape[0]
    height = highs.shape[1]
    highest = jnp.max(highs, axis=0)
    factor = jnp.exp(highs - highest[None])
    totals = jnp.sum(factor * totals, axis=0)
    weighted = jnp.sum(weighted.reshape(sources, height, HQ, HD) * factor[:, :, :, None], axis=0)
    return (weighted.reshape(height, HQ * HD), highest, totals)


def per_device(
    prefill_q, cache_k, cache_v, page_counts, page_owner, decode_q, decode_k, decode_v, context_len
):
    shards = lax.axis_size("seq")
    myself = lax.axis_index("seq")
    shard_rows = cache_k.shape[0]
    page_slots = shard_rows // PAGE
    capacity = max(2, 2 * page_slots // shards)
    before = jnp.cumsum(page_counts) - page_counts
    my_pages = lax.dynamic_index_in_dim(page_counts, myself, keepdims=False)
    my_start = lax.dynamic_index_in_dim(before, myself, keepdims=False)
    local_row = jnp.arange(shard_rows, dtype=jnp.int32)
    usable = local_row < PAGE * my_pages
    places = PAGE * my_start + local_row
    prompt = PAGE * jnp.sum(page_counts)
    queries = lax.all_gather(prefill_q, "seq", axis=0, tiled=True)
    block_rows = queries.shape[0]
    query_places = prompt - block_rows + jnp.arange(block_rows, dtype=jnp.int32)
    allowed = usable[None, :] & (places[None, :] <= query_places[:, None])
    prefill_parts = partial_attend(queries, cache_k, cache_v, allowed)
    owners = page_owner[:, 0]
    page_index = jnp.arange(page_slots, dtype=jnp.int32)
    page_live = page_index < my_pages
    chosen = owners[:, None] == jnp.arange(shards, dtype=jnp.int32)[None, :]
    chosen_live = (chosen & page_live[:, None]).astype(jnp.int32)
    earlier = jnp.cumsum(chosen_live, axis=0) - chosen_live
    ranking = jnp.sum(earlier * chosen.astype(jnp.int32), axis=1)
    target = jnp.where(page_live, owners * capacity + ranking, shards * capacity)
    source_page = jnp.zeros((shards * capacity,), jnp.int32).at[target].set(page_index, mode="drop")
    filled = jnp.zeros((shards * capacity,), jnp.int32).at[target].set(1, mode="drop") > 0
    outgoing_k = jnp.where(filled[:, None], cache_k.reshape(page_slots, PAGE * KVD)[source_page], 0)
    outgoing_v = jnp.where(filled[:, None], cache_v.reshape(page_slots, PAGE * KVD)[source_page], 0)
    outgoing_ids = jnp.where(filled, myself * page_slots + source_page, -1)
    incoming_k, incoming_v, store_page = (
        lax.all_to_all(outgoing_k, "seq", split_axis=0, concat_axis=0, tiled=True),
        lax.all_to_all(outgoing_v, "seq", split_axis=0, concat_axis=0, tiled=True),
        lax.all_to_all(outgoing_ids, "seq", split_axis=0, concat_axis=0, tiled=True),
    )
    store_k = incoming_k.reshape(-1, KVD)
    store_v = incoming_v.reshape(-1, KVD)
    gathered_q, lengths = (
        lax.all_gather(decode_q, "seq", axis=0, tiled=True),
        lax.all_gather(context_len, "seq", axis=0, tiled=True),
    )
    requests = gathered_q.shape[0]
    query_rows = gathered_q.reshape(requests * STEPS, HQ * HD)
    limits = jnp.repeat(lengths, STEPS)
    page_device = store_page // page_slots
    page_within = store_page % page_slots
    device_hit = (page_device[:, None] == jnp.arange(shards, dtype=jnp.int32)[None, :]).astype(
        jnp.int32
    )
    page_begin = PAGE * (jnp.sum(device_hit * before[None, :], axis=1) + page_within)
    key_places = (page_begin[:, None] + jnp.arange(PAGE, dtype=jnp.int32)[None, :]).reshape(-1)
    key_usable = jnp.repeat(store_page >= 0, PAGE)
    decode_allowed = key_usable[None, :] & (key_places[None, :] < limits[:, None])
    decode_parts = partial_attend(query_rows, store_k, store_v, decode_allowed)

    def by_source(array):
        return array.reshape(shards, array.shape[0] // shards, array.shape[1])

    split_at = block_rows // shards
    joined_sums = jnp.concatenate((by_source(prefill_parts[0]), by_source(decode_parts[0])), axis=1)
    joined_highs = jnp.concatenate(
        (by_source(prefill_parts[1]), by_source(decode_parts[1])), axis=1
    )
    joined_totals = jnp.concatenate(
        (by_source(prefill_parts[2]), by_source(decode_parts[2])), axis=1
    )
    merged = combine_parts(
        (
            lax.all_to_all(joined_sums, "seq", split_axis=0, concat_axis=0, tiled=True),
            lax.all_to_all(joined_highs, "seq", split_axis=0, concat_axis=0, tiled=True),
            lax.all_to_all(joined_totals, "seq", split_axis=0, concat_axis=0, tiled=True),
        )
    )
    prefill_merged = (merged[0][:split_at], merged[1][:split_at], merged[2][:split_at])
    decode_merged = (merged[0][split_at:], merged[1][split_at:], merged[2][split_at:])
    prefill_sums, prefill_high, prefill_totals = prefill_merged
    own_rows = prefill_sums.shape[0]
    prefill_out = (
        (prefill_sums.reshape(own_rows, HQ, HD) / prefill_totals[:, :, None])
        .reshape(own_rows, HQ * HD)
        .astype(jnp.bfloat16)
    )
    weighted, highest, totals = decode_merged
    my_requests = decode_q.shape[0]
    grouping = HQ // KVH
    scaling = HD ** (-0.5)
    own_queries = decode_q.reshape(my_requests, STEPS, KVH, grouping, HD)
    own_keys = decode_k.reshape(my_requests, STEPS, KVH, HD)
    own_values = decode_v.reshape(my_requests, STEPS, KVH, HD)
    own_scores = (
        jnp.einsum("rsghd,rtgd->rsght", own_queries, own_keys, preferred_element_type=jnp.float32)
        * scaling
    )
    causal = jnp.arange(STEPS)[:, None] >= jnp.arange(STEPS)[None, :]
    own_scores = jnp.where(causal[None, :, None, None, :], own_scores, MASKED)
    own_high = jnp.max(own_scores, axis=4).reshape(my_requests * STEPS, HQ)
    overall = jnp.maximum(highest, own_high)
    factor = jnp.exp(highest - overall)
    own_weights = jnp.where(
        causal[None, :, None, None, :],
        jnp.exp(own_scores - overall.reshape(my_requests, STEPS, KVH, grouping)[..., None]),
        0.0,
    )
    totals = totals * factor + jnp.sum(own_weights, axis=4).reshape(my_requests * STEPS, HQ)
    own_product = jnp.einsum(
        "rsght,rtgd->rsghd",
        own_weights.astype(jnp.bfloat16),
        own_values,
        preferred_element_type=jnp.float32,
    )
    weighted = weighted.reshape(my_requests * STEPS, HQ, HD) * factor[
        :, :, None
    ] + own_product.reshape(my_requests * STEPS, HQ, HD)
    decode_out = (
        (weighted / totals[:, :, None]).reshape(my_requests, STEPS, HQ * HD).astype(jnp.bfloat16)
    )
    return (prefill_out, decode_out, store_k, store_v, store_page)


def solution(mesh):
    in_specs = (
        P(("groups", "seq"), None),
        P(("groups", "seq"), None),
        P(("groups", "seq"), None),
        P("groups"),
        P(("groups", "seq"), None),
        P(("groups", "seq"), None, None),
        P(("groups", "seq"), None, None),
        P(("groups", "seq"), None, None),
        P(("groups", "seq")),
    )
    out_specs = (
        P(("groups", "seq"), None),
        P(("groups", "seq"), None, None),
        P(("groups", "seq"), None),
        P(("groups", "seq"), None),
        P(("groups", "seq")),
    )
    return jax.shard_map(
        per_device, mesh=mesh, in_specs=in_specs, out_specs=out_specs, check_vma=False
    )
```

profile of v0, /device:TPU:13, one launch (start us, length us, event | category | flops | bytes accessed | tf_op | source)
XLA Modules:
  0.0 291.6 jit_solution(3598061653722434236)
XLA Ops:
  0.7 1.3 dynamic_slice.67
  3.5 0.8 select_reduce_fusion
  4.3 1.3 fusion.50
  7.9 6.5 %all-to-all-start = ((s32[16,8,1]{1,2,0:T(1,128)}), s32[16,8,1]{1,2,0:T(1,128)S(1)}, u32[]{:S(2)}, u32[]{:S(2)}) async-start(s32[16,8,1]{1,2,0:T(1,128)} %bitcast.10), calls=%async_computation | async-start | bytes 16384 | tf_op jit(solution)/shard_map/all_to_all | solution.py:105
  14.5 1.6 reshape.348
  16.6 3.2 %gather_fusion = bf16[128,8192]{1,0:T(8,128)(2,1)} fusion(bf16[64,8192]{1,0:T(8,128)(2,1)S(1)} %reshape.348, s32[1024]{0:T(1024)S(1)} %pad_clamp_fusion), kind=kCustom, calls=%fused_computation | custom fusion | bytes 4194816 | tf_op jit(solution)/shard_map/gather | solution.py:99
  19.8 3.2 %gather_fusion.1 = bf16[128,8192]{1,0:T(8,128)(2,1)} fusion(bf16[64,8192]{1,0:T(8,128)(2,1)S(1)} %reshape.350, s32[1024]{0:T(1024)S(1)} %pad_clamp_fusion), kind=kCustom, calls=%fused_computation.1 | custom fusion | bytes 4194816 | tf_op jit(solution)/shard_map/gather | solution.py:100
  23.1 4.1 %bitcast_select_fusion = (bf16[16,8,8192]{2,1,0:T(8,128)(2,1)}, bf16[16,8,8192]{2,1,0:T(8,128)(2,1)}) fusion(bf16[128,8192]{1,0:T(8,128)(2,1)} %gather_fusion.1, pred[16,8]{1,0:T(8,128)(4,1)S(1)} %broadcast_in_dim.195, bf16[128,8192]{1,0:T(8,128)(2,1)S(1)} %copy-done.1), kind=kLoop, calls=%fused_computation.45 | loop fusion | flops 2097152 | bytes 8388736 | tf_op jit(solution)/shard_map/jit(_where)/select_n | solution.py:100
  27.2 6.2 %all-to-all-start.1 = ((bf16[16,8,8192]{2,1,0:T(8,128)(2,1)}), bf16[16,8,8192]{2,1,0:T(8,128)(2,1)S(1)}, u32[]{:S(2)}, u32[]{:S(2)}) async-start(bf16[16,8,8192]{2,1,0:T(8,128)(2,1)} %get-tuple-element.510), calls=%async_computation.1 | async-start | bytes 4194304 | tf_op jit(solution)/shard_map/all_to_all | solution.py:103
  36.8 55.6 %all-gather = bf16[16,1,8192]{2,1,0:T(2,128)(2,1)S(1)} all-gather(bf16[1,1,8192]{2,1,0:T(2,128)(2,1)S(1)} %bitcast.166), channel_id=1, replica_groups=mesh['groups'=2,'seq'=16] {'seq'}, dimensions={0}, use_global_device_ids=true | all-gather | bytes 278528 | tf_op jit(solution)/shard_map/all_gather | solution.py:84
  94.7 4.6 %all-to-all-start.2 = ((bf16[16,8,8192]{2,1,0:T(8,128)(2,1)}), bf16[16,8,8192]{2,1,0:T(8,128)(2,1)}, u32[]{:S(2)}, u32[]{:S(2)}) async-start(bf16[16,8,8192]{2,1,0:T(8,128)(2,1)} %get-tuple-element.509), calls=%async_computation.2 | async-start | bytes 4194304 | tf_op jit(solution)/shard_map/all_to_all | solution.py:104
  99.4 25.8 %while.40 = (s32[]{:T(128)}, f32[16,8192]{1,0:T(8,128)S(1)}, f32[16,64]{1,0:T(8,128)S(1)}, f32[16,64]{1,0:T(8,128)S(1)}, bf16[16,8192]{1,0:T(8,128)(2,1)S(1)}, /...) while((s32[]{:T(128)}, f32[16,8192]{1,0:T(8,128)S(1)}, ...), condition=%wide.region_5.6_spmd.clone, body=%wide.region_2.5_spmd.clone.sunk | while | flops 34160392 | bytes 1448831 | solution.py:55
  99.5 1.2 fusion.78
  100.7 1.1 fusion.79
  102.7 1.2 fusion.78
  103.9 1.1 fusion.79
  105.9 1.2 fusion.78
  107.1 1.1 fusion.79
  109.1 1.2 fusion.78
  110.3 1.1 fusion.79
  112.4 1.2 fusion.78
  113.5 1.1 fusion.79
  115.6 1.2 fusion.78
  116.8 1.1 fusion.79
  118.8 1.2 fusion.78
  120.0 1.1 fusion.79
  122.0 1.2 fusion.78
  123.2 1.1 fusion.79
  125.1 19.5 %all-reduce = s32[16]{0:T(128)S(1)} all-reduce(s32[16]{0:T(128)S(1)} %dynamic-update-slice), channel_id=1, replica_groups=mesh['groups'=2,'seq'=16] {'seq'}, use_global_device_ids=true, to_apply=%add | all-reduce | flops 16 | bytes 128
  144.8 20.3 %all_gather.11 = bf16[16,2,8192]{2,1,0:T(2,128)(2,1)S(1)} all-gather(bf16[1,2,8192]{2,1,0:T(2,128)(2,1)S(1)} %copy-done.5), channel_id=1, replica_groups=mesh['groups'=2,'seq'=16] {'seq'}, dimensions={0}, use_global_device_ids=true | all-gather | bytes 557056 | tf_op jit(solution)/shard_map/all_gather | solution.py:110
  165.1 1.0 reshape.347
  166.0 1.3 reshape.346
  169.2 2.3 reshape.349
  171.5 2.9 reshape.351
  174.4 1.1 broadcast_in_dim.189
  175.5 35.4 %while.41 = (s32[]{:T(128)}, f32[32,8192]{1,0:T(8,128)}, f32[32,64]{1,0:T(8,128)S(1)}, f32[32,64]{1,0:T(8,128)S(1)}, bf16[32,8192]{1,0:T(8,128)(2,1)}, /*index=5...) while((s32[]{:T(128)}, f32[32,8192]{1,0:T(8,128)}, ...), condition=%wide.region_14.15_spmd.clone, body=%wide.region_11.14_spmd.clone.sunk | while | flops 136642048 | bytes 4551103 | solution.py:55
  175.5 0.8 dynamic-slice_bitcast_fusion.5
  176.4 1.4 fusion.84
  179.7 0.9 dynamic-slice_bitcast_fusion.5
  180.7 1.4 fusion.84
  184.1 0.9 dynamic-slice_bitcast_fusion.5
  185.1 1.4 fusion.84
  188.6 0.9 dynamic-slice_bitcast_fusion.5
  189.6 1.4 fusion.84
  193.1 0.9 dynamic-slice_bitcast_fusion.5
  194.0 1.4 fusion.84
  197.5 0.9 dynamic-slice_bitcast_fusion.5
  198.5 1.4 fusion.84
  202.0 0.9 dynamic-slice_bitcast_fusion.5
  202.9 1.4 fusion.84
  206.4 0.9 dynamic-slice_bitcast_fusion.5
  207.4 1.4 fusion.84
  210.9 0.9 reshape.429
  211.8 7.9 %all-to-all-start.4 = ((f32[16,1,192]{2,1,0:T(1,128)}), f32[16,1,192]{2,1,0:T(1,128)S(1)}, u32[]{:S(2)}, u32[]{:S(2)}) async-start(f32[16,1,192]{2,1,0:T(1,128)} %reshape.429), calls=%async_computation.4 | async-start | bytes 32768 | tf_op jit(solution)/shard_map/all_to_all | solution.py:141
  220.4 1.8 reshape.352
  222.3 1.6 all-to-all-done.4
  223.9 5.8 %all-to-all-start.5 = ((f32[16,1,192]{2,1,0:T(1,128)}), f32[16,1,192]{2,1,0:T(1,128)S(1)}, u32[]{:S(2)}, u32[]{:S(2)}) async-start(f32[16,1,192]{2,1,0:T(1,128)} %reshape.431), calls=%async_computation.5 | async-start | bytes 32768 | tf_op jit(solution)/shard_map/all_to_all | solution.py:142
  229.7 3.3 %pad_maximum_fusion = f32[16,3,8192]{2,1,0:T(4,128)} fusion(f32[16,2,8192]{2,1,0:T(2,128)S(1)} %reshape.352, f32[16,1,8192]{2,1,0:T(1,128)} %reshape.346), kind=kLoop, calls=%fused_computation.44 | loop fusion | flops 393216 | bytes 3145728 | tf_op jit(solution)/shard_map/concatenate | solution.py:131
  233.0 0.8 all-to-all-done.5
  233.8 6.0 %all-to-all-start.3 = ((f32[16,3,8192]{2,1,0:T(4,128)}), f32[16,3,8192]{2,1,0:T(4,128)S(1)}, u32[]{:S(2)}, u32[]{:S(2)}) async-start(f32[16,3,8192]{2,1,0:T(4,128)} %pad_maximum_fusion), calls=%async_computation.3 | async-start | bytes 4194304 | tf_op jit(solution)/shard_map/all_to_all | solution.py:140
  242.7 1.7 mul.187
  244.3 2.6 mul.188
  247.3 40.0 %all-to-all-done.3 = f32[16,3,8192]{2,1,0:T(4,128)S(1)} async-done(((f32[16,3,8192]{2,1,0:T(4,128)}), f32[16,3,8192]{2,1,0:T(4,128)S(1)}, u32[]{:S(2)}, u32[]{:S(2)}) %all-to-all-start.3) | async-done | bytes 1572896 | tf_op jit(solution)/shard_map/all_to_all | solution.py:140
  287.3 2.9 fusion.34
  (208 shorter events, 38.5 us)
Async XLA Ops:
  0.6 246.3 %copy-start = (bf16[1,2,1024]{2,1,0:T(2,128)(2,1)S(1)}, bf16[1,2,1024]{2,1,0:T(2,128)(2,1)}, u32[]{:S(2)}) copy-start(bf16[1,2,1024]{2,1,0:T(2,128)(2,1)} %param.20) | copy-start | bytes 12292
  0.6 15.4 %copy-start.3 = (bf16[512,1024]{1,0:T(8,128)(2,1)S(1)}, bf16[512,1024]{1,0:T(8,128)(2,1)}, u32[]{:S(2)}) copy-start(bf16[512,1024]{1,0:T(8,128)(2,1)} %param.15) | copy-start | bytes 3145732
  7.9 19.3 %all-to-all-start = ((s32[16,8,1]{1,2,0:T(1,128)}), s32[16,8,1]{1,2,0:T(1,128)S(1)}, u32[]{:S(2)}, u32[]{:S(2)}) async-start(s32[16,8,1]{1,2,0:T(1,128)} %bitcast.10), calls=%async_computation | async-start | bytes 16384 | tf_op jit(solution)/shard_map/all_to_all | solution.py:105
  19.8 3.3 %copy-start.1 = (bf16[128,8192]{1,0:T(8,128)(2,1)S(1)}, bf16[128,8192]{1,0:T(8,128)(2,1)}, u32[]{:S(2)}) copy-start(bf16[128,8192]{1,0:T(8,128)(2,1)} %gather_fusion) | copy-start | bytes 6291460
  27.2 6.2 %copy-start.6 = (s32[16]{0:T(128)S(1)}, s32[16]{0:T(128)}, u32[]{:S(2)}) copy-start(s32[16]{0:T(128)} %param.16) | copy-start | bytes 196
  27.2 9.6 %copy-start.4 = (bf16[1,8192]{1,0:T(2,128)(2,1)S(1)}, bf16[1,8192]{1,0:T(2,128)(2,1)}, u32[]{:S(2)}) copy-start(bf16[1,8192]{1,0:T(2,128)(2,1)} %param.13) | copy-start | bytes 49156
  27.2 65.5 %copy-start.9 = (u32[32]{0:T(128)S(1)}, u32[32]{0:T(128)}, u32[]{:S(2)}) copy-start(u32[32]{0:T(128)} %constant.304) | copy-start | bytes 388
  27.2 67.5 %all-to-all-start.1 = ((bf16[16,8,8192]{2,1,0:T(8,128)(2,1)}), bf16[16,8,8192]{2,1,0:T(8,128)(2,1)S(1)}, u32[]{:S(2)}, u32[]{:S(2)}) async-start(bf16[16,8,8192]{2,1,0:T(8,128)(2,1)} %get-tuple-element.510), calls=%async_computation.1 | async-start | bytes 4194304 | tf_op jit(solution)/shard_map/all_to_all | solution.py:103
  94.7 76.8 %all-to-all-start.2 = ((bf16[16,8,8192]{2,1,0:T(8,128)(2,1)}), bf16[16,8,8192]{2,1,0:T(8,128)(2,1)}, u32[]{:S(2)}, u32[]{:S(2)}) async-start(bf16[16,8,8192]{2,1,0:T(8,128)(2,1)} %get-tuple-element.509), calls=%async_computation.2 | async-start | bytes 4194304 | tf_op jit(solution)/shard_map/all_to_all | solution.py:104
  99.3 45.4 %copy-start.5 = (bf16[1,2,8192]{2,1,0:T(2,128)(2,1)S(1)}, bf16[1,2,8192]{2,1,0:T(2,128)(2,1)}, u32[]{:S(2)}) copy-start(bf16[1,2,8192]{2,1,0:T(2,128)(2,1)} %param.18) | copy-start | bytes 98308
  168.6 2.9 copy-start.7
  210.8 22.2 %copy-start.2 = (bf16[1024,1024]{1,0:T(8,128)(2,1)}, bf16[1024,1024]{1,0:T(8,128)(2,1)S(1)}, u32[]{:S(2)}) copy-start(bf16[1024,1024]{1,0:T(8,128)(2,1)S(1)} %get-tuple-element.754) | copy-start | bytes 6291460
  211.8 12.1 %all-to-all-start.4 = ((f32[16,1,192]{2,1,0:T(1,128)}), f32[16,1,192]{2,1,0:T(1,128)S(1)}, u32[]{:S(2)}, u32[]{:S(2)}) async-start(f32[16,1,192]{2,1,0:T(1,128)} %reshape.429), calls=%async_computation.4 | async-start | bytes 32768 | tf_op jit(solution)/shard_map/all_to_all | solution.py:141
  223.9 10.0 %all-to-all-start.5 = ((f32[16,1,192]{2,1,0:T(1,128)}), f32[16,1,192]{2,1,0:T(1,128)S(1)}, u32[]{:S(2)}, u32[]{:S(2)}) async-start(f32[16,1,192]{2,1,0:T(1,128)} %reshape.431), calls=%async_computation.5 | async-start | bytes 32768 | tf_op jit(solution)/shard_map/all_to_all | solution.py:142
  233.0 6.8 %copy-start.8 = (bf16[1,2,1024]{2,1,0:T(2,128)(2,1)S(1)}, bf16[1,2,1024]{2,1,0:T(2,128)(2,1)}, u32[]{:S(2)}) copy-start(bf16[1,2,1024]{2,1,0:T(2,128)(2,1)} %param.19) | copy-start | bytes 12292
  233.8 53.4 %all-to-all-start.3 = ((f32[16,3,8192]{2,1,0:T(4,128)}), f32[16,3,8192]{2,1,0:T(4,128)S(1)}, u32[]{:S(2)}, u32[]{:S(2)}) async-start(f32[16,3,8192]{2,1,0:T(4,128)} %pad_maximum_fusion), calls=%async_computation.3 | async-start | bytes 4194304 | tf_op jit(solution)/shard_map/all_to_all | solution.py:140
where the time goes:
time: 293 us; the launch traced here: 292 us
  blocking collectives  95.3 us (33%)
  local copies, waits for them, and re-layouts  54 us (18%)
  waiting for transfers between devices  42.4 us (14%)
  starting transfers between devices  37 us (13%)
  matrix products  33.5 us (11%)
  other arithmetic  24.9 us (8%)
  between operations  3.66 us (1%)
    all_gather x1, blocking collectives, per_device(): queries = lax.all_gather(prefill_q, 'seq', axis=0, tiled=True)  55.6 us
    all_to_all x1, waiting for transfers between devices, per_device(): lax.all_to_all(joined_sums, 'seq', split_axis=0, concat_axis=0, tiled=True)  40 us
    dot_general x16, matrix products, one_group(): jnp.einsum('qhd,kd->qhk', query_group, key_group, preferred_element_type=...  20.6 us
    all_gather x1, blocking collectives, per_device(): lax.all_gather(decode_q, 'seq', axis=0, tiled=True)  20.3 us
    unnamed x1, blocking collectives  19.5 us
    dot_general x16, matrix products, one_group(): jnp.einsum('qhk,kd->qhd', weights.astype(jnp.bfloat16), value_group, pref...  12.3 us
    all_to_all x1, starting transfers between devices, per_device(): lax.all_to_all(joined_highs, 'seq', split_axis=0, concat_axis=0, tiled=True)  7.89 us
    while x32, local copies, waits for them, and re-layouts  7 us
  transfers between devices with their start and end apart: 6, of which 3 were waited for; matrix products, arithmetic and copies ran while one was open for 21% of the time, Pallas kernels for 0%

commit v1 on v0

v1 whole, which is shorter than its diff:
```python
import functools
import jax
import jax.numpy as jnp
from jax import lax
from jax.experimental import pallas as pl
from jax.experimental.pallas import tpu as pltpu
from jax.sharding import PartitionSpec as P

HQ = 64
KVH = 8
HD = 128
PAGE = 8
STEPS = 2
KVD = 1024
GRP = HQ // KVH
MASKED = -1e30
VMEM = pltpu.MemorySpace.VMEM
SMEM = pltpu.MemorySpace.SMEM
LIMIT = 48 * 1024 * 1024


def whole(space):
    return pl.BlockSpec(memory_space=space)


def message_kernel(rows_p, rows_d, length, prefill_q, decode_q, owners, out, rows):
    for r in range(rows_p + rows_d):
        ref, at = (prefill_q, r) if r < rows_p else (decode_q, r - rows_p)
        line = ref[at : at + 1, :].astype(jnp.float32)
        for h in range(HQ):
            rows[r * HQ + h : r * HQ + h + 1, :] = line[:, h * HD : (h + 1) * HD]
    base = (rows_p + rows_d) * HQ
    slots = owners.shape[1]
    rows[base : base + 8, :] = jnp.zeros((8, 128), jnp.float32)
    rows[base : base + 1, 0:slots] = owners[...].astype(jnp.float32)
    lane = lax.broadcasted_iota(jnp.int32, (1, 128), 1)
    digits = jnp.zeros((1, 128), jnp.int32)
    for q in range(length.shape[0]):
        value = length[q]
        digits = jnp.where(lane == 2 * q, value // 256, digits)
        digits = jnp.where(lane == 2 * q + 1, value % 256, digits)
    rows[base + 1 : base + 2, :] = digits.astype(jnp.float32)
    out[...] = rows[...].reshape(out.shape).astype(jnp.bfloat16)


def make_message(prefill_q, decode_q, page_owner, context_len):
    rows_p = prefill_q.shape[0]
    rows_d = decode_q.shape[0] * STEPS
    blocks = (rows_p + rows_d) * KVH + 1
    return pl.pallas_call(
        functools.partial(message_kernel, rows_p, rows_d),
        out_shape=jax.ShapeDtypeStruct((blocks, 8, 128), jnp.bfloat16),
        in_specs=[whole(SMEM), whole(VMEM), whole(VMEM), whole(VMEM)],
        out_specs=whole(VMEM),
        scratch_shapes=[pltpu.VMEM((blocks * 8, 128), jnp.float32)],
        name="message",
    )(context_len, prefill_q, decode_q.reshape(rows_d, HQ * HD), page_owner.reshape(1, -1))


def pack_kernel(shards, capacity, owners, counts, pages, out, held, blank, taken, sem_in, sem_out):
    me = lax.axis_index("seq")
    fetch = pltpu.make_async_copy(pages, held, sem_in)
    fetch.start()
    blank[...] = jnp.zeros_like(blank)

    def reset(o, carry):
        taken[o] = 0
        return carry

    lax.fori_loop(0, shards, reset, 0)
    fetch.wait()

    def place(j, carry):
        o = owners[j]
        k = taken[o]
        taken[o] = k + 1
        pltpu.make_async_copy(held.at[j], out.at[o * capacity + k], sem_out).start()
        return carry

    lax.fori_loop(0, counts[me], place, 0)

    def fill(o, carry):
        def one(k, inner):
            pltpu.make_async_copy(blank, out.at[o * capacity + k], sem_out).start()
            return inner

        return lax.fori_loop(taken[o], capacity, one, carry)

    lax.fori_loop(0, shards, fill, 0)
    pltpu.make_async_copy(out, out, sem_out).wait()


def pack(owners, counts, pages, shards, capacity):
    slots = pages.shape[0]
    return pl.pallas_call(
        functools.partial(pack_kernel, shards, capacity),
        out_shape=jax.ShapeDtypeStruct((shards * capacity, PAGE, KVD), pages.dtype),
        in_specs=[whole(SMEM), whole(SMEM), whole(pl.ANY)],
        out_specs=whole(pl.ANY),
        scratch_shapes=[
            pltpu.VMEM((slots, PAGE, KVD), pages.dtype),
            pltpu.VMEM((PAGE, KVD), pages.dtype),
            pltpu.SMEM((shards,), jnp.int32),
            pltpu.SemaphoreType.DMA,
            pltpu.SemaphoreType.DMA,
        ],
        cost_estimate=pl.CostEstimate(
            flops=0, transcendentals=0, bytes_accessed=(slots + shards * capacity) * PAGE * KVD * 2
        ),
        name="pack",
    )(owners, counts, pages)


def attend_kernel(
    rows_p, rows_d, capacity, counts, message, keys, values, out, table, limits, stats, hits
):
    me = lax.axis_index("seq")
    shards = message.shape[0]
    rows = rows_p + rows_d
    height = shards * rows * GRP
    held = keys.shape[0]

    def count(d, carry):
        before, total = carry
        here = counts[d]
        return (before + jnp.where(d < me, here, 0), total + here)

    before, total = lax.fori_loop(0, shards, count, (jnp.int32(0), jnp.int32(0)))
    start = PAGE * before
    live = PAGE * counts[me]
    first = PAGE * total - shards * rows_p + 1
    lane = lax.broadcasted_iota(jnp.int32, (1, 128), 1)
    last = rows * KVH
    for d in range(shards):
        tail = message[d, last].astype(jnp.float32)
        for r in range(rows):
            at = (d * rows + r) * GRP
            if r < rows_p:
                bound = jnp.minimum(first + d * rows_p + r - start, live)
                limits[at : at + GRP, :] = jnp.full((GRP, 128), bound, jnp.int32)
            else:
                q = (r - rows_p) // STEPS
                length = tail[1:2, 2 * q : 2 * q + 1] * 256.0 + tail[1:2, 2 * q + 1 : 2 * q + 2]
                bound = jnp.minimum(length.astype(jnp.int32) - start, live)
                limits[at : at + GRP, :] = jnp.broadcast_to(bound, (GRP, 128))
        hit = (tail[0:1, :].astype(jnp.int32) == me) & (lane < counts[d])
        hits[d : d + 1, :] = hit.astype(jnp.float32)

    hit = hits[...]
    earlier = (
        lax.broadcasted_iota(jnp.int32, (128, 128), 0)
        < lax.broadcasted_iota(jnp.int32, (128, 128), 1)
    ).astype(jnp.bfloat16)
    rank = jnp.dot(hit.astype(jnp.bfloat16), earlier, preferred_element_type=jnp.float32)
    wide = lax.broadcasted_iota(jnp.int32, hit.shape, 1)
    depth = lax.broadcasted_iota(jnp.int32, hit.shape, 0)
    numbered = jnp.zeros(hit.shape, jnp.float32)
    for k in range(capacity):
        match = jnp.where((hit > 0.5) & (rank == float(k)), (wide + 1).astype(jnp.float32), 0.0)
        found = jnp.sum(match, axis=1, keepdims=True)
        numbered = jnp.where(wide == k, found, numbered)
    within = numbered.astype(jnp.int32)
    slots = held // PAGE
    table[...] = jnp.where(within > 0, depth * slots + within - 1, -1)

    stats[...] = jnp.zeros_like(stats)
    spot = lax.broadcasted_iota(jnp.int32, (height, 128), 1)
    column = lax.broadcasted_iota(jnp.int32, (height, held), 1)

    def one_group(g, carry):
        query = jnp.concatenate(
            [
                message[d, r * KVH + g].astype(jnp.float32)
                for d in range(shards)
                for r in range(rows)
            ],
            axis=0,
        ).astype(jnp.bfloat16)
        across = pl.ds(pl.multiple_of(g * HD, HD), HD)
        scores = lax.dot_general(
            query, keys[:, across], (((1,), (1,)), ((), ())), preferred_element_type=jnp.float32
        ) * (HD ** (-0.5))
        allowed = column < jnp.concatenate([limits[...]] * (held // 128), axis=1)
        scores = jnp.where(allowed, scores, MASKED)
        high = jnp.max(scores, axis=1, keepdims=True).astype(jnp.bfloat16).astype(jnp.float32)
        weights = jnp.where(allowed, jnp.exp(scores - high), 0.0)
        total = jnp.sum(weights, axis=1, keepdims=True)
        product = jnp.dot(
            weights.astype(jnp.bfloat16), values[:, across], preferred_element_type=jnp.float32
        )
        coarse = total.astype(jnp.bfloat16).astype(jnp.float32)
        kept = jnp.where(spot == g, high, stats[...])
        kept = jnp.where(spot == KVH + g, coarse, kept)
        stats[...] = jnp.where(spot == 2 * KVH + g, total - coarse, kept)
        for d in range(shards):
            for r in range(rows):
                at = (d * rows + r) * GRP
                out[d, r * KVH + g] = product[at : at + GRP, :].astype(jnp.bfloat16)
        return carry

    lax.fori_loop(0, KVH, one_group, 0)
    for d in range(shards):
        for r in range(rows):
            at = (d * rows + r) * GRP
            out[d, rows * KVH + r] = stats[at : at + GRP, :].astype(jnp.bfloat16)


def attend(rows_p, rows_d, capacity, counts, message, keys, values):
    shards = message.shape[0]
    rows = rows_p + rows_d
    height = shards * rows * GRP
    held = keys.shape[0]
    return pl.pallas_call(
        functools.partial(attend_kernel, rows_p, rows_d, capacity),
        out_shape=(
            jax.ShapeDtypeStruct((shards, rows * (KVH + 1), GRP, 128), jnp.bfloat16),
            jax.ShapeDtypeStruct((shards, 128), jnp.int32),
        ),
        in_specs=[whole(SMEM), whole(VMEM), whole(VMEM), whole(VMEM)],
        out_specs=(whole(VMEM), whole(VMEM)),
        scratch_shapes=[
            pltpu.VMEM((height, 128), jnp.int32),
            pltpu.VMEM((height, 128), jnp.float32),
            pltpu.VMEM((shards, 128), jnp.float32),
        ],
        compiler_params=pltpu.CompilerParams(vmem_limit_bytes=LIMIT),
        cost_estimate=pl.CostEstimate(
            flops=4 * height * KVH * held * HD,
            transcendentals=height * KVH * held,
            bytes_accessed=2 * held * KVD * 2 + 4 * height * KVH * HD,
        ),
        name="attend",
    )(counts, message, keys, values)


def merge_kernel(rows_p, rows_d, parts, message, new_k, new_v, prefill_out, decode_out, lines):
    sources = parts.shape[0]
    rows = rows_p + rows_d
    lane = lax.broadcasted_iota(jnp.int32, (GRP, 128), 1)
    for r in range(rows):
        raw = [parts[s, rows * KVH + r].astype(jnp.float32) for s in range(sources)]
        high = functools.reduce(jnp.maximum, raw)
        fresh = []
        if r >= rows_p:
            request, step = divmod(r - rows_p, STEPS)
            for t in range(step + 1):
                score = jnp.zeros((GRP, 128), jnp.float32)
                for g in range(KVH):
                    query = message[r * KVH + g].astype(jnp.float32)
                    at = request * STEPS + t
                    key = new_k[at : at + 1, g * HD : (g + 1) * HD].astype(jnp.float32)
                    column = jnp.sum(query * key, axis=1, keepdims=True) * (HD ** (-0.5))
                    score = jnp.where(lane == g, column, score)
                fresh.append((request * STEPS + t, score))
                high = jnp.maximum(high, score)
        high = jnp.where(lane < KVH, high, 0.0)
        total = jnp.zeros((GRP, 128), jnp.float32)
        factors = []
        for s in range(sources):
            factor = jnp.exp(jnp.where(lane < KVH, raw[s], 0.0) - high)
            size = pltpu.roll(raw[s], 128 - KVH, 1) + pltpu.roll(raw[s], 128 - 2 * KVH, 1)
            total = total + factor * size
            factors.append(factor)
        fresh = [(at, jnp.exp(score - high)) for at, score in fresh]
        for _, weight in fresh:
            total = total + weight
        total = jnp.where(lane < KVH, total, 1.0)
        factors = [factor / total for factor in factors]
        fresh = [
            (at, (weight / total).astype(jnp.bfloat16).astype(jnp.float32)) for at, weight in fresh
        ]
        for g in range(KVH):
            result = jnp.zeros((GRP, HD), jnp.float32)
            for s in range(sources):
                result = result + factors[s][:, g : g + 1] * parts[s, r * KVH + g].astype(jnp.float32)
            for at, weight in fresh:
                value = new_v[at : at + 1, g * HD : (g + 1) * HD].astype(jnp.float32)
                result = result + weight[:, g : g + 1] * value
            for h in range(GRP):
                column = (g * GRP + h) * HD
                lines[r : r + 1, column : column + HD] = result[h : h + 1, :]
    prefill_out[...] = lines[0:rows_p, :].astype(jnp.bfloat16)
    decode_out[...] = lines[rows_p:rows, :].astype(jnp.bfloat16)


def merge(rows_p, rows_d, parts, message, new_k, new_v):
    rows = rows_p + rows_d
    return pl.pallas_call(
        functools.partial(merge_kernel, rows_p, rows_d),
        out_shape=(
            jax.ShapeDtypeStruct((rows_p, HQ * HD), jnp.bfloat16),
            jax.ShapeDtypeStruct((rows_d, HQ * HD), jnp.bfloat16),
        ),
        in_specs=[whole(VMEM)] * 4,
        out_specs=(whole(VMEM), whole(VMEM)),
        scratch_shapes=[pltpu.VMEM((rows, HQ * HD), jnp.float32)],
        compiler_params=pltpu.CompilerParams(vmem_limit_bytes=LIMIT),
        cost_estimate=pl.CostEstimate(
            flops=parts.size * 4, transcendentals=0, bytes_accessed=parts.size * 2
        ),
        name="merge",
    )(parts, message, new_k.reshape(rows_d, KVD), new_v.reshape(rows_d, KVD))


def exchange(array):
    return lax.all_to_all(array, "seq", split_axis=0, concat_axis=0, tiled=True)


def per_device(
    prefill_q, cache_k, cache_v, page_counts, page_owner, decode_q, decode_k, decode_v, context_len
):
    shards = lax.axis_size("seq")
    page_slots = cache_k.shape[0] // PAGE
    capacity = max(2, 2 * page_slots // shards)
    rows_p = prefill_q.shape[0]
    rows_d = decode_q.shape[0] * STEPS
    owners = page_owner.reshape(-1)
    pages_k = cache_k.reshape(page_slots, PAGE, KVD)
    pages_v = cache_v.reshape(page_slots, PAGE, KVD)
    message = make_message(prefill_q, decode_q, page_owner, context_len)
    gathered = lax.all_gather(message, "seq", axis=0)
    packed_k = pack(owners, page_counts, pages_k, shards, capacity)
    packed_v = pack(owners, page_counts, pages_v, shards, capacity)
    packed_k, gathered = lax.optimization_barrier((packed_k, gathered))
    store_k = exchange(packed_k)
    parts, table = attend(rows_p, rows_d, capacity, page_counts, gathered, cache_k, cache_v)
    packed_v, parts, store_k = lax.optimization_barrier((packed_v, parts, store_k))
    received = exchange(parts)
    packed_v, received = lax.optimization_barrier((packed_v, received))
    store_v = exchange(packed_v)
    prefill_out, decode_out = merge(
        rows_p, rows_d, received, message, decode_k, decode_v
    )
    store_page = table[:, :capacity].reshape(-1)
    return (
        prefill_out,
        decode_out.reshape(decode_q.shape),
        store_k.reshape(-1, KVD),
        store_v.reshape(-1, KVD),
        store_page,
    )


def solution(mesh):
    in_specs = (
        P(("groups", "seq"), None),
        P(("groups", "seq"), None),
        P(("groups", "seq"), None),
        P("groups"),
        P(("groups", "seq"), None),
        P(("groups", "seq"), None, None),
        P(("groups", "seq"), None, None),
        P(("groups", "seq"), None, None),
        P(("groups", "seq")),
    )
    out_specs = (
        P(("groups", "seq"), None),
        P(("groups", "seq"), None, None),
        P(("groups", "seq"), None),
        P(("groups", "seq"), None),
        P(("groups", "seq")),
    )
    return jax.shard_map(
        per_device, mesh=mesh, in_specs=in_specs, out_specs=out_specs, check_vma=False
    )
```

time: 293 us -> 169 us (0.58)
  blocking collectives: 95.3 us -> 45.4 us
  local copies, waits for them, and re-layouts: 54 us -> 7.92 us
  waiting for transfers between devices: 42.4 us -> 80.4 us
  matrix products: 33.5 us -> 0 us
  other arithmetic: 24.9 us -> 0 us
  starting transfers between devices: 37 us -> 16 us
  Pallas kernels: 0 us -> 17.8 us
    all_gather x2 -> x1, blocking collectives: 75.8 us -> 19.6 us  [per_device(): gathered = lax.all_gather(message, 'seq', axis=0)]
    all_to_all x6 -> x2, waiting for transfers between devices: 42.4 us -> 80.4 us  [exchange(): return lax.all_to_all(array, 'seq', split_axis=0, concat_axis=0, tiled=True)]
    dot_general x34 -> x0, matrix products: 33.5 us -> none  [the longest x16 20.6 us: one_group(): jnp.einsum('qhd,kd->qhk', query_group, key_group, preferred_element_type=...]
    all_to_all x0 -> x1, blocking collectives: none -> 25.8 us  [exchange(): return lax.all_to_all(array, 'seq', split_axis=0, concat_axis=0, tiled=True)]
    all_to_all x6 -> x2, starting transfers between devices: 37 us -> 16 us  [exchange(): return lax.all_to_all(array, 'seq', split_axis=0, concat_axis=0, tiled=True)]
    unnamed x1 -> x0, blocking collectives: 19.5 us -> none
    pallas_call x0 -> x5, Pallas kernels: none -> 17.8 us  [the longest x1 7.5 us: attend(): pl.pallas_call(functools.partial(attend_kernel, rows_p, rows_d, capacity)...]
    dynamic_update_slice x48 -> x0, local copies, waits for them, and re-layouts: 14.1 us -> none  [the longest x16 5.6 us: one_group(): lax.dynamic_update_slice_in_dim(weighted, product.reshape(height, groupin...]
  transfers between devices with their start and end apart: 6 -> 2, of which waited for: 3 -> 2; matrix products, arithmetic and copies ran while one was open for 21% -> 0% of each run, Pallas kernels for 0% -> 8%
where the time goes in v1:
time: 169 us
  waiting for transfers between devices  80.4 us (48%)
  blocking collectives  45.4 us (27%)
  Pallas kernels  17.8 us (11%)
  starting transfers between devices  16 us (9%)
  local copies, waits for them, and re-layouts  7.92 us (5%)
    all_to_all x2, waiting for transfers between devices, exchange(): return lax.all_to_all(array, 'seq', split_axis=0, concat_axis=0, tiled=True)  80.4 us
    all_to_all x1, blocking collectives, exchange(): return lax.all_to_all(array, 'seq', split_axis=0, concat_axis=0, tiled=True)  25.8 us
    all_gather x1, blocking collectives, per_device(): gathered = lax.all_gather(message, 'seq', axis=0)  19.6 us
    all_to_all x2, starting transfers between devices, exchange(): return lax.all_to_all(array, 'seq', split_axis=0, concat_axis=0, tiled=True)  16 us
    pallas_call x1, Pallas kernels, attend(): pl.pallas_call(functools.partial(attend_kernel, rows_p, rows_d, capacity)...  7.5 us
    unnamed x16, local copies, waits for them, and re-layouts  7.32 us
    pallas_call x2, Pallas kernels, pack(): pl.pallas_call(functools.partial(pack_kernel, shards, capacity), out_shap...  7.04 us
  transfers between devices with their start and end apart: 2, of which 2 were waited for; matrix products, arithmetic and copies ran while one was open for 0% of the time, Pallas kernels for 8%

profile of v1, /device:TPU:13, one launch (start us, length us, event | category | flops | bytes accessed | tf_op | source)
XLA Modules:
  0.0 168.8 jit_solution(14309453119560942303)
XLA Ops:
  1.3 1.5 message.1
  2.7 19.6 %all-gather = bf16[400,8,128]{2,1,0:T(8,128)(2,1)} all-gather(bf16[25,8,128]{2,1,0:T(8,128)(2,1)} %message.1), channel_id=2, replica_groups=mesh['groups'=2,'seq'=16] {'seq'}, dimensions={0}, use_global_device_ids=true | all-gather | bytes 870400 | tf_op jit(solution)/shard_map/all_gather | solution.py:321
  22.3 3.5 %pack.3 = bf16[128,8,1024]{2,1,0:T(8,128)(2,1)} custom-call(s32[64]{0:T(128)} %bitcast.20, s32[16]{0:T(128)} %counts.5, bf16[64,8,1024]{2,1,0:T(8,128)(2,1)} %bitcast.12), custom_call_target="tpu_custom_call" | custom-call | bytes 3145728 | tf_op jit(solution)/shard_map/pack/pallas_call | solution.py:95
  25.8 11.0 %all-to-all-start = ((bf16[128,8,1024]{2,1,0:T(8,128)(2,1)}), bf16[128,8,1024]{2,1,0:T(8,128)(2,1)}, u32[]{:S(2)}, u32[]{:S(2)}) async-start(bf16[128,8,1024]{2,1,0:T(8,128)(2,1)} %pack.3), calls=%async_computation | async-start | bytes 4194304 | tf_op jit(solution)/shard_map/all_to_all | solution.py:306
  36.7 0.0 copy-start
  36.7 0.0 copy-start.1
  36.8 0.0 copy-start.6
  36.8 3.6 %pack.2 = bf16[128,8,1024]{2,1,0:T(8,128)(2,1)} custom-call(s32[64]{0:T(128)} %bitcast.21, s32[16]{0:T(128)} %counts.5, bf16[64,8,1024]{2,1,0:T(8,128)(2,1)} %bitcast.13), custom_call_target="tpu_custom_call" | custom-call | bytes 3145728 | tf_op jit(solution)/shard_map/pack/pallas_call | solution.py:95
  40.4 0.0 copy-done
  40.4 0.0 copy-done.1
  40.4 0.0 copy-done.6
  40.4 0.0 copy-start.2
  40.4 1.1 copy-done.2
  41.5 7.5 %attend.1 = (bf16[16,27,8,128]{3,2,1,0:T(8,128)(2,1)S(1)}, s32[16,128]{1,0:T(8,128)S(1)}) custom-call(s32[16]{0:T(128)S(1)} %copy-done.6, bf16[16,25,8,128]{3,2,1,0:T(8,128)(2,1)S(1)} %bitcast.14, bf16[512,1024]{1,0:T(8,128)(2,1)S(1)} %copy-done, bf16[512,1024]{1,0:T(8,128)(2,1)S(1)} %copy-done.1), custom_call_target="tpu_custom_call" | custom-call | flops 805306368 | bytes 3670016 | tf_op jit(solution)/shard_map/attend/pallas_call | solution.py:213
  49.1 35.2 %all-to-all-done = bf16[128,8,1024]{2,1,0:T(8,128)(2,1)} async-done(((bf16[128,8,1024]{2,1,0:T(8,128)(2,1)}), bf16[128,8,1024]{2,1,0:T(8,128)(2,1)}, u32[]{:S(2)}, u32[]{:S(2)}) %all-to-all-start) | async-done | bytes 2097184 | tf_op jit(solution)/shard_map/all_to_all | solution.py:306
  84.3 25.8 %all_to_all.15.parts = bf16[16,27,8,128]{3,2,1,0:T(8,128)(2,1)S(1)} all-to-all(bf16[16,27,8,128]{3,2,1,0:T(8,128)(2,1)S(1)} %get-tuple-element.20), channel_id=1, replica_groups=mesh['groups'=2,'seq'=16] {'seq'}, dimensions={0} | all-to-all | bytes 1769472 | tf_op jit(solution)/shard_map/all_to_all | solution.py:306
  110.1 0.0 copy-start.3
  110.1 0.0 copy-start.4
  110.1 0.0 copy-start.5
  110.1 5.0 %all-to-all-start.2 = ((bf16[128,8,1024]{2,1,0:T(8,128)(2,1)}), bf16[128,8,1024]{2,1,0:T(8,128)(2,1)}, u32[]{:S(2)}, u32[]{:S(2)}) async-start(bf16[128,8,1024]{2,1,0:T(8,128)(2,1)} %pack.2), calls=%async_computation.2 | async-start | bytes 4194304 | tf_op jit(solution)/shard_map/all_to_all | solution.py:306
  115.2 0.6 reshape.53
  115.8 0.0 copy-done.3
  115.8 0.0 copy-done.4
  115.8 0.0 copy-done.5
  115.8 1.8 %merge.1 = (bf16[1,8192]{1,0:T(2,128)(2,1)}, bf16[2,8192]{1,0:T(2,128)(2,1)}) custom-call(bf16[16,27,8,128]{3,2,1,0:T(8,128)(2,1)S(1)} %all_to_all.15.parts, bf16[25,8,128]{2,1,0:T(8,128)(2,1)S(1)} %copy-done.3, bf16[2,1024]{1,0:T(2,128)(2,1)S(1)} %bitcast.16, bf16[2,1024]{1,0:T(2,128)(2,1)S(1)} %bitcast.17), custom_call_target="tpu_custom_call" | custom-call | flops 1769472 | bytes 884736 | tf_op jit(solution)/shard_map/merge/pallas_call | solution.py:288
  117.5 45.2 %all-to-all-done.2 = bf16[128,8,1024]{2,1,0:T(8,128)(2,1)} async-done(((bf16[128,8,1024]{2,1,0:T(8,128)(2,1)}), bf16[128,8,1024]{2,1,0:T(8,128)(2,1)}, u32[]{:S(2)}, u32[]{:S(2)}) %all-to-all-start.2) | async-done | bytes 2097184 | tf_op jit(solution)/shard_map/all_to_all | solution.py:306
  162.7 3.1 %copy.17 = bf16[1024,1024]{1,0:T(8,128)(2,1)} copy(bf16[1024,1024]{1,0:T(8,128)(2,1)} %bitcast.9) | data formatting | bytes 4194304
  165.8 3.1 %copy.18 = bf16[1024,1024]{1,0:T(8,128)(2,1)} copy(bf16[1024,1024]{1,0:T(8,128)(2,1)} %bitcast.10) | data formatting | bytes 4194304
Async XLA Ops:
  25.8 58.5 %all-to-all-start = ((bf16[128,8,1024]{2,1,0:T(8,128)(2,1)}), bf16[128,8,1024]{2,1,0:T(8,128)(2,1)}, u32[]{:S(2)}, u32[]{:S(2)}) async-start(bf16[128,8,1024]{2,1,0:T(8,128)(2,1)} %pack.3), calls=%async_computation | async-start | bytes 4194304 | tf_op jit(solution)/shard_map/all_to_all | solution.py:306
  36.7 3.6 %copy-start = (bf16[512,1024]{1,0:T(8,128)(2,1)S(1)}, bf16[512,1024]{1,0:T(8,128)(2,1)}, u32[]{:S(2)}) copy-start(bf16[512,1024]{1,0:T(8,128)(2,1)} %keys.1) | copy-start | bytes 3145732
  36.7 3.6 %copy-start.1 = (bf16[512,1024]{1,0:T(8,128)(2,1)S(1)}, bf16[512,1024]{1,0:T(8,128)(2,1)}, u32[]{:S(2)}) copy-start(bf16[512,1024]{1,0:T(8,128)(2,1)} %values.1) | copy-start | bytes 3145732
  36.8 3.6 %copy-start.6 = (s32[16]{0:T(128)S(1)}, s32[16]{0:T(128)}, u32[]{:S(2)}) copy-start(s32[16]{0:T(128)} %counts.5) | copy-start | bytes 196
  40.4 1.1 copy-start.2
  110.1 5.6 %copy-start.3 = (bf16[25,8,128]{2,1,0:T(8,128)(2,1)S(1)}, bf16[25,8,128]{2,1,0:T(8,128)(2,1)}, u32[]{:S(2)}) copy-start(bf16[25,8,128]{2,1,0:T(8,128)(2,1)} %message.1) | copy-start | bytes 153604
  110.1 5.6 %copy-start.4 = (bf16[1,2,1024]{2,1,0:T(2,128)(2,1)S(1)}, bf16[1,2,1024]{2,1,0:T(2,128)(2,1)}, u32[]{:S(2)}) copy-start(bf16[1,2,1024]{2,1,0:T(2,128)(2,1)} %param.15) | copy-start | bytes 12292
  110.1 5.7 %copy-start.5 = (bf16[1,2,1024]{2,1,0:T(2,128)(2,1)S(1)}, bf16[1,2,1024]{2,1,0:T(2,128)(2,1)}, u32[]{:S(2)}) copy-start(bf16[1,2,1024]{2,1,0:T(2,128)(2,1)} %param.16) | copy-start | bytes 12292
  110.1 52.6 %all-to-all-start.2 = ((bf16[128,8,1024]{2,1,0:T(8,128)(2,1)}), bf16[128,8,1024]{2,1,0:T(8,128)(2,1)}, u32[]{:S(2)}, u32[]{:S(2)}) async-start(bf16[128,8,1024]{2,1,0:T(8,128)(2,1)} %pack.2), calls=%async_computation.2 | async-start | bytes 4194304 | tf_op jit(solution)/shard_map/all_to_all | solution.py:306

commit v2 on v1

--- a/solution.py
+++ b/solution.py
@@ -111,14 +111,18 @@
     )(owners, counts, pages)
 
 
-def attend_kernel(
-    rows_p, rows_d, capacity, counts, message, keys, values, out, table, limits, stats, hits
-):
+def attend_kernel(rows_p, rows_d, capacity, counts, *refs):
+    messages, refs = refs[:4], refs[4:]
+    keys, values, keep, give, table, limits, stats, hits = refs
     me = lax.axis_index("seq")
-    shards = message.shape[0]
     rows = rows_p + rows_d
+    blocks = rows * KVH + 1
+    shards = 4 * messages[0].shape[0] // blocks
     height = shards * rows * GRP
     held = keys.shape[0]
+
+    def block(k, at):
+        return messages[k % 4][(k // 4) * blocks + at]
 
     def count(d, carry):
         before, total = carry
@@ -130,11 +134,11 @@
     live = PAGE * counts[me]
     first = PAGE * total - shards * rows_p + 1
     lane = lax.broadcasted_iota(jnp.int32, (1, 128), 1)
-    last = rows * KVH
-    for d in range(shards):
-        tail = message[d, last].astype(jnp.float32)
+    for k in range(shards):
+        d = me ^ k
+        tail = block(k, rows * KVH).astype(jnp.float32)
         for r in range(rows):
-            at = (d * rows + r) * GRP
+            at = (k * rows + r) * GRP
             if r < rows_p:
                 bound = jnp.minimum(first + d * rows_p + r - start, live)
                 limits[at : at + GRP, :] = jnp.full((GRP, 128), bound, jnp.int32)
@@ -144,7 +148,7 @@
                 bound = jnp.minimum(length.astype(jnp.int32) - start, live)
                 limits[at : at + GRP, :] = jnp.broadcast_to(bound, (GRP, 128))
         hit = (tail[0:1, :].astype(jnp.int32) == me) & (lane < counts[d])
-        hits[d : d + 1, :] = hit.astype(jnp.float32)
+        hits[pl.ds(d, 1), :] = hit.astype(jnp.float32)
 
     hit = hits[...]
     earlier = (
@@ -166,15 +170,14 @@
     stats[...] = jnp.zeros_like(stats)
     spot = lax.broadcasted_iota(jnp.int32, (height, 128), 1)
     column = lax.broadcasted_iota(jnp.int32, (height, held), 1)
+    pieces = [(k, r, (k * rows + r) * GRP) for k in range(shards) for r in range(rows)]
+
+    def target(k):
+        return give if k % 2 else keep
 
     def one_group(g, carry):
         query = jnp.concatenate(
-            [
-                message[d, r * KVH + g].astype(jnp.float32)
-                for d in range(shards)
-                for r in range(rows)
-            ],
-            axis=0,
+            [block(k, r * KVH + g).astype(jnp.float32) for k, r, _ in pieces], axis=0
         ).astype(jnp.bfloat16)
         across = pl.ds(pl.multiple_of(g * HD, HD), HD)
         scores = lax.dot_general(
@@ -192,32 +195,26 @@
         kept = jnp.where(spot == g, high, stats[...])
         kept = jnp.where(spot == KVH + g, coarse, kept)
         stats[...] = jnp.where(spot == 2 * KVH + g, total - coarse, kept)
-        for d in range(shards):
-            for r in range(rows):
-                at = (d * rows + r) * GRP
-                out[d, r * KVH + g] = product[at : at + GRP, :].astype(jnp.bfloat16)
+        for k, r, at in pieces:
+            target(k)[k // 2, r * KVH + g] = product[at : at + GRP, :].astype(jnp.bfloat16)
         return carry
 
     lax.fori_loop(0, KVH, one_group, 0)
-    for d in range(shards):
-        for r in range(rows):
-            at = (d * rows + r) * GRP
-            out[d, rows * KVH + r] = stats[at : at + GRP, :].astype(jnp.bfloat16)
-
-
-def attend(rows_p, rows_d, capacity, counts, message, keys, values):
-    shards = message.shape[0]
+    for k, r, at in pieces:
+        target(k)[k // 2, rows * KVH + r] = stats[at : at + GRP, :].astype(jnp.bfloat16)
+
+
+def attend(rows_p, rows_d, capacity, counts, messages, keys, values):
     rows = rows_p + rows_d
+    shards = 4 * messages[0].shape[0] // (rows * KVH + 1)
     height = shards * rows * GRP
     held = keys.shape[0]
+    half = jax.ShapeDtypeStruct((shards // 2, rows * (KVH + 1), GRP, 128), jnp.bfloat16)
     return pl.pallas_call(
         functools.partial(attend_kernel, rows_p, rows_d, capacity),
-        out_shape=(
-            jax.ShapeDtypeStruct((shards, rows * (KVH + 1), GRP, 128), jnp.bfloat16),
-            jax.ShapeDtypeStruct((shards, 128), jnp.int32),
-        ),
-        in_specs=[whole(SMEM), whole(VMEM), whole(VMEM), whole(VMEM)],
-        out_specs=(whole(VMEM), whole(VMEM)),
+        out_shape=(half, half, jax.ShapeDtypeStruct((shards, 128), jnp.int32)),
+        in_specs=[whole(SMEM)] + [whole(VMEM)] * 6,
+        out_specs=(whole(VMEM),) * 3,
         scratch_shapes=[
             pltpu.VMEM((height, 128), jnp.int32),
             pltpu.VMEM((height, 128), jnp.float32),
@@ -230,15 +227,81 @@
             bytes_accessed=2 * held * KVD * 2 + 4 * height * KVH * HD,
         ),
         name="attend",
-    )(counts, message, keys, values)
-
-
-def merge_kernel(rows_p, rows_d, parts, message, new_k, new_v, prefill_out, decode_out, lines):
-    sources = parts.shape[0]
+    )(counts, *messages, keys, values)
+
+
+def fold_kernel(rows, keep, got, *outs):
+    lane = lax.broadcasted_iota(jnp.int32, (GRP, 128), 1)
+    inside = lane < KVH
+    for j, out in enumerate(outs):
+        for r in range(rows):
+            raw = [ref[j, rows * KVH + r].astype(jnp.float32) for ref in (keep, got)]
+            high = jnp.maximum(jnp.where(inside, raw[0], 0.0), jnp.where(inside, raw[1], 0.0))
+            factors = [jnp.exp(jnp.where(inside, part, 0.0) - high) for part in raw]
+            sizes = [
+                pltpu.roll(part, 128 - KVH, 1) + pltpu.roll(part, 128 - 2 * KVH, 1) for part in raw
+            ]
+            total = jnp.where(inside, factors[0] * sizes[0] + factors[1] * sizes[1], 0.0)
+            coarse = total.astype(jnp.bfloat16).astype(jnp.float32)
+            line = high + pltpu.roll(coarse, KVH, 1) + pltpu.roll(total - coarse, 2 * KVH, 1)
+            out[rows * KVH + r] = line.astype(jnp.bfloat16)
+            for g in range(KVH):
+                at = r * KVH + g
+                mixed = factors[0][:, g : g + 1] * keep[j, at].astype(jnp.float32)
+                mixed = mixed + factors[1][:, g : g + 1] * got[j, at].astype(jnp.float32)
+                out[at] = mixed.astype(jnp.bfloat16)
+
+
+def fold(rows, keep, got):
+    piece = jax.ShapeDtypeStruct(keep.shape[1:], keep.dtype)
+    return pl.pallas_call(
+        functools.partial(fold_kernel, rows),
+        out_shape=(piece,) * keep.shape[0],
+        in_specs=[whole(VMEM)] * 2,
+        out_specs=(whole(VMEM),) * keep.shape[0],
+        compiler_params=pltpu.CompilerParams(vmem_limit_bytes=LIMIT),
+        cost_estimate=pl.CostEstimate(
+            flops=keep.size * 4, transcendentals=0, bytes_accessed=keep.size * 6
+        ),
+        name="fold",
+    )(keep, got)
+
+
+def settle_kernel(pieces, source, out, sems):
+    step = source.shape[0] // pieces
+    spans = [pl.ds(i * step, step) for i in range(pieces)]
+    puts = [
+        pltpu.make_async_copy(source.at[span], out.at[span], sems.at[i])
+        for i, span in enumerate(spans)
+    ]
+    for put in puts:
+        put.start()
+    for put in puts:
+        put.wait()
+
+
+def settle(source):
+    pieces = 4
+    return pl.pallas_call(
+        functools.partial(settle_kernel, pieces),
+        out_shape=jax.ShapeDtypeStruct(source.shape, source.dtype),
+        in_specs=[whole(VMEM)],
+        out_specs=whole(pl.ANY),
+        scratch_shapes=[pltpu.SemaphoreType.DMA((pieces,))],
+        cost_estimate=pl.CostEstimate(
+            flops=0, transcendentals=0, bytes_accessed=2 * source.size * 2
+        ),
+        name="settle",
+    )(source)
+
+
+def merge_kernel(rows_p, rows_d, message, new_k, new_v, *refs):
+    parts, (prefill_out, decode_out, lines) = refs[:-3], refs[-3:]
+    sources = len(parts)
     rows = rows_p + rows_d
     lane = lax.broadcasted_iota(jnp.int32, (GRP, 128), 1)
     for r in range(rows):
-        raw = [parts[s, rows * KVH + r].astype(jnp.float32) for s in range(sources)]
+        raw = [part[rows * KVH + r].astype(jnp.float32) for part in parts]
         high = functools.reduce(jnp.maximum, raw)
         fresh = []
         if r >= rows_p:
@@ -272,7 +335,8 @@
         for g in range(KVH):
             result = jnp.zeros((GRP, HD), jnp.float32)
             for s in range(sources):
-                result = result + factors[s][:, g : g + 1] * parts[s, r * KVH + g].astype(jnp.float32)
+                block = parts[s][r * KVH + g].astype(jnp.float32)
+                result = result + factors[s][:, g : g + 1] * block
             for at, weight in fresh:
                 value = new_v[at : at + 1, g * HD : (g + 1) * HD].astype(jnp.float32)
                 result = result + weight[:, g : g + 1] * value
@@ -291,15 +355,22 @@
             jax.ShapeDtypeStruct((rows_p, HQ * HD), jnp.bfloat16),
             jax.ShapeDtypeStruct((rows_d, HQ * HD), jnp.bfloat16),
         ),
-        in_specs=[whole(VMEM)] * 4,
+        in_specs=[whole(VMEM)] * (3 + len(parts)),
         out_specs=(whole(VMEM), whole(VMEM)),
         scratch_shapes=[pltpu.VMEM((rows, HQ * HD), jnp.float32)],
         compiler_params=pltpu.CompilerParams(vmem_limit_bytes=LIMIT),
         cost_estimate=pl.CostEstimate(
-            flops=parts.size * 4, transcendentals=0, bytes_accessed=parts.size * 2
+            flops=len(parts) * parts[0].size * 4,
+            transcendentals=0,
+            bytes_accessed=len(parts) * parts[0].size * 2,
         ),
         name="merge",
-    )(parts, message, new_k.reshape(rows_d, KVD), new_v.reshape(rows_d, KVD))
+    )(message, new_k.reshape(rows_d, KVD), new_v.reshape(rows_d, KVD), *parts)
+
+
+def swap(array, distance):
+    shards = lax.axis_size("seq")
+    return lax.ppermute(array, "seq", [(i, i ^ distance) for i in range(shards)])
 
 
 def exchange(array):
@@ -317,20 +388,37 @@
     owners = page_owner.reshape(-1)
     pages_k = cache_k.reshape(page_slots, PAGE, KVD)
     pages_v = cache_v.reshape(page_slots, PAGE, KVD)
+    rows = rows_p + rows_d
     message = make_message(prefill_q, decode_q, page_owner, context_len)
-    gathered = lax.all_gather(message, "seq", axis=0)
+    far = [message]
+    for k in range(4, shards, 4):
+        far.append(swap(message, k))
     packed_k = pack(owners, page_counts, pages_k, shards, capacity)
     packed_v = pack(owners, page_counts, pages_v, shards, capacity)
-    packed_k, gathered = lax.optimization_barrier((packed_k, gathered))
+    own = jnp.concatenate(far, axis=0)
+    across = swap(own, 2)
+    beside = swap(own, 1)
+    corner = swap(across, 1)
     store_k = exchange(packed_k)
-    parts, table = attend(rows_p, rows_d, capacity, page_counts, gathered, cache_k, cache_v)
-    packed_v, parts, store_k = lax.optimization_barrier((packed_v, parts, store_k))
-    received = exchange(parts)
-    packed_v, received = lax.optimization_barrier((packed_v, received))
+    keep, give, table = attend(
+        rows_p,
+        rows_d,
+        capacity,
+        page_counts,
+        (own, beside, across, corner),
+        cache_k,
+        cache_v,
+    )
+    got = swap(give, 1)
+    folded = fold(rows, keep, got)
+    parts = [folded[0]]
+    for j in range(1, shards // 2):
+        parts.append(swap(folded[j], 2 * j))
+    packed_v, store_k = lax.optimization_barrier((packed_v, store_k))
     store_v = exchange(packed_v)
-    prefill_out, decode_out = merge(
-        rows_p, rows_d, received, message, decode_k, decode_v
-    )
+    prefill_out, decode_out = merge(rows_p, rows_d, parts, message, decode_k, decode_v)
+    store_k = settle(store_k)
+    store_v = settle(store_v)
     store_page = table[:, :capacity].reshape(-1)
     return (
         prefill_out,

time: 169 us -> 161 us (0.953)
  the two profiles are of different devices: /device:TPU:13 before, /device:TPU:0 now
where the time goes in v2:
time: 161 us
  waiting for transfers between devices  96.2 us (60%)
  starting transfers between devices  36.2 us (22%)
  Pallas kernels  25.6 us (16%)
    ppermute x14, waiting for transfers between devices, swap(): lax.ppermute(array, 'seq', [(i, i ^ distance) for i in range(shards)])  58.6 us
    all_to_all x2, waiting for transfers between devices, exchange(): return lax.all_to_all(array, 'seq', split_axis=0, concat_axis=0, tiled=True)  37.6 us
    all_to_all x2, starting transfers between devices, exchange(): return lax.all_to_all(array, 'seq', split_axis=0, concat_axis=0, tiled=True)  18.8 us
    ppermute x14, starting transfers between devices, swap(): lax.ppermute(array, 'seq', [(i, i ^ distance) for i in range(shards)])  17.4 us
    pallas_call x1, Pallas kernels, attend(): pl.pallas_call(functools.partial(attend_kernel, rows_p, rows_d, capacity)...  7.5 us
    pallas_call x2, Pallas kernels, pack(): pl.pallas_call(functools.partial(pack_kernel, shards, capacity), out_shap...  6.82 us
    pallas_call x2, Pallas kernels, settle(): pl.pallas_call(functools.partial(settle_kernel, pieces), out_shape=jax.Sh...  5.87 us
  transfers between devices with their start and end apart: 16, of which 8 were waited for; matrix products, arithmetic and copies ran while one was open for 1% of the time, Pallas kernels for 12%

profile of v2, /device:TPU:0, one launch (start us, length us, event | category | flops | bytes accessed | tf_op | source)
XLA Modules:
  0.0 160.9 jit_solution(17641977918305990523)
XLA Ops:
  0.6 3.4 %pack.3 = bf16[128,8,1024]{2,1,0:T(8,128)(2,1)} custom-call(s32[64]{0:T(128)} %bitcast.19, s32[16]{0:T(128)} %counts.5, bf16[64,8,1024]{2,1,0:T(8,128)(2,1)} %bitcast.11), custom_call_target="tpu_custom_call" | custom-call | bytes 3145728 | tf_op jit(solution)/shard_map/pack/pallas_call | solution.py:95
  4.0 7.5 %all-to-all-start = ((bf16[128,8,1024]{2,1,0:T(8,128)(2,1)}), bf16[128,8,1024]{2,1,0:T(8,128)(2,1)}, u32[]{:S(2)}, u32[]{:S(2)}) async-start(bf16[128,8,1024]{2,1,0:T(8,128)(2,1)} %pack.3), calls=%async_computation | async-start | bytes 4194304 | tf_op jit(solution)/shard_map/all_to_all | solution.py:377
  11.6 3.4 %pack.2 = bf16[128,8,1024]{2,1,0:T(8,128)(2,1)} custom-call(s32[64]{0:T(128)} %bitcast.20, s32[16]{0:T(128)} %counts.5, bf16[64,8,1024]{2,1,0:T(8,128)(2,1)} %bitcast.12), custom_call_target="tpu_custom_call" | custom-call | bytes 3145728 | tf_op jit(solution)/shard_map/pack/pallas_call | solution.py:95
  15.0 0.0 copy-start
  15.0 0.0 copy-start.1
  15.0 0.0 copy-start.5
  15.0 37.6 %all-to-all-done.source = bf16[128,8,1024]{2,1,0:T(8,128)(2,1)} async-done(((bf16[128,8,1024]{2,1,0:T(8,128)(2,1)}), bf16[128,8,1024]{2,1,0:T(8,128)(2,1)}, u32[]{:S(2)}, u32[]{:S(2)}) %all-to-all-start) | async-done | bytes 2097184 | tf_op jit(solution)/shard_map/all_to_all | solution.py:377
  52.6 11.3 %all-to-all-start.1 = ((bf16[128,8,1024]{2,1,0:T(8,128)(2,1)}), bf16[128,8,1024]{2,1,0:T(8,128)(2,1)}, u32[]{:S(2)}, u32[]{:S(2)}) async-start(bf16[128,8,1024]{2,1,0:T(8,128)(2,1)} %pack.2), calls=%async_computation.1 | async-start | bytes 4194304 | tf_op jit(solution)/shard_map/all_to_all | solution.py:377
  64.5 1.5 message.1
  66.0 0.0 copy-start.2
  66.0 0.0 copy-start.3
  66.0 0.0 copy-start.4
  66.0 3.7 %collective-permute-start.2 = (bf16[25,8,128]{2,1,0:T(8,128)(2,1)}, bf16[25,8,128]{2,1,0:T(8,128)(2,1)S(1)}, u32[]{:S(2)}, u32[]{:S(2)}) collective-permute-start(bf16[25,8,128]{2,1,0:T(8,128)(2,1)} %message.1), channel_id=1, source_target_pairs={{0,12},{1,13},{2,14},{3,15},{4,8},{5,9},{6,10},{7,11},{8,4},{9,5},... | collective-permute-start | bytes 153608 | tf_op jit(solution)/shard_map/ppermute | solution.py:373
  69.7 0.0 collective-permute-start.1
  69.7 0.7 collective-permute-start
  70.4 33.9 %collective-permute-done.2 = bf16[25,8,128]{2,1,0:T(8,128)(2,1)S(1)} collective-permute-done((bf16[25,8,128]{2,1,0:T(8,128)(2,1)}, bf16[25,8,128]{2,1,0:T(8,128)(2,1)S(1)}, u32[]{:S(2)}, u32[]{:S(2)}) %collective-permute-start.2) | collective-permute-done | bytes 51232 | tf_op jit(solution)/shard_map/ppermute | solution.py:373
  104.3 12.9 %collective-permute-done.1 = bf16[25,8,128]{2,1,0:T(8,128)(2,1)S(1)} collective-permute-done((bf16[25,8,128]{2,1,0:T(8,128)(2,1)}, bf16[25,8,128]{2,1,0:T(8,128)(2,1)S(1)}, u32[]{:S(2)}, u32[]{:S(2)}) %collective-permute-start.1) | collective-permute-done | bytes 51232 | tf_op jit(solution)/shard_map/ppermute | solution.py:373
  117.2 0.0 collective-permute-done
  117.2 0.8 pad_maximum_fusion.refs_0_
  118.1 1.6 collective-permute-start.4
  119.7 0.0 collective-permute-start.3
  119.7 4.7 %collective-permute-done.4.refs_2_ = bf16[100,8,128]{2,1,0:T(8,128)(2,1)S(1)} collective-permute-done((bf16[100,8,128]{2,1,0:T(8,128)(2,1)S(1)}, bf16[100,8,128]{2,1,0:T(8,128)(2,1)S(1)}, u32[]{:S(2)}, u32[]{:S(2)}) %collective-permute-start.4) | collective-permute-done | bytes 204832 | tf_op jit(solution)/shard_map/ppermute | solution.py:373
  124.4 0.0 collective-permute-start.5
  124.4 0.0 collective-permute-done.3.refs_1_
  124.4 1.4 collective-permute-done.5.refs_3_
  125.8 0.0 copy-done
  125.8 0.0 copy-done.1
  125.8 0.0 copy-done.5
  125.8 7.5 %attend.1 = (bf16[8,27,8,128]{3,2,1,0:T(8,128)(2,1)S(1)}, bf16[8,27,8,128]{3,2,1,0:T(8,128)(2,1)S(1)}, s32[16,128]{1,0:T(8,128)S(1)}) custom-call(s32[16]{0:T(128)S(1)} %copy-done.5, bf16[100,8,128]{2,1,0:T(8,128)(2,1)S(1)} %pad_maximum_fusion.refs_0_, bf16[100,8,128]{2,1,0:T(8,128)(2,1)S(1)} %collective-permute-done.3.refs_1_, ...), custom_call_target="tpu_custom_call" | custom-call | flops 805306368 | bytes 3670016 | tf_op jit(solution)/shard_map/attend/pallas_call | solution.py:213
  133.3 0.2 collective-permute-start.6
  133.5 1.7 %collective-permute-done.6.got = bf16[8,27,8,128]{3,2,1,0:T(8,128)(2,1)S(1)} collective-permute-done((bf16[8,27,8,128]{3,2,1,0:T(8,128)(2,1)S(1)}, bf16[8,27,8,128]{3,2,1,0:T(8,128)(2,1)S(1)}, u32[]{:S(2)}, u32[]{:S(2)}) %collective-permute-start.6) | collective-permute-done | bytes 442400 | tf_op jit(solution)/shard_map/ppermute | solution.py:373
  135.2 2.6 %fold.1 = (bf16[27,8,128]{2,1,0:T(8,128)(2,1)S(1)}, bf16[27,8,128]{2,1,0:T(8,128)(2,1)S(1)}, bf16[27,8,128]{2,1,0:T(8,128)(2,1)S(1)}, bf16[27,8,128]{2,1,0:T(8,1...) custom-call(bf16[8,27,8,128]{3,2,1,0:T(8,128)(2,1)S(1)} %get-tuple-e, ...), custom_call_target="tpu_custom_call" | custom-call | flops 884736 | bytes 1327104 | tf_op jit(solution)/shard_map/fold/pallas_call | solution.py:257
  137.8 1.6 collective-permute-start.7
  139.3 0.0 collective-permute-start.8
  139.3 2.0 %collective-permute-start.9 = (bf16[27,8,128]{2,1,0:T(8,128)(2,1)S(1)}, bf16[27,8,128]{2,1,0:T(8,128)(2,1)S(1)}, u32[]{:S(2)}, u32[]{:S(2)}) collective-permute-start(bf16[27,8,128]{2,1,0:T(8,128)(2,1)S(1)} %get-tuple-element.25), channel_id=1, source_target_pairs={{0,6},{1,7},{2,4},{3,5},{4,2},{5,3},{6,0},{7,1},{8,14},{9,15},{10,... | collective-permute-start | bytes 165896 | tf_op jit(solution)/shard_map/ppermute | solution.py:373
  141.3 0.0 collective-permute-start.10
  141.3 3.9 %collective-permute-start.11 = (bf16[27,8,128]{2,1,0:T(8,128)(2,1)S(1)}, bf16[27,8,128]{2,1,0:T(8,128)(2,1)S(1)}, u32[]{:S(2)}, u32[]{:S(2)}) collective-permute-start(bf16[27,8,128]{2,1,0:T(8,128)(2,1)S(1)} %get-tuple-element.27), channel_id=1, source_target_pairs={{0,10},{1,11},{2,8},{3,9},{4,14},{5,15},{6,12},{7,13},{8,2},{9,3},... | collective-permute-start | bytes 165896 | tf_op jit(solution)/shard_map/ppermute | solution.py:373
  145.2 0.0 collective-permute-done.7.refs_1_
  145.2 1.4 collective-permute-start.12
  146.6 0.0 collective-permute-done.8.refs_2_
  146.6 2.4 %collective-permute-start.13 = (bf16[27,8,128]{2,1,0:T(8,128)(2,1)S(1)}, bf16[27,8,128]{2,1,0:T(8,128)(2,1)S(1)}, u32[]{:S(2)}, u32[]{:S(2)}) collective-permute-start(bf16[27,8,128]{2,1,0:T(8,128)(2,1)S(1)} %get-tuple-element.29), channel_id=1, source_target_pairs={{0,14},{1,15},{2,12},{3,13},{4,10},{5,11},{6,8},{7,9},{8,6},{9,7},... | collective-permute-start | bytes 165896 | tf_op jit(solution)/shard_map/ppermute | solution.py:373
  149.0 0.6 reshape.53
  149.6 0.0 collective-permute-done.9.refs_3_
  149.6 0.0 collective-permute-done.10.refs_4_
  149.6 2.6 %collective-permute-done.11.refs_5_ = bf16[27,8,128]{2,1,0:T(8,128)(2,1)S(1)} collective-permute-done((bf16[27,8,128]{2,1,0:T(8,128)(2,1)S(1)}, bf16[27,8,128]{2,1,0:T(8,128)(2,1)S(1)}, u32[]{:S(2)}, u32[]{:S(2)}) %collective-permute-start.11) | collective-permute-done | bytes 55328 | tf_op jit(solution)/shard_map/ppermute | solution.py:373
  152.2 0.0 collective-permute-done.12.refs_6_
  152.2 1.3 collective-permute-done.13.refs_7_
  153.5 0.0 copy-done.2
  153.5 0.0 copy-done.3
  153.5 0.0 copy-done.4
  153.5 1.4 merge.1
  155.0 2.9 %settle.2 = bf16[128,8,1024]{2,1,0:T(8,128)(2,1)} custom-call(bf16[128,8,1024]{2,1,0:T(8,128)(2,1)} %all-to-all-done.source), custom_call_target="tpu_custom_call" | custom-call | bytes 4194304 | tf_op jit(solution)/shard_map/settle/pallas_call | solution.py:285
  157.9 0.0 all-to-all-done.1.source
  157.9 2.9 %settle.3 = bf16[128,8,1024]{2,1,0:T(8,128)(2,1)} custom-call(bf16[128,8,1024]{2,1,0:T(8,128)(2,1)} %all-to-all-done.1.source), custom_call_target="tpu_custom_call" | custom-call | bytes 4194304 | tf_op jit(solution)/shard_map/settle/pallas_call | solution.py:285
Async XLA Ops:
  4.0 48.6 %all-to-all-start = ((bf16[128,8,1024]{2,1,0:T(8,128)(2,1)}), bf16[128,8,1024]{2,1,0:T(8,128)(2,1)}, u32[]{:S(2)}, u32[]{:S(2)}) async-start(bf16[128,8,1024]{2,1,0:T(8,128)(2,1)} %pack.3), calls=%async_computation | async-start | bytes 4194304 | tf_op jit(solution)/shard_map/all_to_all | solution.py:377
  15.0 110.8 %copy-start = (bf16[512,1024]{1,0:T(8,128)(2,1)S(1)}, bf16[512,1024]{1,0:T(8,128)(2,1)}, u32[]{:S(2)}) copy-start(bf16[512,1024]{1,0:T(8,128)(2,1)} %refs_4_.1) | copy-start | bytes 3145732
  15.0 110.8 %copy-start.1 = (bf16[512,1024]{1,0:T(8,128)(2,1)S(1)}, bf16[512,1024]{1,0:T(8,128)(2,1)}, u32[]{:S(2)}) copy-start(bf16[512,1024]{1,0:T(8,128)(2,1)} %refs_5_.1) | copy-start | bytes 3145732
  15.0 110.8 %copy-start.5 = (s32[16]{0:T(128)S(1)}, s32[16]{0:T(128)}, u32[]{:S(2)}) copy-start(s32[16]{0:T(128)} %counts.5) | copy-start | bytes 196
  52.6 105.3 %all-to-all-start.1 = ((bf16[128,8,1024]{2,1,0:T(8,128)(2,1)}), bf16[128,8,1024]{2,1,0:T(8,128)(2,1)}, u32[]{:S(2)}, u32[]{:S(2)}) async-start(bf16[128,8,1024]{2,1,0:T(8,128)(2,1)} %pack.2), calls=%async_computation.1 | async-start | bytes 4194304 | tf_op jit(solution)/shard_map/all_to_all | solution.py:377
  66.0 87.5 %copy-start.2 = (bf16[25,8,128]{2,1,0:T(8,128)(2,1)S(1)}, bf16[25,8,128]{2,1,0:T(8,128)(2,1)}, u32[]{:S(2)}) copy-start(bf16[25,8,128]{2,1,0:T(8,128)(2,1)} %message.1) | copy-start | bytes 153604
  66.0 87.5 %copy-start.3 = (bf16[1,2,1024]{2,1,0:T(2,128)(2,1)S(1)}, bf16[1,2,1024]{2,1,0:T(2,128)(2,1)}, u32[]{:S(2)}) copy-start(bf16[1,2,1024]{2,1,0:T(2,128)(2,1)} %param.15) | copy-start | bytes 12292
  66.0 87.5 %copy-start.4 = (bf16[1,2,1024]{2,1,0:T(2,128)(2,1)S(1)}, bf16[1,2,1024]{2,1,0:T(2,128)(2,1)}, u32[]{:S(2)}) copy-start(bf16[1,2,1024]{2,1,0:T(2,128)(2,1)} %param.16) | copy-start | bytes 12292
  66.0 38.3 %collective-permute-start.2 = (bf16[25,8,128]{2,1,0:T(8,128)(2,1)}, bf16[25,8,128]{2,1,0:T(8,128)(2,1)S(1)}, u32[]{:S(2)}, u32[]{:S(2)}) collective-permute-start(bf16[25,8,128]{2,1,0:T(8,128)(2,1)} %message.1), channel_id=1, source_target_pairs={{0,12},{1,13},{2,14},{3,15},{4,8},{5,9},{6,10},{7,11},{8,4},{9,5},... | collective-permute-start | bytes 153608 | tf_op jit(solution)/shard_map/ppermute | solution.py:373
  69.7 47.6 %collective-permute-start.1 = (bf16[25,8,128]{2,1,0:T(8,128)(2,1)}, bf16[25,8,128]{2,1,0:T(8,128)(2,1)S(1)}, u32[]{:S(2)}, u32[]{:S(2)}) collective-permute-start(bf16[25,8,128]{2,1,0:T(8,128)(2,1)} %message.1), channel_id=1, source_target_pairs={{0,8},{1,9},{2,10},{3,11},{4,12},{5,13},{6,14},{7,15},{8,0},{9,1},... | collective-permute-start | bytes 153608 | tf_op jit(solution)/shard_map/ppermute | solution.py:373
  69.7 47.6 %collective-permute-start = (bf16[25,8,128]{2,1,0:T(8,128)(2,1)}, bf16[25,8,128]{2,1,0:T(8,128)(2,1)S(1)}, u32[]{:S(2)}, u32[]{:S(2)}) collective-permute-start(bf16[25,8,128]{2,1,0:T(8,128)(2,1)} %message.1), channel_id=1, source_target_pairs={{0,4},{1,5},{2,6},{3,7},{4,0},{5,1},{6,2},{7,3},{8,12},{9,13},{10,... | collective-permute-start | bytes 153608 | tf_op jit(solution)/shard_map/ppermute | solution.py:373
  118.1 6.3 %collective-permute-start.4 = (bf16[100,8,128]{2,1,0:T(8,128)(2,1)S(1)}, bf16[100,8,128]{2,1,0:T(8,128)(2,1)S(1)}, u32[]{:S(2)}, u32[]{:S(2)}) collective-permute-start(bf16[100,8,128]{2,1,0:T(8,128)(2,1)S(1)} %pad_maximum_fusion.refs_0_), channel_id=1, source_target_pairs={{0,2},{1,3},{2,0},{3,1},{4,6},{5,7},{6,4},{7,5},{8,10},{9,11},{10,... | collective-permute-start | bytes 614408 | tf_op jit(solution)/shard_map/ppermute | solution.py:373
  119.7 4.7 %collective-permute-start.3 = (bf16[100,8,128]{2,1,0:T(8,128)(2,1)S(1)}, bf16[100,8,128]{2,1,0:T(8,128)(2,1)S(1)}, u32[]{:S(2)}, u32[]{:S(2)}) collective-permute-start(bf16[100,8,128]{2,1,0:T(8,128)(2,1)S(1)} %pad_maximum_fusion.refs_0_), channel_id=1, source_target_pairs={{0,1},{1,0},{2,3},{3,2},{4,5},{5,4},{6,7},{7,6},{8,9},{9,8},{10,11... | collective-permute-start | bytes 614408 | tf_op jit(solution)/shard_map/ppermute | solution.py:373
  124.4 1.5 collective-permute-start.5
  133.3 1.9 %collective-permute-start.6 = (bf16[8,27,8,128]{3,2,1,0:T(8,128)(2,1)S(1)}, bf16[8,27,8,128]{3,2,1,0:T(8,128)(2,1)S(1)}, u32[]{:S(2)}, u32[]{:S(2)}) collective-permute-start(bf16[8,27,8,128]{3,2,1,0:T(8,128)(2,1)S(1)} %get-tuple-element.21), channel_id=1, source_target_pairs={{0,1},{1,0},{2,3},{3,2},{4,5},{5,4},{6,7},{7,6},{8,9},{9,8},{10,11... | collective-permute-start | bytes 1327112 | tf_op jit(solution)/shard_map/ppermute | solution.py:373
  137.8 7.4 %collective-permute-start.7 = (bf16[27,8,128]{2,1,0:T(8,128)(2,1)S(1)}, bf16[27,8,128]{2,1,0:T(8,128)(2,1)S(1)}, u32[]{:S(2)}, u32[]{:S(2)}) collective-permute-start(bf16[27,8,128]{2,1,0:T(8,128)(2,1)S(1)} %get-tuple-element.23), channel_id=1, source_target_pairs={{0,2},{1,3},{2,0},{3,1},{4,6},{5,7},{6,4},{7,5},{8,10},{9,11},{10,... | collective-permute-start | bytes 165896 | tf_op jit(solution)/shard_map/ppermute | solution.py:373
  139.3 7.2 %collective-permute-start.8 = (bf16[27,8,128]{2,1,0:T(8,128)(2,1)S(1)}, bf16[27,8,128]{2,1,0:T(8,128)(2,1)S(1)}, u32[]{:S(2)}, u32[]{:S(2)}) collective-permute-start(bf16[27,8,128]{2,1,0:T(8,128)(2,1)S(1)} %get-tuple-element.24), channel_id=1, source_target_pairs={{0,4},{1,5},{2,6},{3,7},{4,0},{5,1},{6,2},{7,3},{8,12},{9,13},{10,... | collective-permute-start | bytes 165896 | tf_op jit(solution)/shard_map/ppermute | solution.py:373
  139.3 10.2 %collective-permute-start.9 = (bf16[27,8,128]{2,1,0:T(8,128)(2,1)S(1)}, bf16[27,8,128]{2,1,0:T(8,128)(2,1)S(1)}, u32[]{:S(2)}, u32[]{:S(2)}) collective-permute-start(bf16[27,8,128]{2,1,0:T(8,128)(2,1)S(1)} %get-tuple-element.25), channel_id=1, source_target_pairs={{0,6},{1,7},{2,4},{3,5},{4,2},{5,3},{6,0},{7,1},{8,14},{9,15},{10,... | collective-permute-start | bytes 165896 | tf_op jit(solution)/shard_map/ppermute | solution.py:373
  141.3 8.3 %collective-permute-start.10 = (bf16[27,8,128]{2,1,0:T(8,128)(2,1)S(1)}, bf16[27,8,128]{2,1,0:T(8,128)(2,1)S(1)}, u32[]{:S(2)}, u32[]{:S(2)}) collective-permute-start(bf16[27,8,128]{2,1,0:T(8,128)(2,1)S(1)} %get-tuple-element.26), channel_id=1, source_target_pairs={{0,8},{1,9},{2,10},{3,11},{4,12},{5,13},{6,14},{7,15},{8,0},{9,1},... | collective-permute-start | bytes 165896 | tf_op jit(solution)/shard_map/ppermute | solution.py:373
  141.3 10.9 %collective-permute-start.11 = (bf16[27,8,128]{2,1,0:T(8,128)(2,1)S(1)}, bf16[27,8,128]{2,1,0:T(8,128)(2,1)S(1)}, u32[]{:S(2)}, u32[]{:S(2)}) collective-permute-start(bf16[27,8,128]{2,1,0:T(8,128)(2,1)S(1)} %get-tuple-element.27), channel_id=1, source_target_pairs={{0,10},{1,11},{2,8},{3,9},{4,14},{5,15},{6,12},{7,13},{8,2},{9,3},... | collective-permute-start | bytes 165896 | tf_op jit(solution)/shard_map/ppermute | solution.py:373
  145.2 7.0 %collective-permute-start.12 = (bf16[27,8,128]{2,1,0:T(8,128)(2,1)S(1)}, bf16[27,8,128]{2,1,0:T(8,128)(2,1)S(1)}, u32[]{:S(2)}, u32[]{:S(2)}) collective-permute-start(bf16[27,8,128]{2,1,0:T(8,128)(2,1)S(1)} %get-tuple-element.28), channel_id=1, source_target_pairs={{0,12},{1,13},{2,14},{3,15},{4,8},{5,9},{6,10},{7,11},{8,4},{9,5},... | collective-permute-start | bytes 165896 | tf_op jit(solution)/shard_map/ppermute | solution.py:373
  146.6 7.0 %collective-permute-start.13 = (bf16[27,8,128]{2,1,0:T(8,128)(2,1)S(1)}, bf16[27,8,128]{2,1,0:T(8,128)(2,1)S(1)}, u32[]{:S(2)}, u32[]{:S(2)}) collective-permute-start(bf16[27,8,128]{2,1,0:T(8,128)(2,1)S(1)} %get-tuple-element.29), channel_id=1, source_target_pairs={{0,14},{1,15},{2,12},{3,13},{4,10},{5,11},{6,8},{7,9},{8,6},{9,7},... | collective-permute-start | bytes 165896 | tf_op jit(solution)/shard_map/ppermute | solution.py:373

commit v3 on v2

--- a/solution.py
+++ b/solution.py
@@ -16,7 +16,8 @@
 MASKED = -1e30
 VMEM = pltpu.MemorySpace.VMEM
 SMEM = pltpu.MemorySpace.SMEM
-LIMIT = 48 * 1024 * 1024
+LIMIT = 32 * 1024 * 1024
+SMALL = 8 * 1024 * 1024
 
 
 def whole(space):
@@ -53,59 +54,54 @@
         in_specs=[whole(SMEM), whole(VMEM), whole(VMEM), whole(VMEM)],
         out_specs=whole(VMEM),
         scratch_shapes=[pltpu.VMEM((blocks * 8, 128), jnp.float32)],
+        compiler_params=pltpu.CompilerParams(vmem_limit_bytes=SMALL),
         name="message",
     )(context_len, prefill_q, decode_q.reshape(rows_d, HQ * HD), page_owner.reshape(1, -1))
 
 
-def pack_kernel(shards, capacity, owners, counts, pages, out, held, blank, taken, sem_in, sem_out):
+def pack_kernel(shards, first, depth, owners, counts, pages, out, taken):
     me = lax.axis_index("seq")
-    fetch = pltpu.make_async_copy(pages, held, sem_in)
-    fetch.start()
-    blank[...] = jnp.zeros_like(blank)
+    blank = jnp.zeros(pages.shape[1:], pages.dtype)
 
     def reset(o, carry):
         taken[o] = 0
         return carry
 
     lax.fori_loop(0, shards, reset, 0)
-    fetch.wait()
+
+    def clear(i, carry):
+        out[i] = blank
+        return carry
+
+    lax.fori_loop(0, shards * depth, clear, 0, unroll=4)
 
     def place(j, carry):
         o = owners[j]
-        k = taken[o]
-        taken[o] = k + 1
-        pltpu.make_async_copy(held.at[j], out.at[o * capacity + k], sem_out).start()
+        k = taken[o] - first
+        taken[o] = k + first + 1
+
+        @pl.when((k >= 0) & (k < depth))
+        def _():
+            out[o * depth + k] = pages[j]
+
         return carry
 
     lax.fori_loop(0, counts[me], place, 0)
 
-    def fill(o, carry):
-        def one(k, inner):
-            pltpu.make_async_copy(blank, out.at[o * capacity + k], sem_out).start()
-            return inner
-
-        return lax.fori_loop(taken[o], capacity, one, carry)
-
-    lax.fori_loop(0, shards, fill, 0)
-    pltpu.make_async_copy(out, out, sem_out).wait()
-
-
-def pack(owners, counts, pages, shards, capacity):
+
+def pack(owners, counts, pages, shards, first, depth, limit=None):
     slots = pages.shape[0]
     return pl.pallas_call(
-        functools.partial(pack_kernel, shards, capacity),
-        out_shape=jax.ShapeDtypeStruct((shards * capacity, PAGE, KVD), pages.dtype),
-        in_specs=[whole(SMEM), whole(SMEM), whole(pl.ANY)],
-        out_specs=whole(pl.ANY),
-        scratch_shapes=[
-            pltpu.VMEM((slots, PAGE, KVD), pages.dtype),
-            pltpu.VMEM((PAGE, KVD), pages.dtype),
-            pltpu.SMEM((shards,), jnp.int32),
-            pltpu.SemaphoreType.DMA,
-            pltpu.SemaphoreType.DMA,
-        ],
+        functools.partial(pack_kernel, shards, first, depth),
+        out_shape=jax.ShapeDtypeStruct((shards * depth, PAGE, KVD), pages.dtype),
+        in_specs=[whole(SMEM), whole(SMEM), whole(VMEM)],
+        out_specs=whole(VMEM),
+        scratch_shapes=[pltpu.SMEM((shards,), jnp.int32)],
+        compiler_params=pltpu.CompilerParams(vmem_limit_bytes=limit),
         cost_estimate=pl.CostEstimate(
-            flops=0, transcendentals=0, bytes_accessed=(slots + shards * capacity) * PAGE * KVD * 2
+            flops=0,
+            transcendentals=0,
+            bytes_accessed=(slots + shards * depth) * PAGE * KVD * 2,
         ),
         name="pack",
     )(owners, counts, pages)
@@ -288,11 +284,49 @@
         in_specs=[whole(VMEM)],
         out_specs=whole(pl.ANY),
         scratch_shapes=[pltpu.SemaphoreType.DMA((pieces,))],
-        cost_estimate=pl.CostEstimate(
-            flops=0, transcendentals=0, bytes_accessed=2 * source.size * 2
-        ),
+        compiler_params=pltpu.CompilerParams(vmem_limit_bytes=SMALL),
+        cost_estimate=pl.CostEstimate(flops=0, transcendentals=0, bytes_accessed=4 * source.size),
         name="settle",
     )(source)
+
+
+def join_kernel(*refs):
+    sources, (out, held, sems_in, sems_out) = refs[:-4], refs[-4:]
+    base = 0
+    fetches, puts = [], []
+    for i, source in enumerate(sources):
+        span = pl.ds(base, source.shape[1])
+        fetches.append(pltpu.make_async_copy(source, held.at[:, span], sems_in.at[i]))
+        puts.append(pltpu.make_async_copy(held.at[:, span], out.at[:, span], sems_out.at[i]))
+        base += source.shape[1]
+    for fetch in fetches:
+        fetch.start()
+    for fetch, put in zip(fetches, puts):
+        fetch.wait()
+        put.start()
+    for put in puts:
+        put.wait()
+
+
+def join(shards, *sources):
+    sources = [source.reshape(shards, -1, PAGE, KVD) for source in sources]
+    depth = sum(source.shape[1] for source in sources)
+    shape = (shards, depth, PAGE, KVD)
+    return pl.pallas_call(
+        join_kernel,
+        out_shape=jax.ShapeDtypeStruct(shape, sources[0].dtype),
+        in_specs=[whole(pl.ANY)] * len(sources),
+        out_specs=whole(pl.ANY),
+        scratch_shapes=[
+            pltpu.VMEM(shape, sources[0].dtype),
+            pltpu.SemaphoreType.DMA((len(sources),)),
+            pltpu.SemaphoreType.DMA((len(sources),)),
+        ],
+        cost_estimate=pl.CostEstimate(
+            flops=0, transcendentals=0, bytes_accessed=4 * shards * depth * PAGE * KVD
+        ),
+        name="join",
+    )(*sources)
 
 
 def merge_kernel(rows_p, rows_d, message, new_k, new_v, *refs):
@@ -389,17 +423,20 @@
     pages_k = cache_k.reshape(page_slots, PAGE, KVD)
     pages_v = cache_v.reshape(page_slots, PAGE, KVD)
     rows = rows_p + rows_d
+    lead = max(1, capacity // 4)
+    early_k = pack(owners, page_counts, pages_k, shards, 0, lead, SMALL)
+    store_k1 = exchange(early_k)
     message = make_message(prefill_q, decode_q, page_owner, context_len)
     far = [message]
     for k in range(4, shards, 4):
         far.append(swap(message, k))
-    packed_k = pack(owners, page_counts, pages_k, shards, capacity)
-    packed_v = pack(owners, page_counts, pages_v, shards, capacity)
+    late_k = pack(owners, page_counts, pages_k, shards, lead, capacity - lead)
+    packed_v = pack(owners, page_counts, pages_v, shards, 0, capacity)
+    store_k2 = exchange(late_k)
     own = jnp.concatenate(far, axis=0)
     across = swap(own, 2)
     beside = swap(own, 1)
     corner = swap(across, 1)
-    store_k = exchange(packed_k)
     keep, give, table = attend(
         rows_p,
         rows_d,
@@ -414,10 +451,9 @@
     parts = [folded[0]]
     for j in range(1, shards // 2):
         parts.append(swap(folded[j], 2 * j))
-    packed_v, store_k = lax.optimization_barrier((packed_v, store_k))
     store_v = exchange(packed_v)
     prefill_out, decode_out = merge(rows_p, rows_d, parts, message, decode_k, decode_v)
-    store_k = settle(store_k)
+    store_k = join(shards, store_k1, store_k2)
     store_v = settle(store_v)
     store_page = table[:, :capacity].reshape(-1)
     return (

time: 161 us -> 171 us (1.062)
  local copies, waits for them, and re-layouts: 0.63 us -> 6.36 us
  waiting for transfers between devices: 96.2 us -> 99 us
  starting transfers between devices: 36.2 us -> 38.5 us
    unnamed x12 -> x26, local copies, waits for them, and re-layouts: 0.03 us -> 5.76 us
    pallas_call x2 -> x4, Pallas kernels: 6.82 us -> 12.1 us  [the longest x3 9.37 us: pack(): pl.pallas_call(functools.partial(pack_kernel, shards, first, depth), out_...]
    pallas_call x2 -> x1, Pallas kernels: 5.87 us -> 1.35 us  [settle(): pl.pallas_call(functools.partial(settle_kernel, pieces), out_shape=jax.Sh...]
    all_to_all x2 -> x3, starting transfers between devices: 18.8 us -> 21 us  [exchange(): return lax.all_to_all(array, 'seq', split_axis=0, concat_axis=0, tiled=True)]
    all_to_all x2 -> x3, waiting for transfers between devices: 37.6 us -> 39 us  [exchange(): return lax.all_to_all(array, 'seq', split_axis=0, concat_axis=0, tiled=True)]
  transfers between devices with their start and end apart: 16 -> 17, of which waited for: 8 -> 9; matrix products, arithmetic and copies ran while one was open for 1% -> 0% of each run, Pallas kernels for 12% -> 13%
where the time goes in v3:
time: 171 us; the launch traced here: 170 us
  waiting for transfers between devices  99 us (58%)
  starting transfers between devices  38.5 us (23%)
  Pallas kernels  25 us (15%)
  local copies, waits for them, and re-layouts  6.36 us (4%)
    ppermute x14, waiting for transfers between devices, swap(): lax.ppermute(array, 'seq', [(i, i ^ distance) for i in range(shards)])  60 us
    all_to_all x3, waiting for transfers between devices, exchange(): return lax.all_to_all(array, 'seq', split_axis=0, concat_axis=0, tiled=True)  39 us
    all_to_all x3, starting transfers between devices, exchange(): return lax.all_to_all(array, 'seq', split_axis=0, concat_axis=0, tiled=True)  21 us
    ppermute x14, starting transfers between devices, swap(): lax.ppermute(array, 'seq', [(i, i ^ distance) for i in range(shards)])  17.4 us
    pallas_call x3, Pallas kernels, pack(): pl.pallas_call(functools.partial(pack_kernel, shards, first, depth), out_...  9.37 us
    pallas_call x1, Pallas kernels, attend(): pl.pallas_call(functools.partial(attend_kernel, rows_p, rows_d, capacity)...  7.51 us
    unnamed x26, local copies, waits for them, and re-layouts  5.76 us
  transfers between devices with their start and end apart: 17, of which 9 were waited for; matrix products, arithmetic and copies ran while one was open for 0% of the time, Pallas kernels for 13%

profile of v3, /device:TPU:0, one launch (start us, length us, event | category | flops | bytes accessed | tf_op | source)
XLA Modules:
  0.0 170.3 jit_solution(447594523700104150)
XLA Ops:
  0.6 0.0 copy-start
  0.6 1.2 copy-done
  1.9 0.0 copy-start.5
  1.9 0.7 copy-done.5
  2.5 0.0 copy-start.7
  2.5 0.7 copy-done.7
  3.2 2.3 %pack.3 = bf16[32,8,1024]{2,1,0:T(8,128)(2,1)} custom-call(s32[64]{0:T(128)S(1)} %bitcast.19, s32[16]{0:T(128)S(1)} %copy-done.7, bf16[64,8,1024]{2,1,0:T(8,128)(2,1)S(1)} %bitcast.14), custom_call_target="tpu_custom_call" | custom-call | bytes 1572864 | tf_op jit(solution)/shard_map/pack/pallas_call | solution.py:94
  5.5 7.8 %all-to-all-start = ((bf16[32,8,1024]{2,1,0:T(8,128)(2,1)}), bf16[32,8,1024]{2,1,0:T(8,128)(2,1)S(1)}, u32[]{:S(2)}, u32[]{:S(2)}) async-start(bf16[32,8,1024]{2,1,0:T(8,128)(2,1)} %pack.3), calls=%async_computation | async-start | bytes 1048576 | tf_op jit(solution)/shard_map/all_to_all | solution.py:411
  13.2 3.5 %pack.4 = bf16[96,8,1024]{2,1,0:T(8,128)(2,1)} custom-call(s32[64]{0:T(128)} %bitcast.17, s32[16]{0:T(128)} %counts.7, bf16[64,8,1024]{2,1,0:T(8,128)(2,1)} %bitcast.13), custom_call_target="tpu_custom_call" | custom-call | bytes 2621440 | tf_op jit(solution)/shard_map/pack/pallas_call | solution.py:94
  16.7 10.8 %all-to-all-done = bf16[32,8,1024]{2,1,0:T(8,128)(2,1)S(1)} async-done(((bf16[32,8,1024]{2,1,0:T(8,128)(2,1)}), bf16[32,8,1024]{2,1,0:T(8,128)(2,1)S(1)}, u32[]{:S(2)}, u32[]{:S(2)}) %all-to-all-start) | async-done | bytes 524320 | tf_op jit(solution)/shard_map/all_to_all | solution.py:411
  27.5 0.0 copy-start.12
  27.5 0.8 copy-done.12
  28.3 4.2 %all-to-all-start.1 = ((bf16[96,8,1024]{2,1,0:T(8,128)(2,1)}), bf16[96,8,1024]{2,1,0:T(8,128)(2,1)S(1)}, u32[]{:S(2)}, u32[]{:S(2)}) async-start(bf16[96,8,1024]{2,1,0:T(8,128)(2,1)} %pack.4), calls=%async_computation.1 | async-start | bytes 3145728 | tf_op jit(solution)/shard_map/all_to_all | solution.py:411
  32.5 3.6 %pack.5 = bf16[128,8,1024]{2,1,0:T(8,128)(2,1)} custom-call(s32[64]{0:T(128)} %bitcast.18, s32[16]{0:T(128)} %counts.7, bf16[64,8,1024]{2,1,0:T(8,128)(2,1)} %bitcast.15), custom_call_target="tpu_custom_call" | custom-call | bytes 3145728 | tf_op jit(solution)/shard_map/pack/pallas_call | solution.py:94
  36.1 0.0 copy-start.8
  36.1 28.2 %all-to-all-done.1 = bf16[96,8,1024]{2,1,0:T(8,128)(2,1)S(1)} async-done(((bf16[96,8,1024]{2,1,0:T(8,128)(2,1)}), bf16[96,8,1024]{2,1,0:T(8,128)(2,1)S(1)}, u32[]{:S(2)}, u32[]{:S(2)}) %all-to-all-start.1) | async-done | bytes 1572896 | tf_op jit(solution)/shard_map/all_to_all | solution.py:411
  64.3 1.2 copy-done.11
  65.5 9.1 %all-to-all-start.2 = ((bf16[128,8,1024]{2,1,0:T(8,128)(2,1)}), bf16[128,8,1024]{2,1,0:T(8,128)(2,1)S(1)}, u32[]{:S(2)}, u32[]{:S(2)}) async-start(bf16[128,8,1024]{2,1,0:T(8,128)(2,1)} %pack.5), calls=%async_computation.2 | async-start | bytes 4194304 | tf_op jit(solution)/shard_map/all_to_all | solution.py:411
  75.2 0.0 copy-done.3
  75.3 0.0 copy-done.4
  75.3 0.0 copy-done.6
  75.3 0.1 message.1
  75.4 0.0 copy-start.9
  75.4 0.0 copy-start.10
  75.4 3.8 %collective-permute-start.2 = (bf16[25,8,128]{2,1,0:T(8,128)(2,1)S(1)}, bf16[25,8,128]{2,1,0:T(8,128)(2,1)S(1)}, u32[]{:S(2)}, u32[]{:S(2)}) collective-permute-start(bf16[25,8,128]{2,1,0:T(8,128)(2,1)S(1)} %message.1), channel_id=1, source_target_pairs={{0,12},{1,13},{2,14},{3,15},{4,8},{5,9},{6,10},{7,11},{8,4},{9,5},... | collective-permute-start | bytes 153608 | tf_op jit(solution)/shard_map/ppermute | solution.py:407
  79.2 0.0 collective-permute-start.1
  79.2 0.7 collective-permute-start
  79.8 35.3 %collective-permute-done.2 = bf16[25,8,128]{2,1,0:T(8,128)(2,1)S(1)} collective-permute-done((bf16[25,8,128]{2,1,0:T(8,128)(2,1)S(1)}, bf16[25,8,128]{2,1,0:T(8,128)(2,1)S(1)}, u32[]{:S(2)}, u32[]{:S(2)}) %collective-permute-start.2) | collective-permute-done | bytes 51232 | tf_op jit(solution)/shard_map/ppermute | solution.py:407
  115.1 12.9 %collective-permute-done.1 = bf16[25,8,128]{2,1,0:T(8,128)(2,1)S(1)} collective-permute-done((bf16[25,8,128]{2,1,0:T(8,128)(2,1)S(1)}, bf16[25,8,128]{2,1,0:T(8,128)(2,1)S(1)}, u32[]{:S(2)}, u32[]{:S(2)}) %collective-permute-start.1) | collective-permute-done | bytes 51232 | tf_op jit(solution)/shard_map/ppermute | solution.py:407
  128.0 0.0 collective-permute-done
  128.1 1.6 collective-permute-start.4
  129.6 0.0 collective-permute-start.3
  129.6 4.7 %collective-permute-done.4.refs_2_ = bf16[100,8,128]{2,1,0:T(8,128)(2,1)S(1)} collective-permute-done((bf16[100,8,128]{2,1,0:T(8,128)(2,1)S(1)}, bf16[100,8,128]{2,1,0:T(8,128)(2,1)S(1)}, u32[]{:S(2)}, u32[]{:S(2)}) %collective-permute-start.4) | collective-permute-done | bytes 204832 | tf_op jit(solution)/shard_map/ppermute | solution.py:407
  134.3 0.0 collective-permute-start.5
  134.4 0.0 collective-permute-done.3.refs_1_
  134.4 1.4 collective-permute-done.5.refs_3_
  135.8 0.0 copy-done.1
  135.8 0.0 copy-done.8
  135.8 1.2 copy-done.2
  137.0 7.5 %attend.1 = (bf16[8,27,8,128]{3,2,1,0:T(8,128)(2,1)S(1)}, bf16[8,27,8,128]{3,2,1,0:T(8,128)(2,1)S(1)}, s32[16,128]{1,0:T(8,128)S(1)}) custom-call(s32[16]{0:T(128)S(1)} %copy-done.8, bf16[100,8,128]{2,1,0:T(8,128)(2,1)S(1)} %pad_maximum_fusion.refs_0_, bf16[100,8,128]{2,1,0:T(8,128)(2,1)S(1)} %collective-permute-done.3.refs_1_, ...), custom_call_target="tpu_custom_call" | custom-call | flops 805306368 | bytes 3670016 | tf_op jit(solution)/shard_map/attend/pallas_call | solution.py:209
  144.6 0.2 collective-permute-start.6
  144.8 1.7 collective-permute-done.6.got
  146.4 2.6 %fold.1 = (bf16[27,8,128]{2,1,0:T(8,128)(2,1)S(1)}, bf16[27,8,128]{2,1,0:T(8,128)(2,1)S(1)}, bf16[27,8,128]{2,1,0:T(8,128)(2,1)S(1)}, bf16[27,8,128]{2,1,0:T(8,1...) custom-call(bf16[8,27,8,128]{3,2,1,0:T(8,128)(2,1)S(1)} %get-tuple-e, ...), custom_call_target="tpu_custom_call" | custom-call | flops 884736 | bytes 1327104 | tf_op jit(solution)/shard_map/fold/pallas_call | solution.py:253
  149.0 1.6 collective-permute-start.7
  150.5 0.0 collective-permute-start.8
  150.6 2.0 %collective-permute-start.9 = (bf16[27,8,128]{2,1,0:T(8,128)(2,1)S(1)}, bf16[27,8,128]{2,1,0:T(8,128)(2,1)S(1)}, u32[]{:S(2)}, u32[]{:S(2)}) collective-permute-start(bf16[27,8,128]{2,1,0:T(8,128)(2,1)S(1)} %get-tuple-element.23), channel_id=1, source_target_pairs={{0,6},{1,7},{2,4},{3,5},{4,2},{5,3},{6,0},{7,1},{8,14},{9,15},{10,... | collective-permute-start | bytes 165896 | tf_op jit(solution)/shard_map/ppermute | solution.py:407
  152.5 0.0 collective-permute-start.10
  152.5 3.9 %collective-permute-start.11 = (bf16[27,8,128]{2,1,0:T(8,128)(2,1)S(1)}, bf16[27,8,128]{2,1,0:T(8,128)(2,1)S(1)}, u32[]{:S(2)}, u32[]{:S(2)}) collective-permute-start(bf16[27,8,128]{2,1,0:T(8,128)(2,1)S(1)} %get-tuple-element.25), channel_id=1, source_target_pairs={{0,10},{1,11},{2,8},{3,9},{4,14},{5,15},{6,12},{7,13},{8,2},{9,3},... | collective-permute-start | bytes 165896 | tf_op jit(solution)/shard_map/ppermute | solution.py:407
  156.4 0.0 collective-permute-done.7.refs_1_
  156.4 1.4 collective-permute-start.12
  157.8 0.0 collective-permute-done.8.refs_2_
  157.8 2.4 %collective-permute-start.13 = (bf16[27,8,128]{2,1,0:T(8,128)(2,1)S(1)}, bf16[27,8,128]{2,1,0:T(8,128)(2,1)S(1)}, u32[]{:S(2)}, u32[]{:S(2)}) collective-permute-start(bf16[27,8,128]{2,1,0:T(8,128)(2,1)S(1)} %get-tuple-element.27), channel_id=1, source_target_pairs={{0,14},{1,15},{2,12},{3,13},{4,10},{5,11},{6,8},{7,9},{8,6},{9,7},... | collective-permute-start | bytes 165896 | tf_op jit(solution)/shard_map/ppermute | solution.py:407
  160.2 0.6 reshape.61
  160.8 0.0 collective-permute-done.9.refs_3_
  160.8 0.0 collective-permute-done.10.refs_4_
  160.8 2.6 %collective-permute-done.11.refs_5_ = bf16[27,8,128]{2,1,0:T(8,128)(2,1)S(1)} collective-permute-done((bf16[27,8,128]{2,1,0:T(8,128)(2,1)S(1)}, bf16[27,8,128]{2,1,0:T(8,128)(2,1)S(1)}, u32[]{:S(2)}, u32[]{:S(2)}) %collective-permute-start.11) | collective-permute-done | bytes 55328 | tf_op jit(solution)/shard_map/ppermute | solution.py:407
  163.4 0.0 collective-permute-done.12.refs_6_
  163.4 1.3 collective-permute-done.13.refs_7_
  164.7 0.0 copy-done.9
  164.7 0.0 copy-done.10
  164.7 1.4 merge.1
  166.2 2.8 %join.1 = bf16[16,8,8,1024]{3,2,1,0:T(8,128)(2,1)} custom-call(bf16[16,2,8,1024]{3,2,1,0:T(8,128)(2,1)} %bitcast.27, bf16[16,6,8,1024]{3,2,1,0:T(8,128)(2,1)} %bitcast.24), custom_call_target="tpu_custom_call" | custom-call | bytes 4194304 | tf_op jit(solution)/shard_map/join/pallas_call | solution.py:315
  168.9 0.0 all-to-all-done.2.source
  168.9 1.3 settle.1
  (7 shorter events, 0.0 us)
Async XLA Ops:
  0.6 1.2 copy-start
  1.9 0.7 copy-start.5
  2.5 0.7 copy-start.7
  5.5 22.0 %all-to-all-start = ((bf16[32,8,1024]{2,1,0:T(8,128)(2,1)}), bf16[32,8,1024]{2,1,0:T(8,128)(2,1)S(1)}, u32[]{:S(2)}, u32[]{:S(2)}) async-start(bf16[32,8,1024]{2,1,0:T(8,128)(2,1)} %pack.3), calls=%async_computation | async-start | bytes 1048576 | tf_op jit(solution)/shard_map/all_to_all | solution.py:411
  27.5 0.8 copy-start.12
  28.3 36.0 %all-to-all-start.1 = ((bf16[96,8,1024]{2,1,0:T(8,128)(2,1)}), bf16[96,8,1024]{2,1,0:T(8,128)(2,1)S(1)}, u32[]{:S(2)}, u32[]{:S(2)}) async-start(bf16[96,8,1024]{2,1,0:T(8,128)(2,1)} %pack.4), calls=%async_computation.1 | async-start | bytes 3145728 | tf_op jit(solution)/shard_map/all_to_all | solution.py:411
  36.1 39.2 %copy-start.3 = (bf16[1,8192]{1,0:T(2,128)(2,1)S(1)}, bf16[1,8192]{1,0:T(2,128)(2,1)}, u32[]{:S(2)}) copy-start(bf16[1,8192]{1,0:T(2,128)(2,1)} %prefill_q.1) | copy-start | bytes 49156
  36.1 39.2 %copy-start.4 = (bf16[1,2,8192]{2,1,0:T(2,128)(2,1)S(1)}, bf16[1,2,8192]{2,1,0:T(2,128)(2,1)}, u32[]{:S(2)}) copy-start(bf16[1,2,8192]{2,1,0:T(2,128)(2,1)} %param.14) | copy-start | bytes 98308
  36.1 39.2 %copy-start.6 = (s32[64,1]{0,1:T(1,128)S(1)}, s32[64,1]{0,1:T(1,128)}, u32[]{:S(2)}) copy-start(s32[64,1]{0,1:T(1,128)} %param.13) | copy-start | bytes 772
  36.1 99.7 %copy-start.1 = (bf16[512,1024]{1,0:T(8,128)(2,1)S(1)}, bf16[512,1024]{1,0:T(8,128)(2,1)}, u32[]{:S(2)}) copy-start(bf16[512,1024]{1,0:T(8,128)(2,1)} %refs_4_.1) | copy-start | bytes 3145732
  36.1 99.7 %copy-start.8 = (s32[16]{0:T(128)S(1)}, s32[16]{0:T(128)}, u32[]{:S(2)}) copy-start(s32[16]{0:T(128)} %counts.7) | copy-start | bytes 196
  64.3 1.2 copy-start.11
  65.5 103.4 %all-to-all-start.2 = ((bf16[128,8,1024]{2,1,0:T(8,128)(2,1)}), bf16[128,8,1024]{2,1,0:T(8,128)(2,1)S(1)}, u32[]{:S(2)}, u32[]{:S(2)}) async-start(bf16[128,8,1024]{2,1,0:T(8,128)(2,1)} %pack.5), calls=%async_computation.2 | async-start | bytes 4194304 | tf_op jit(solution)/shard_map/all_to_all | solution.py:411
  75.4 89.4 %copy-start.9 = (bf16[1,2,1024]{2,1,0:T(2,128)(2,1)S(1)}, bf16[1,2,1024]{2,1,0:T(2,128)(2,1)}, u32[]{:S(2)}) copy-start(bf16[1,2,1024]{2,1,0:T(2,128)(2,1)} %param.15) | copy-start | bytes 12292
  75.4 89.4 %copy-start.10 = (bf16[1,2,1024]{2,1,0:T(2,128)(2,1)S(1)}, bf16[1,2,1024]{2,1,0:T(2,128)(2,1)}, u32[]{:S(2)}) copy-start(bf16[1,2,1024]{2,1,0:T(2,128)(2,1)} %param.16) | copy-start | bytes 12292
  75.4 39.7 %collective-permute-start.2 = (bf16[25,8,128]{2,1,0:T(8,128)(2,1)S(1)}, bf16[25,8,128]{2,1,0:T(8,128)(2,1)S(1)}, u32[]{:S(2)}, u32[]{:S(2)}) collective-permute-start(bf16[25,8,128]{2,1,0:T(8,128)(2,1)S(1)} %message.1), channel_id=1, source_target_pairs={{0,12},{1,13},{2,14},{3,15},{4,8},{5,9},{6,10},{7,11},{8,4},{9,5},... | collective-permute-start | bytes 153608 | tf_op jit(solution)/shard_map/ppermute | solution.py:407
  79.2 48.8 %collective-permute-start.1 = (bf16[25,8,128]{2,1,0:T(8,128)(2,1)S(1)}, bf16[25,8,128]{2,1,0:T(8,128)(2,1)S(1)}, u32[]{:S(2)}, u32[]{:S(2)}) collective-permute-start(bf16[25,8,128]{2,1,0:T(8,128)(2,1)S(1)} %message.1), channel_id=1, source_target_pairs={{0,8},{1,9},{2,10},{3,11},{4,12},{5,13},{6,14},{7,15},{8,0},{9,1},... | collective-permute-start | bytes 153608 | tf_op jit(solution)/shard_map/ppermute | solution.py:407
  79.2 48.8 %collective-permute-start = (bf16[25,8,128]{2,1,0:T(8,128)(2,1)S(1)}, bf16[25,8,128]{2,1,0:T(8,128)(2,1)S(1)}, u32[]{:S(2)}, u32[]{:S(2)}) collective-permute-start(bf16[25,8,128]{2,1,0:T(8,128)(2,1)S(1)} %message.1), channel_id=1, source_target_pairs={{0,4},{1,5},{2,6},{3,7},{4,0},{5,1},{6,2},{7,3},{8,12},{9,13},{10,... | collective-permute-start | bytes 153608 | tf_op jit(solution)/shard_map/ppermute | solution.py:407
  128.1 6.3 %collective-permute-start.4 = (bf16[100,8,128]{2,1,0:T(8,128)(2,1)S(1)}, bf16[100,8,128]{2,1,0:T(8,128)(2,1)S(1)}, u32[]{:S(2)}, u32[]{:S(2)}) collective-permute-start(bf16[100,8,128]{2,1,0:T(8,128)(2,1)S(1)} %pad_maximum_fusion.refs_0_), channel_id=1, source_target_pairs={{0,2},{1,3},{2,0},{3,1},{4,6},{5,7},{6,4},{7,5},{8,10},{9,11},{10,... | collective-permute-start | bytes 614408 | tf_op jit(solution)/shard_map/ppermute | solution.py:407
  129.6 4.7 %collective-permute-start.3 = (bf16[100,8,128]{2,1,0:T(8,128)(2,1)S(1)}, bf16[100,8,128]{2,1,0:T(8,128)(2,1)S(1)}, u32[]{:S(2)}, u32[]{:S(2)}) collective-permute-start(bf16[100,8,128]{2,1,0:T(8,128)(2,1)S(1)} %pad_maximum_fusion.refs_0_), channel_id=1, source_target_pairs={{0,1},{1,0},{2,3},{3,2},{4,5},{5,4},{6,7},{7,6},{8,9},{9,8},{10,11... | collective-permute-start | bytes 614408 | tf_op jit(solution)/shard_map/ppermute | solution.py:407
  134.3 1.5 collective-permute-start.5
  135.8 1.2 copy-start.2
  144.6 1.9 %collective-permute-start.6 = (bf16[8,27,8,128]{3,2,1,0:T(8,128)(2,1)S(1)}, bf16[8,27,8,128]{3,2,1,0:T(8,128)(2,1)S(1)}, u32[]{:S(2)}, u32[]{:S(2)}) collective-permute-start(bf16[8,27,8,128]{3,2,1,0:T(8,128)(2,1)S(1)} %get-tuple-element.19), channel_id=1, source_target_pairs={{0,1},{1,0},{2,3},{3,2},{4,5},{5,4},{6,7},{7,6},{8,9},{9,8},{10,11... | collective-permute-start | bytes 1327112 | tf_op jit(solution)/shard_map/ppermute | solution.py:407
  149.0 7.4 %collective-permute-start.7 = (bf16[27,8,128]{2,1,0:T(8,128)(2,1)S(1)}, bf16[27,8,128]{2,1,0:T(8,128)(2,1)S(1)}, u32[]{:S(2)}, u32[]{:S(2)}) collective-permute-start(bf16[27,8,128]{2,1,0:T(8,128)(2,1)S(1)} %get-tuple-element.21), channel_id=1, source_target_pairs={{0,2},{1,3},{2,0},{3,1},{4,6},{5,7},{6,4},{7,5},{8,10},{9,11},{10,... | collective-permute-start | bytes 165896 | tf_op jit(solution)/shard_map/ppermute | solution.py:407
  150.5 7.2 %collective-permute-start.8 = (bf16[27,8,128]{2,1,0:T(8,128)(2,1)S(1)}, bf16[27,8,128]{2,1,0:T(8,128)(2,1)S(1)}, u32[]{:S(2)}, u32[]{:S(2)}) collective-permute-start(bf16[27,8,128]{2,1,0:T(8,128)(2,1)S(1)} %get-tuple-element.22), channel_id=1, source_target_pairs={{0,4},{1,5},{2,6},{3,7},{4,0},{5,1},{6,2},{7,3},{8,12},{9,13},{10,... | collective-permute-start | bytes 165896 | tf_op jit(solution)/shard_map/ppermute | solution.py:407
  150.6 10.2 %collective-permute-start.9 = (bf16[27,8,128]{2,1,0:T(8,128)(2,1)S(1)}, bf16[27,8,128]{2,1,0:T(8,128)(2,1)S(1)}, u32[]{:S(2)}, u32[]{:S(2)}) collective-permute-start(bf16[27,8,128]{2,1,0:T(8,128)(2,1)S(1)} %get-tuple-element.23), channel_id=1, source_target_pairs={{0,6},{1,7},{2,4},{3,5},{4,2},{5,3},{6,0},{7,1},{8,14},{9,15},{10,... | collective-permute-start | bytes 165896 | tf_op jit(solution)/shard_map/ppermute | solution.py:407
  152.5 8.3 %collective-permute-start.10 = (bf16[27,8,128]{2,1,0:T(8,128)(2,1)S(1)}, bf16[27,8,128]{2,1,0:T(8,128)(2,1)S(1)}, u32[]{:S(2)}, u32[]{:S(2)}) collective-permute-start(bf16[27,8,128]{2,1,0:T(8,128)(2,1)S(1)} %get-tuple-element.24), channel_id=1, source_target_pairs={{0,8},{1,9},{2,10},{3,11},{4,12},{5,13},{6,14},{7,15},{8,0},{9,1},... | collective-permute-start | bytes 165896 | tf_op jit(solution)/shard_map/ppermute | solution.py:407
  152.5 10.9 %collective-permute-start.11 = (bf16[27,8,128]{2,1,0:T(8,128)(2,1)S(1)}, bf16[27,8,128]{2,1,0:T(8,128)(2,1)S(1)}, u32[]{:S(2)}, u32[]{:S(2)}) collective-permute-start(bf16[27,8,128]{2,1,0:T(8,128)(2,1)S(1)} %get-tuple-element.25), channel_id=1, source_target_pairs={{0,10},{1,11},{2,8},{3,9},{4,14},{5,15},{6,12},{7,13},{8,2},{9,3},... | collective-permute-start | bytes 165896 | tf_op jit(solution)/shard_map/ppermute | solution.py:407
  156.4 7.0 %collective-permute-start.12 = (bf16[27,8,128]{2,1,0:T(8,128)(2,1)S(1)}, bf16[27,8,128]{2,1,0:T(8,128)(2,1)S(1)}, u32[]{:S(2)}, u32[]{:S(2)}) collective-permute-start(bf16[27,8,128]{2,1,0:T(8,128)(2,1)S(1)} %get-tuple-element.26), channel_id=1, source_target_pairs={{0,12},{1,13},{2,14},{3,15},{4,8},{5,9},{6,10},{7,11},{8,4},{9,5},... | collective-permute-start | bytes 165896 | tf_op jit(solution)/shard_map/ppermute | solution.py:407
  157.8 7.0 %collective-permute-start.13 = (bf16[27,8,128]{2,1,0:T(8,128)(2,1)S(1)}, bf16[27,8,128]{2,1,0:T(8,128)(2,1)S(1)}, u32[]{:S(2)}, u32[]{:S(2)}) collective-permute-start(bf16[27,8,128]{2,1,0:T(8,128)(2,1)S(1)} %get-tuple-element.27), channel_id=1, source_target_pairs={{0,14},{1,15},{2,12},{3,13},{4,10},{5,11},{6,8},{7,9},{8,6},{9,7},... | collective-permute-start | bytes 165896 | tf_op jit(solution)/shard_map/ppermute | solution.py:407

commit v4 on v3

--- a/solution.py
+++ b/solution.py
@@ -423,16 +423,13 @@
     pages_k = cache_k.reshape(page_slots, PAGE, KVD)
     pages_v = cache_v.reshape(page_slots, PAGE, KVD)
     rows = rows_p + rows_d
-    lead = max(1, capacity // 4)
-    early_k = pack(owners, page_counts, pages_k, shards, 0, lead, SMALL)
-    store_k1 = exchange(early_k)
     message = make_message(prefill_q, decode_q, page_owner, context_len)
     far = [message]
     for k in range(4, shards, 4):
         far.append(swap(message, k))
-    late_k = pack(owners, page_counts, pages_k, shards, lead, capacity - lead)
+    packed_k = pack(owners, page_counts, pages_k, shards, 0, capacity)
+    store_k = exchange(packed_k)
     packed_v = pack(owners, page_counts, pages_v, shards, 0, capacity)
-    store_k2 = exchange(late_k)
     own = jnp.concatenate(far, axis=0)
     across = swap(own, 2)
     beside = swap(own, 1)
@@ -453,7 +450,7 @@
         parts.append(swap(folded[j], 2 * j))
     store_v = exchange(packed_v)
     prefill_out, decode_out = merge(rows_p, rows_d, parts, message, decode_k, decode_v)
-    store_k = join(shards, store_k1, store_k2)
+    store_k = join(shards, store_k)
     store_v = settle(store_v)
     store_page = table[:, :capacity].reshape(-1)
     return (

time: 171 us -> 162 us (0.947)
  local copies, waits for them, and re-layouts: 6.36 us -> 3.18 us
  starting transfers between devices: 38.5 us -> 36.4 us
  Pallas kernels: 25 us -> 23.1 us
    unnamed x26 -> x18, local copies, waits for them, and re-layouts: 5.76 us -> 2.58 us
    pallas_call x3 -> x2, Pallas kernels: 9.37 us -> 7.28 us  [pack(): pl.pallas_call(functools.partial(pack_kernel, shards, first, depth), out_...]
    all_to_all x3 -> x2, starting transfers between devices: 21 us -> 19 us  [exchange(): return lax.all_to_all(array, 'seq', split_axis=0, concat_axis=0, tiled=True)]
    all_to_all x3 -> x2, waiting for transfers between devices: 39 us -> 37.3 us  [exchange(): return lax.all_to_all(array, 'seq', split_axis=0, concat_axis=0, tiled=True)]
  transfers between devices with their start and end apart: 17 -> 16, of which waited for: 9 -> 8; matrix products, arithmetic and copies ran while one was open for 0% -> 0% of each run, Pallas kernels for 13% -> 11%
where the time goes in v4:
time: 162 us; the launch traced here: 161 us
  waiting for transfers between devices  97.3 us (60%)
  starting transfers between devices  36.4 us (22%)
  Pallas kernels  23.1 us (14%)
  local copies, waits for them, and re-layouts  3.18 us (2%)
    ppermute x14, waiting for transfers between devices, swap(): lax.ppermute(array, 'seq', [(i, i ^ distance) for i in range(shards)])  59.9 us
    all_to_all x2, waiting for transfers between devices, exchange(): return lax.all_to_all(array, 'seq', split_axis=0, concat_axis=0, tiled=True)  37.3 us
    all_to_all x2, starting transfers between devices, exchange(): return lax.all_to_all(array, 'seq', split_axis=0, concat_axis=0, tiled=True)  19 us
    ppermute x14, starting transfers between devices, swap(): lax.ppermute(array, 'seq', [(i, i ^ distance) for i in range(shards)])  17.4 us
    pallas_call x1, Pallas kernels, attend(): pl.pallas_call(functools.partial(attend_kernel, rows_p, rows_d, capacity)...  7.5 us
    pallas_call x2, Pallas kernels, pack(): pl.pallas_call(functools.partial(pack_kernel, shards, first, depth), out_...  7.28 us
  transfers between devices with their start and end apart: 16, of which 8 were waited for; matrix products, arithmetic and copies ran while one was open for 0% of the time, Pallas kernels for 11%

profile of v4, /device:TPU:0, one launch (start us, length us, event | category | flops | bytes accessed | tf_op | source)
XLA Modules:
  0.0 161.4 jit_solution(6782401913035190566)
XLA Ops:
  0.6 3.6 %pack.2 = bf16[128,8,1024]{2,1,0:T(8,128)(2,1)} custom-call(s32[64]{0:T(128)} %bitcast.16, s32[16]{0:T(128)} %counts.5, bf16[64,8,1024]{2,1,0:T(8,128)(2,1)} %bitcast.12), custom_call_target="tpu_custom_call" | custom-call | bytes 3145728 | tf_op jit(solution)/shard_map/pack/pallas_call | solution.py:94
  4.3 7.7 %all-to-all-start = ((bf16[128,8,1024]{2,1,0:T(8,128)(2,1)}), bf16[128,8,1024]{2,1,0:T(8,128)(2,1)S(1)}, u32[]{:S(2)}, u32[]{:S(2)}) async-start(bf16[128,8,1024]{2,1,0:T(8,128)(2,1)} %pack.2), calls=%async_computation | async-start | bytes 4194304 | tf_op jit(solution)/shard_map/all_to_all | solution.py:411
  12.0 3.6 %pack.3 = bf16[128,8,1024]{2,1,0:T(8,128)(2,1)} custom-call(s32[64]{0:T(128)} %bitcast.17, s32[16]{0:T(128)} %counts.5, bf16[64,8,1024]{2,1,0:T(8,128)(2,1)} %bitcast.13), custom_call_target="tpu_custom_call" | custom-call | bytes 3145728 | tf_op jit(solution)/shard_map/pack/pallas_call | solution.py:94
  15.7 0.0 copy-start.2
  15.7 0.0 copy-start.3
  15.7 0.0 copy-start.4
  15.7 0.0 copy-start
  15.7 0.0 copy-start.7
  15.7 37.3 %all-to-all-done = bf16[128,8,1024]{2,1,0:T(8,128)(2,1)S(1)} async-done(((bf16[128,8,1024]{2,1,0:T(8,128)(2,1)}), bf16[128,8,1024]{2,1,0:T(8,128)(2,1)S(1)}, u32[]{:S(2)}, u32[]{:S(2)}) %all-to-all-start) | async-done | bytes 2097184 | tf_op jit(solution)/shard_map/all_to_all | solution.py:411
  53.0 0.0 copy-start.8
  53.0 1.3 copy-done.8
  54.3 11.2 %all-to-all-start.1 = ((bf16[128,8,1024]{2,1,0:T(8,128)(2,1)}), bf16[128,8,1024]{2,1,0:T(8,128)(2,1)S(1)}, u32[]{:S(2)}, u32[]{:S(2)}) async-start(bf16[128,8,1024]{2,1,0:T(8,128)(2,1)} %pack.3), calls=%async_computation.1 | async-start | bytes 4194304 | tf_op jit(solution)/shard_map/all_to_all | solution.py:411
  66.2 0.0 copy-done.2
  66.2 0.0 copy-done.3
  66.2 0.0 copy-done.4
  66.2 0.1 message.1
  66.3 0.0 copy-start.5
  66.3 0.0 copy-start.6
  66.3 3.8 %collective-permute-start.2 = (bf16[25,8,128]{2,1,0:T(8,128)(2,1)S(1)}, bf16[25,8,128]{2,1,0:T(8,128)(2,1)S(1)}, u32[]{:S(2)}, u32[]{:S(2)}) collective-permute-start(bf16[25,8,128]{2,1,0:T(8,128)(2,1)S(1)} %message.1), channel_id=1, source_target_pairs={{0,12},{1,13},{2,14},{3,15},{4,8},{5,9},{6,10},{7,11},{8,4},{9,5},... | collective-permute-start | bytes 153608 | tf_op jit(solution)/shard_map/ppermute | solution.py:407
  70.1 0.0 collective-permute-start.1
  70.1 0.7 collective-permute-start
  70.8 35.3 %collective-permute-done.2 = bf16[25,8,128]{2,1,0:T(8,128)(2,1)S(1)} collective-permute-done((bf16[25,8,128]{2,1,0:T(8,128)(2,1)S(1)}, bf16[25,8,128]{2,1,0:T(8,128)(2,1)S(1)}, u32[]{:S(2)}, u32[]{:S(2)}) %collective-permute-start.2) | collective-permute-done | bytes 51232 | tf_op jit(solution)/shard_map/ppermute | solution.py:407
  106.0 12.9 %collective-permute-done.1 = bf16[25,8,128]{2,1,0:T(8,128)(2,1)S(1)} collective-permute-done((bf16[25,8,128]{2,1,0:T(8,128)(2,1)S(1)}, bf16[25,8,128]{2,1,0:T(8,128)(2,1)S(1)}, u32[]{:S(2)}, u32[]{:S(2)}) %collective-permute-start.1) | collective-permute-done | bytes 51232 | tf_op jit(solution)/shard_map/ppermute | solution.py:407
  118.9 0.0 collective-permute-done
  119.0 1.6 collective-permute-start.4
  120.6 0.0 collective-permute-start.3
  120.6 4.7 %collective-permute-done.4.refs_2_ = bf16[100,8,128]{2,1,0:T(8,128)(2,1)S(1)} collective-permute-done((bf16[100,8,128]{2,1,0:T(8,128)(2,1)S(1)}, bf16[100,8,128]{2,1,0:T(8,128)(2,1)S(1)}, u32[]{:S(2)}, u32[]{:S(2)}) %collective-permute-start.4) | collective-permute-done | bytes 204832 | tf_op jit(solution)/shard_map/ppermute | solution.py:407
  125.3 0.0 collective-permute-start.5
  125.3 0.0 collective-permute-done.3.refs_1_
  125.3 1.4 collective-permute-done.5.refs_3_
  126.7 0.0 copy-done
  126.7 0.0 copy-done.7
  126.7 0.0 copy-start.1
  126.7 1.2 copy-done.1
  128.0 7.5 %attend.1 = (bf16[8,27,8,128]{3,2,1,0:T(8,128)(2,1)S(1)}, bf16[8,27,8,128]{3,2,1,0:T(8,128)(2,1)S(1)}, s32[16,128]{1,0:T(8,128)S(1)}) custom-call(s32[16]{0:T(128)S(1)} %copy-done.7, bf16[100,8,128]{2,1,0:T(8,128)(2,1)S(1)} %pad_maximum_fusion.refs_0_, bf16[100,8,128]{2,1,0:T(8,128)(2,1)S(1)} %collective-permute-done.3.refs_1_, ...), custom_call_target="tpu_custom_call" | custom-call | flops 805306368 | bytes 3670016 | tf_op jit(solution)/shard_map/attend/pallas_call | solution.py:209
  135.5 0.2 collective-permute-start.6
  135.7 1.7 %collective-permute-done.6.got = bf16[8,27,8,128]{3,2,1,0:T(8,128)(2,1)S(1)} collective-permute-done((bf16[8,27,8,128]{3,2,1,0:T(8,128)(2,1)S(1)}, bf16[8,27,8,128]{3,2,1,0:T(8,128)(2,1)S(1)}, u32[]{:S(2)}, u32[]{:S(2)}) %collective-permute-start.6) | collective-permute-done | bytes 442400 | tf_op jit(solution)/shard_map/ppermute | solution.py:407
  137.3 2.6 %fold.1 = (bf16[27,8,128]{2,1,0:T(8,128)(2,1)S(1)}, bf16[27,8,128]{2,1,0:T(8,128)(2,1)S(1)}, bf16[27,8,128]{2,1,0:T(8,128)(2,1)S(1)}, bf16[27,8,128]{2,1,0:T(8,1...) custom-call(bf16[8,27,8,128]{3,2,1,0:T(8,128)(2,1)S(1)} %get-tuple-e, ...), custom_call_target="tpu_custom_call" | custom-call | flops 884736 | bytes 1327104 | tf_op jit(solution)/shard_map/fold/pallas_call | solution.py:253
  139.9 1.6 collective-permute-start.7
  141.5 0.0 collective-permute-start.8
  141.5 2.0 %collective-permute-start.9 = (bf16[27,8,128]{2,1,0:T(8,128)(2,1)S(1)}, bf16[27,8,128]{2,1,0:T(8,128)(2,1)S(1)}, u32[]{:S(2)}, u32[]{:S(2)}) collective-permute-start(bf16[27,8,128]{2,1,0:T(8,128)(2,1)S(1)} %get-tuple-element.23), channel_id=1, source_target_pairs={{0,6},{1,7},{2,4},{3,5},{4,2},{5,3},{6,0},{7,1},{8,14},{9,15},{10,... | collective-permute-start | bytes 165896 | tf_op jit(solution)/shard_map/ppermute | solution.py:407
  143.4 0.0 collective-permute-start.10
  143.4 3.9 %collective-permute-start.11 = (bf16[27,8,128]{2,1,0:T(8,128)(2,1)S(1)}, bf16[27,8,128]{2,1,0:T(8,128)(2,1)S(1)}, u32[]{:S(2)}, u32[]{:S(2)}) collective-permute-start(bf16[27,8,128]{2,1,0:T(8,128)(2,1)S(1)} %get-tuple-element.25), channel_id=1, source_target_pairs={{0,10},{1,11},{2,8},{3,9},{4,14},{5,15},{6,12},{7,13},{8,2},{9,3},... | collective-permute-start | bytes 165896 | tf_op jit(solution)/shard_map/ppermute | solution.py:407
  147.3 0.0 collective-permute-done.7.refs_1_
  147.3 1.4 collective-permute-start.12
  148.7 0.0 collective-permute-done.8.refs_2_
  148.7 2.4 %collective-permute-start.13 = (bf16[27,8,128]{2,1,0:T(8,128)(2,1)S(1)}, bf16[27,8,128]{2,1,0:T(8,128)(2,1)S(1)}, u32[]{:S(2)}, u32[]{:S(2)}) collective-permute-start(bf16[27,8,128]{2,1,0:T(8,128)(2,1)S(1)} %get-tuple-element.27), channel_id=1, source_target_pairs={{0,14},{1,15},{2,12},{3,13},{4,10},{5,11},{6,8},{7,9},{8,6},{9,7},... | collective-permute-start | bytes 165896 | tf_op jit(solution)/shard_map/ppermute | solution.py:407
  151.1 0.6 reshape.57
  151.7 0.0 collective-permute-done.9.refs_3_
  151.7 0.0 collective-permute-done.10.refs_4_
  151.7 2.6 %collective-permute-done.11.refs_5_ = bf16[27,8,128]{2,1,0:T(8,128)(2,1)S(1)} collective-permute-done((bf16[27,8,128]{2,1,0:T(8,128)(2,1)S(1)}, bf16[27,8,128]{2,1,0:T(8,128)(2,1)S(1)}, u32[]{:S(2)}, u32[]{:S(2)}) %collective-permute-start.11) | collective-permute-done | bytes 55328 | tf_op jit(solution)/shard_map/ppermute | solution.py:407
  154.3 0.0 collective-permute-done.12.refs_6_
  154.3 1.3 collective-permute-done.13.refs_7_
  155.6 0.0 copy-done.5
  155.6 0.0 copy-done.6
  155.6 1.4 merge.1
  157.1 2.9 %join.1 = bf16[16,8,8,1024]{3,2,1,0:T(8,128)(2,1)} custom-call(bf16[16,8,8,1024]{3,2,1,0:T(8,128)(2,1)} %bitcast.21), custom_call_target="tpu_custom_call" | custom-call | bytes 4194304 | tf_op jit(solution)/shard_map/join/pallas_call | solution.py:315
  160.0 0.0 all-to-all-done.1.source
  160.0 1.3 settle.1
  (1 shorter events, 0.0 us)
Async XLA Ops:
  4.3 48.7 %all-to-all-start = ((bf16[128,8,1024]{2,1,0:T(8,128)(2,1)}), bf16[128,8,1024]{2,1,0:T(8,128)(2,1)S(1)}, u32[]{:S(2)}, u32[]{:S(2)}) async-start(bf16[128,8,1024]{2,1,0:T(8,128)(2,1)} %pack.2), calls=%async_computation | async-start | bytes 4194304 | tf_op jit(solution)/shard_map/all_to_all | solution.py:411
  15.7 50.5 %copy-start.2 = (bf16[1,8192]{1,0:T(2,128)(2,1)S(1)}, bf16[1,8192]{1,0:T(2,128)(2,1)}, u32[]{:S(2)}) copy-start(bf16[1,8192]{1,0:T(2,128)(2,1)} %prefill_q.1) | copy-start | bytes 49156
  15.7 50.5 %copy-start.3 = (bf16[1,2,8192]{2,1,0:T(2,128)(2,1)S(1)}, bf16[1,2,8192]{2,1,0:T(2,128)(2,1)}, u32[]{:S(2)}) copy-start(bf16[1,2,8192]{2,1,0:T(2,128)(2,1)} %param.14) | copy-start | bytes 98308
  15.7 50.5 %copy-start.4 = (s32[64,1]{0,1:T(1,128)S(1)}, s32[64,1]{0,1:T(1,128)}, u32[]{:S(2)}) copy-start(s32[64,1]{0,1:T(1,128)} %param.13) | copy-start | bytes 772
  15.7 111.1 %copy-start = (bf16[512,1024]{1,0:T(8,128)(2,1)S(1)}, bf16[512,1024]{1,0:T(8,128)(2,1)}, u32[]{:S(2)}) copy-start(bf16[512,1024]{1,0:T(8,128)(2,1)} %refs_4_.1) | copy-start | bytes 3145732
  15.7 111.1 %copy-start.7 = (s32[16]{0:T(128)S(1)}, s32[16]{0:T(128)}, u32[]{:S(2)}) copy-start(s32[16]{0:T(128)} %counts.5) | copy-start | bytes 196
  53.0 1.3 copy-start.8
  54.3 105.7 %all-to-all-start.1 = ((bf16[128,8,1024]{2,1,0:T(8,128)(2,1)}), bf16[128,8,1024]{2,1,0:T(8,128)(2,1)S(1)}, u32[]{:S(2)}, u32[]{:S(2)}) async-start(bf16[128,8,1024]{2,1,0:T(8,128)(2,1)} %pack.3), calls=%async_computation.1 | async-start | bytes 4194304 | tf_op jit(solution)/shard_map/all_to_all | solution.py:411
  66.3 89.4 %copy-start.5 = (bf16[1,2,1024]{2,1,0:T(2,128)(2,1)S(1)}, bf16[1,2,1024]{2,1,0:T(2,128)(2,1)}, u32[]{:S(2)}) copy-start(bf16[1,2,1024]{2,1,0:T(2,128)(2,1)} %param.15) | copy-start | bytes 12292
  66.3 89.4 %copy-start.6 = (bf16[1,2,1024]{2,1,0:T(2,128)(2,1)S(1)}, bf16[1,2,1024]{2,1,0:T(2,128)(2,1)}, u32[]{:S(2)}) copy-start(bf16[1,2,1024]{2,1,0:T(2,128)(2,1)} %param.16) | copy-start | bytes 12292
  66.3 39.7 %collective-permute-start.2 = (bf16[25,8,128]{2,1,0:T(8,128)(2,1)S(1)}, bf16[25,8,128]{2,1,0:T(8,128)(2,1)S(1)}, u32[]{:S(2)}, u32[]{:S(2)}) collective-permute-start(bf16[25,8,128]{2,1,0:T(8,128)(2,1)S(1)} %message.1), channel_id=1, source_target_pairs={{0,12},{1,13},{2,14},{3,15},{4,8},{5,9},{6,10},{7,11},{8,4},{9,5},... | collective-permute-start | bytes 153608 | tf_op jit(solution)/shard_map/ppermute | solution.py:407
  70.1 48.8 %collective-permute-start.1 = (bf16[25,8,128]{2,1,0:T(8,128)(2,1)S(1)}, bf16[25,8,128]{2,1,0:T(8,128)(2,1)S(1)}, u32[]{:S(2)}, u32[]{:S(2)}) collective-permute-start(bf16[25,8,128]{2,1,0:T(8,128)(2,1)S(1)} %message.1), channel_id=1, source_target_pairs={{0,8},{1,9},{2,10},{3,11},{4,12},{5,13},{6,14},{7,15},{8,0},{9,1},... | collective-permute-start | bytes 153608 | tf_op jit(solution)/shard_map/ppermute | solution.py:407
  70.1 48.8 %collective-permute-start = (bf16[25,8,128]{2,1,0:T(8,128)(2,1)S(1)}, bf16[25,8,128]{2,1,0:T(8,128)(2,1)S(1)}, u32[]{:S(2)}, u32[]{:S(2)}) collective-permute-start(bf16[25,8,128]{2,1,0:T(8,128)(2,1)S(1)} %message.1), channel_id=1, source_target_pairs={{0,4},{1,5},{2,6},{3,7},{4,0},{5,1},{6,2},{7,3},{8,12},{9,13},{10,... | collective-permute-start | bytes 153608 | tf_op jit(solution)/shard_map/ppermute | solution.py:407
  119.0 6.3 %collective-permute-start.4 = (bf16[100,8,128]{2,1,0:T(8,128)(2,1)S(1)}, bf16[100,8,128]{2,1,0:T(8,128)(2,1)S(1)}, u32[]{:S(2)}, u32[]{:S(2)}) collective-permute-start(bf16[100,8,128]{2,1,0:T(8,128)(2,1)S(1)} %pad_maximum_fusion.refs_0_), channel_id=1, source_target_pairs={{0,2},{1,3},{2,0},{3,1},{4,6},{5,7},{6,4},{7,5},{8,10},{9,11},{10,... | collective-permute-start | bytes 614408 | tf_op jit(solution)/shard_map/ppermute | solution.py:407
  120.6 4.7 %collective-permute-start.3 = (bf16[100,8,128]{2,1,0:T(8,128)(2,1)S(1)}, bf16[100,8,128]{2,1,0:T(8,128)(2,1)S(1)}, u32[]{:S(2)}, u32[]{:S(2)}) collective-permute-start(bf16[100,8,128]{2,1,0:T(8,128)(2,1)S(1)} %pad_maximum_fusion.refs_0_), channel_id=1, source_target_pairs={{0,1},{1,0},{2,3},{3,2},{4,5},{5,4},{6,7},{7,6},{8,9},{9,8},{10,11... | collective-permute-start | bytes 614408 | tf_op jit(solution)/shard_map/ppermute | solution.py:407
  125.3 1.5 collective-permute-start.5
  126.7 1.2 copy-start.1
  135.5 1.9 %collective-permute-start.6 = (bf16[8,27,8,128]{3,2,1,0:T(8,128)(2,1)S(1)}, bf16[8,27,8,128]{3,2,1,0:T(8,128)(2,1)S(1)}, u32[]{:S(2)}, u32[]{:S(2)}) collective-permute-start(bf16[8,27,8,128]{3,2,1,0:T(8,128)(2,1)S(1)} %get-tuple-element.19), channel_id=1, source_target_pairs={{0,1},{1,0},{2,3},{3,2},{4,5},{5,4},{6,7},{7,6},{8,9},{9,8},{10,11... | collective-permute-start | bytes 1327112 | tf_op jit(solution)/shard_map/ppermute | solution.py:407
  139.9 7.4 %collective-permute-start.7 = (bf16[27,8,128]{2,1,0:T(8,128)(2,1)S(1)}, bf16[27,8,128]{2,1,0:T(8,128)(2,1)S(1)}, u32[]{:S(2)}, u32[]{:S(2)}) collective-permute-start(bf16[27,8,128]{2,1,0:T(8,128)(2,1)S(1)} %get-tuple-element.21), channel_id=1, source_target_pairs={{0,2},{1,3},{2,0},{3,1},{4,6},{5,7},{6,4},{7,5},{8,10},{9,11},{10,... | collective-permute-start | bytes 165896 | tf_op jit(solution)/shard_map/ppermute | solution.py:407
  141.5 7.2 %collective-permute-start.8 = (bf16[27,8,128]{2,1,0:T(8,128)(2,1)S(1)}, bf16[27,8,128]{2,1,0:T(8,128)(2,1)S(1)}, u32[]{:S(2)}, u32[]{:S(2)}) collective-permute-start(bf16[27,8,128]{2,1,0:T(8,128)(2,1)S(1)} %get-tuple-element.22), channel_id=1, source_target_pairs={{0,4},{1,5},{2,6},{3,7},{4,0},{5,1},{6,2},{7,3},{8,12},{9,13},{10,... | collective-permute-start | bytes 165896 | tf_op jit(solution)/shard_map/ppermute | solution.py:407
  141.5 10.2 %collective-permute-start.9 = (bf16[27,8,128]{2,1,0:T(8,128)(2,1)S(1)}, bf16[27,8,128]{2,1,0:T(8,128)(2,1)S(1)}, u32[]{:S(2)}, u32[]{:S(2)}) collective-permute-start(bf16[27,8,128]{2,1,0:T(8,128)(2,1)S(1)} %get-tuple-element.23), channel_id=1, source_target_pairs={{0,6},{1,7},{2,4},{3,5},{4,2},{5,3},{6,0},{7,1},{8,14},{9,15},{10,... | collective-permute-start | bytes 165896 | tf_op jit(solution)/shard_map/ppermute | solution.py:407
  143.4 8.3 %collective-permute-start.10 = (bf16[27,8,128]{2,1,0:T(8,128)(2,1)S(1)}, bf16[27,8,128]{2,1,0:T(8,128)(2,1)S(1)}, u32[]{:S(2)}, u32[]{:S(2)}) collective-permute-start(bf16[27,8,128]{2,1,0:T(8,128)(2,1)S(1)} %get-tuple-element.24), channel_id=1, source_target_pairs={{0,8},{1,9},{2,10},{3,11},{4,12},{5,13},{6,14},{7,15},{8,0},{9,1},... | collective-permute-start | bytes 165896 | tf_op jit(solution)/shard_map/ppermute | solution.py:407
  143.4 10.9 %collective-permute-start.11 = (bf16[27,8,128]{2,1,0:T(8,128)(2,1)S(1)}, bf16[27,8,128]{2,1,0:T(8,128)(2,1)S(1)}, u32[]{:S(2)}, u32[]{:S(2)}) collective-permute-start(bf16[27,8,128]{2,1,0:T(8,128)(2,1)S(1)} %get-tuple-element.25), channel_id=1, source_target_pairs={{0,10},{1,11},{2,8},{3,9},{4,14},{5,15},{6,12},{7,13},{8,2},{9,3},... | collective-permute-start | bytes 165896 | tf_op jit(solution)/shard_map/ppermute | solution.py:407
  147.3 7.0 %collective-permute-start.12 = (bf16[27,8,128]{2,1,0:T(8,128)(2,1)S(1)}, bf16[27,8,128]{2,1,0:T(8,128)(2,1)S(1)}, u32[]{:S(2)}, u32[]{:S(2)}) collective-permute-start(bf16[27,8,128]{2,1,0:T(8,128)(2,1)S(1)} %get-tuple-element.26), channel_id=1, source_target_pairs={{0,12},{1,13},{2,14},{3,15},{4,8},{5,9},{6,10},{7,11},{8,4},{9,5},... | collective-permute-start | bytes 165896 | tf_op jit(solution)/shard_map/ppermute | solution.py:407
  148.7 7.0 %collective-permute-start.13 = (bf16[27,8,128]{2,1,0:T(8,128)(2,1)S(1)}, bf16[27,8,128]{2,1,0:T(8,128)(2,1)S(1)}, u32[]{:S(2)}, u32[]{:S(2)}) collective-permute-start(bf16[27,8,128]{2,1,0:T(8,128)(2,1)S(1)} %get-tuple-element.27), channel_id=1, source_target_pairs={{0,14},{1,15},{2,12},{3,13},{4,10},{5,11},{6,8},{7,9},{8,6},{9,7},... | collective-permute-start | bytes 165896 | tf_op jit(solution)/shard_map/ppermute | solution.py:407

commit v5 on v2

--- a/solution.py
+++ b/solution.py
@@ -16,7 +16,7 @@
 MASKED = -1e30
 VMEM = pltpu.MemorySpace.VMEM
 SMEM = pltpu.MemorySpace.SMEM
-LIMIT = 48 * 1024 * 1024
+LIMIT = 32 * 1024 * 1024
 
 
 def whole(space):
@@ -35,10 +35,10 @@
     rows[base : base + 1, 0:slots] = owners[...].astype(jnp.float32)
     lane = lax.broadcasted_iota(jnp.int32, (1, 128), 1)
     digits = jnp.zeros((1, 128), jnp.int32)
-    for q in range(length.shape[0]):
-        value = length[q]
-        digits = jnp.where(lane == 2 * q, value // 256, digits)
-        digits = jnp.where(lane == 2 * q + 1, value % 256, digits)
+    for q in range(length.shape[1]):
+        value = length[:, q : q + 1]
+        digits = jnp.where(lane == 2 * q, value >> 8, digits)
+        digits = jnp.where(lane == 2 * q + 1, value & 255, digits)
     rows[base + 1 : base + 2, :] = digits.astype(jnp.float32)
     out[...] = rows[...].reshape(out.shape).astype(jnp.bfloat16)
 
@@ -50,65 +50,65 @@
     return pl.pallas_call(
         functools.partial(message_kernel, rows_p, rows_d),
         out_shape=jax.ShapeDtypeStruct((blocks, 8, 128), jnp.bfloat16),
-        in_specs=[whole(SMEM), whole(VMEM), whole(VMEM), whole(VMEM)],
+        in_specs=[whole(VMEM)] * 4,
         out_specs=whole(VMEM),
         scratch_shapes=[pltpu.VMEM((blocks * 8, 128), jnp.float32)],
         name="message",
-    )(context_len, prefill_q, decode_q.reshape(rows_d, HQ * HD), page_owner.reshape(1, -1))
-
-
-def pack_kernel(shards, capacity, owners, counts, pages, out, held, blank, taken, sem_in, sem_out):
+    )(context_len.reshape(1, -1), prefill_q, decode_q.reshape(rows_d, HQ * HD), page_owner.reshape(1, -1))
+
+
+def pack_kernel(shards, capacity, partners, owners, counts, keys, values, *refs):
+    outs, (taken, chosen) = refs[:-2], refs[-2:]
     me = lax.axis_index("seq")
-    fetch = pltpu.make_async_copy(pages, held, sem_in)
-    fetch.start()
-    blank[...] = jnp.zeros_like(blank)
 
     def reset(o, carry):
         taken[o] = 0
         return carry
 
-    lax.fori_loop(0, shards, reset, 0)
-    fetch.wait()
-
-    def place(j, carry):
+    lax.fori_loop(0, shards, reset, 0, unroll=8)
+
+    def note(j, carry):
         o = owners[j]
         k = taken[o]
         taken[o] = k + 1
-        pltpu.make_async_copy(held.at[j], out.at[o * capacity + k], sem_out).start()
+        chosen[o * capacity + k] = j
         return carry
 
-    lax.fori_loop(0, counts[me], place, 0)
-
-    def fill(o, carry):
-        def one(k, inner):
-            pltpu.make_async_copy(blank, out.at[o * capacity + k], sem_out).start()
-            return inner
-
-        return lax.fori_loop(taken[o], capacity, one, carry)
-
-    lax.fori_loop(0, shards, fill, 0)
-    pltpu.make_async_copy(out, out, sem_out).wait()
-
-
-def pack(owners, counts, pages, shards, capacity):
-    slots = pages.shape[0]
-    return pl.pallas_call(
-        functools.partial(pack_kernel, shards, capacity),
-        out_shape=jax.ShapeDtypeStruct((shards * capacity, PAGE, KVD), pages.dtype),
-        in_specs=[whole(SMEM), whole(SMEM), whole(pl.ANY)],
-        out_specs=whole(pl.ANY),
+    lax.fori_loop(0, counts[me], note, 0)
+    for partner, out in zip(partners, outs):
+        o = me ^ partner
+        count = taken[o]
+
+        def copy(k, carry, o=o, count=count, out=out):
+            full = k < count
+            j = jnp.where(full, chosen[o * capacity + k], 0)
+            for part, pages in enumerate((keys, values)):
+                page = pages[j]
+                out[part, k] = jnp.where(full, page, jnp.zeros_like(page))
+            return carry
+
+        lax.fori_loop(0, capacity, copy, 0, unroll=2)
+
+
+def pack(owners, counts, keys, values, shards, capacity, partners):
+    slots = keys.shape[0]
+    piece = jax.ShapeDtypeStruct((2, capacity, PAGE, KVD), keys.dtype)
+    return pl.pallas_call(
+        functools.partial(pack_kernel, shards, capacity, partners),
+        out_shape=(piece,) * len(partners),
+        in_specs=[whole(SMEM), whole(SMEM), whole(VMEM), whole(VMEM)],
+        out_specs=(whole(VMEM),) * len(partners),
         scratch_shapes=[
-            pltpu.VMEM((slots, PAGE, KVD), pages.dtype),
-            pltpu.VMEM((PAGE, KVD), pages.dtype),
             pltpu.SMEM((shards,), jnp.int32),
-            pltpu.SemaphoreType.DMA,
-            pltpu.SemaphoreType.DMA,
+            pltpu.SMEM((shards * capacity,), jnp.int32),
         ],
         cost_estimate=pl.CostEstimate(
-            flops=0, transcendentals=0, bytes_accessed=(slots + shards * capacity) * PAGE * KVD * 2
+            flops=0,
+            transcendentals=0,
+            bytes_accessed=(2 * slots + 4 * len(partners) * capacity) * PAGE * KVD * 2,
         ),
         name="pack",
-    )(owners, counts, pages)
+    )(owners, counts, keys, values)
 
 
 def attend_kernel(rows_p, rows_d, capacity, counts, *refs):
@@ -267,32 +267,49 @@
     )(keep, got)
 
 
-def settle_kernel(pieces, source, out, sems):
-    step = source.shape[0] // pieces
-    spans = [pl.ds(i * step, step) for i in range(pieces)]
-    puts = [
-        pltpu.make_async_copy(source.at[span], out.at[span], sems.at[i])
-        for i, span in enumerate(spans)
+def settle_kernel(partners, old, *refs):
+    refs = refs[old:]
+    pieces, refs = refs[: len(partners)], refs[len(partners) :]
+    store_k, store_v, held, sems_in, sems_out = refs
+    me = lax.axis_index("seq")
+    fetches = [
+        pltpu.make_async_copy(piece, held.at[i], sems_in.at[i]) for i, piece in enumerate(pieces)
     ]
-    for put in puts:
-        put.start()
+    for fetch in fetches:
+        fetch.start()
+    puts = []
+    for i, (partner, fetch) in enumerate(zip(partners, fetches)):
+        fetch.wait()
+        for part, store in enumerate((store_k, store_v)):
+            put = pltpu.make_async_copy(
+                held.at[i, part], store.at[me ^ partner], sems_out.at[2 * i + part]
+            )
+            put.start()
+            puts.append(put)
     for put in puts:
         put.wait()
 
 
-def settle(source):
-    pieces = 4
-    return pl.pallas_call(
-        functools.partial(settle_kernel, pieces),
-        out_shape=jax.ShapeDtypeStruct(source.shape, source.dtype),
-        in_specs=[whole(VMEM)],
-        out_specs=whole(pl.ANY),
-        scratch_shapes=[pltpu.SemaphoreType.DMA((pieces,))],
+def settle(shards, partners, pieces, stores=()):
+    number = len(partners)
+    shape = (shards,) + pieces[0].shape[1:]
+    store = jax.ShapeDtypeStruct(shape, pieces[0].dtype)
+    return pl.pallas_call(
+        functools.partial(settle_kernel, partners, len(stores)),
+        out_shape=(store, store),
+        in_specs=[whole(pl.ANY)] * (len(stores) + number),
+        out_specs=(whole(pl.ANY),) * 2,
+        input_output_aliases={i: i for i in range(len(stores))},
+        scratch_shapes=[
+            pltpu.VMEM((number,) + pieces[0].shape, pieces[0].dtype),
+            pltpu.SemaphoreType.DMA((number,)),
+            pltpu.SemaphoreType.DMA((2 * number,)),
+        ],
         cost_estimate=pl.CostEstimate(
-            flops=0, transcendentals=0, bytes_accessed=2 * source.size * 2
+            flops=0, transcendentals=0, bytes_accessed=4 * number * pieces[0].size
         ),
         name="settle",
-    )(source)
+    )(*stores, *pieces)
 
 
 def merge_kernel(rows_p, rows_d, message, new_k, new_v, *refs):
@@ -373,8 +390,15 @@
     return lax.ppermute(array, "seq", [(i, i ^ distance) for i in range(shards)])
 
 
-def exchange(array):
-    return lax.all_to_all(array, "seq", split_axis=0, concat_axis=0, tiled=True)
+def send_order(shards):
+    upper = list(range(shards // 2, shards))
+    lower = [k for k in range(1, shards // 2)]
+    quarter = len(upper) // 2
+    early = upper[:quarter]
+    side = [k for k in lower if k >= 4] + [k for k in lower if k < 4]
+    before, after = side[: quarter // 2], side[quarter // 2 :]
+    late = upper[quarter:]
+    return early, before, late, after
 
 
 def per_device(
@@ -389,17 +413,20 @@
     pages_k = cache_k.reshape(page_slots, PAGE, KVD)
     pages_v = cache_v.reshape(page_slots, PAGE, KVD)
     rows = rows_p + rows_d
+    early, before, late, after = send_order(shards)
+    pieces = {}
     message = make_message(prefill_q, decode_q, page_owner, context_len)
     far = [message]
     for k in range(4, shards, 4):
         far.append(swap(message, k))
-    packed_k = pack(owners, page_counts, pages_k, shards, capacity)
-    packed_v = pack(owners, page_counts, pages_v, shards, capacity)
+    for group in (early, [0] + before + late + after):
+        packed = pack(owners, page_counts, pages_k, pages_v, shards, capacity, group)
+        for k, piece in zip(group, packed):
+            pieces[k] = swap(piece, k) if k else piece
     own = jnp.concatenate(far, axis=0)
     across = swap(own, 2)
     beside = swap(own, 1)
     corner = swap(across, 1)
-    store_k = exchange(packed_k)
     keep, give, table = attend(
         rows_p,
         rows_d,
@@ -414,17 +441,16 @@
     parts = [folded[0]]
     for j in range(1, shards // 2):
         parts.append(swap(folded[j], 2 * j))
-    packed_v, store_k = lax.optimization_barrier((packed_v, store_k))
-    store_v = exchange(packed_v)
     prefill_out, decode_out = merge(rows_p, rows_d, parts, message, decode_k, decode_v)
-    store_k = settle(store_k)
-    store_v = settle(store_v)
+    stores = ()
+    for group in ([0] + early + before, late[:-2] + after, late[-2:]):
+        stores = settle(shards, group, [pieces[k] for k in group], stores)
     store_page = table[:, :capacity].reshape(-1)
     return (
         prefill_out,
         decode_out.reshape(decode_q.shape),
-        store_k.reshape(-1, KVD),
-        store_v.reshape(-1, KVD),
+        stores[0].reshape(-1, KVD),
+        stores[1].reshape(-1, KVD),
         store_page,
     )
 

time: 161 us -> 144 us (0.89)
  the two profiles are of different devices: /device:TPU:0 before, /device:TPU:13 now
where the time goes in v5:
time: 144 us; the launch traced here: 142 us
  waiting for transfers between devices  56.3 us (39%)
  starting transfers between devices  54.2 us (38%)
  Pallas kernels  28 us (19%)
  between operations  1.6 us (1%)
    ppermute x29, waiting for transfers between devices, swap(): lax.ppermute(array, 'seq', [(i, i ^ distance) for i in range(shards)])  56.3 us
    ppermute x29, starting transfers between devices, swap(): lax.ppermute(array, 'seq', [(i, i ^ distance) for i in range(shards)])  54.2 us
    pallas_call x2, Pallas kernels, pack(): pl.pallas_call(functools.partial(pack_kernel, shards, capacity, partners)...  8.48 us
    pallas_call x1, Pallas kernels, attend(): pl.pallas_call(functools.partial(attend_kernel, rows_p, rows_d, capacity)...  7.5 us
    pallas_call x3, Pallas kernels, settle(): pl.pallas_call(functools.partial(settle_kernel, partners, len(stores)), o...  6.51 us
  transfers between devices with their start and end apart: 29, of which 11 were waited for; matrix products, arithmetic and copies ran while one was open for 0% of the time, Pallas kernels for 18%

profile of v5, /device:TPU:13, one launch (start us, length us, event | category | flops | bytes accessed | tf_op | source)
XLA Modules:
  0.0 141.6 jit_solution(15282397577896039202)
XLA Ops:
  1.3 1.5 %message.1 = bf16[25,8,128]{2,1,0:T(8,128)(2,1)} custom-call(s32[1,1]{1,0:T(1,128)} %bitcast.12.length, bf16[1,8192]{1,0:T(2,128)(2,1)} %prefill_q.1, bf16[2,8192]{1,0:T(2,128)(2,1)} %bitcast.22, s32[1,64]{1,0:T(1,128)} %bitcast.23), custom_call_target="tpu_custom_call" | custom-call | tf_op jit(solution)/shard_map/message/pallas_call | solution.py:50
  2.8 0.2 collective-permute-start
  2.9 2.3 %collective-permute-start.1 = (bf16[25,8,128]{2,1,0:T(8,128)(2,1)}, bf16[25,8,128]{2,1,0:T(8,128)(2,1)S(1)}, u32[]{:S(2)}, u32[]{:S(2)}) collective-permute-start(bf16[25,8,128]{2,1,0:T(8,128)(2,1)} %message.1), channel_id=1, source_target_pairs={{0,8},{1,9},{2,10},{3,11},{4,12},{5,13},{6,14},{7,15},{8,0},{9,1},... | collective-permute-start | bytes 153608 | tf_op jit(solution)/shard_map/ppermute | solution.py:390
  5.2 0.2 collective-permute-start.2
  5.4 0.5 collective-permute-done
  5.9 1.7 %collective-permute-done.1 = bf16[25,8,128]{2,1,0:T(8,128)(2,1)S(1)} collective-permute-done((bf16[25,8,128]{2,1,0:T(8,128)(2,1)}, bf16[25,8,128]{2,1,0:T(8,128)(2,1)S(1)}, u32[]{:S(2)}, u32[]{:S(2)}) %collective-permute-start.1) | collective-permute-done | bytes 51232 | tf_op jit(solution)/shard_map/ppermute | solution.py:390
  7.6 1.8 %collective-permute-done.2 = bf16[25,8,128]{2,1,0:T(8,128)(2,1)S(1)} collective-permute-done((bf16[25,8,128]{2,1,0:T(8,128)(2,1)}, bf16[25,8,128]{2,1,0:T(8,128)(2,1)S(1)}, u32[]{:S(2)}, u32[]{:S(2)}) %collective-permute-start.2) | collective-permute-done | bytes 51232 | tf_op jit(solution)/shard_map/ppermute | solution.py:390
  9.4 0.8 pad_maximum_fusion.refs_0_
  10.2 0.3 collective-permute-start.4
  10.5 4.9 %pack.2 = (bf16[2,8,8,1024]{3,2,1,0:T(8,128)(2,1)}, bf16[2,8,8,1024]{3,2,1,0:T(8,128)(2,1)}, bf16[2,8,8,1024]{3,2,1,0:T(8,128)(2,1)}, bf16[2,8,8,1024]{3,2,1,0:T...) custom-call(s32[64]{0:T(128)} %bitcast.24, ...), custom_call_target="tpu_custom_call" | custom-call | bytes 8388608 | tf_op jit(solution)/shard_map/pack/pallas_call | solution.py:96
  15.4 2.2 %collective-permute-start.18 = (bf16[2,8,8,1024]{3,2,1,0:T(8,128)(2,1)}, bf16[2,8,8,1024]{3,2,1,0:T(8,128)(2,1)S(1)}, u32[]{:S(2)}, u32[]{:S(2)}) collective-permute-start(bf16[2,8,8,1024]{3,2,1,0:T(8,128)(2,1)} %get-tuple-element.57), channel_id=1, source_target_pairs={{0,4},{1,5},{2,6},{3,7},{4,0},{5,1},{6,2},{7,3},{8,12},{9,13},{10,... | collective-permute-start | bytes 786440 | tf_op jit(solution)/shard_map/ppermute | solution.py:390
  17.6 2.5 %collective-permute-start.3 = (bf16[100,8,128]{2,1,0:T(8,128)(2,1)S(1)}, bf16[100,8,128]{2,1,0:T(8,128)(2,1)S(1)}, u32[]{:S(2)}, u32[]{:S(2)}) collective-permute-start(bf16[100,8,128]{2,1,0:T(8,128)(2,1)S(1)} %pad_maximum_fusion.refs_0_), channel_id=1, source_target_pairs={{0,1},{1,0},{2,3},{3,2},{4,5},{5,4},{6,7},{7,6},{8,9},{9,8},{10,11... | collective-permute-start | bytes 614408 | tf_op jit(solution)/shard_map/ppermute | solution.py:390
  20.1 0.0 collective-permute-done.4.refs_2_
  20.1 0.0 collective-permute-start.5
  20.1 0.3 collective-permute-start.19
  20.4 3.6 %pack.3 = (bf16[2,8,8,1024]{3,2,1,0:T(8,128)(2,1)}, bf16[2,8,8,1024]{3,2,1,0:T(8,128)(2,1)}, bf16[2,8,8,1024]{3,2,1,0:T(8,128)(2,1)}, bf16[2,8,8,1024]{3,2,1,0:T(8,128)(2,1)}) custom-call(s32[64]{0:T(128)} %bitcast.25, s32[16]{0:T(128)} %counts.5, bf16[64,8,1024]{2,1,0:T(8,128)(2,1)} %bitcast.14, bf16[64,8,1024]{2,1,0:T(8,128)(2,1)} %bitcast.16), custom_call_target="tpu_custom_call" | custom-call | bytes 4194304 | tf_op jit(solution)/shard_map/pack/pallas_call | solution.py:96
  24.1 0.8 collective-permute-start.14
  25.0 0.0 collective-permute-done.3.refs_1_
  25.0 2.3 %collective-permute-start.15 = (bf16[2,8,8,1024]{3,2,1,0:T(8,128)(2,1)}, bf16[2,8,8,1024]{3,2,1,0:T(8,128)(2,1)S(1)}, u32[]{:S(2)}, u32[]{:S(2)}) collective-permute-start(bf16[2,8,8,1024]{3,2,1,0:T(8,128)(2,1)} %get-tuple-element.54), channel_id=1, source_target_pairs={{0,9},{1,8},{2,11},{3,10},{4,13},{5,12},{6,15},{7,14},{8,1},{9,0},... | collective-permute-start | bytes 786440 | tf_op jit(solution)/shard_map/ppermute | solution.py:390
  27.2 0.0 collective-permute-done.18.refs_5_
  27.2 0.5 collective-permute-start.16
  27.7 2.8 %collective-permute-start.17 = (bf16[2,8,8,1024]{3,2,1,0:T(8,128)(2,1)}, bf16[2,8,8,1024]{3,2,1,0:T(8,128)(2,1)S(1)}, u32[]{:S(2)}, u32[]{:S(2)}) collective-permute-start(bf16[2,8,8,1024]{3,2,1,0:T(8,128)(2,1)} %get-tuple-element.56), channel_id=1, source_target_pairs={{0,11},{1,10},{2,9},{3,8},{4,15},{5,14},{6,13},{7,12},{8,3},{9,2},... | collective-permute-start | bytes 786440 | tf_op jit(solution)/shard_map/ppermute | solution.py:390
  30.6 7.5 %attend.1 = (bf16[8,27,8,128]{3,2,1,0:T(8,128)(2,1)S(1)}, bf16[8,27,8,128]{3,2,1,0:T(8,128)(2,1)S(1)}, s32[16,128]{1,0:T(8,128)S(1)}) custom-call(s32[16]{0:T(128)S(1)} %copy-done.5, bf16[100,8,128]{2,1,0:T(8,128)(2,1)S(1)} %pad_maximum_fusion.refs_0_, bf16[100,8,128]{2,1,0:T(8,128)(2,1)S(1)} %collective-permute-done.3.refs_1_, ...), custom_call_target="tpu_custom_call" | custom-call | flops 805306368 | bytes 3670016 | tf_op jit(solution)/shard_map/attend/pallas_call | solution.py:213
  38.1 0.0 collective-permute-done.19.refs_6_
  38.1 0.4 collective-permute-start.6
  38.5 14.4 %collective-permute-done.14.refs_1_ = bf16[2,8,8,1024]{3,2,1,0:T(8,128)(2,1)S(1)} collective-permute-done((bf16[2,8,8,1024]{3,2,1,0:T(8,128)(2,1)}, bf16[2,8,8,1024]{3,2,1,0:T(8,128)(2,1)S(1)}, u32[]{:S(2)}, u32[]{:S(2)}) %collective-permute-start.14) | collective-permute-done | bytes 262176 | tf_op jit(solution)/shard_map/ppermute | solution.py:390
  53.0 2.8 %collective-permute-start.20 = (bf16[2,8,8,1024]{3,2,1,0:T(8,128)(2,1)S(1)}, bf16[2,8,8,1024]{3,2,1,0:T(8,128)(2,1)S(1)}, u32[]{:S(2)}, u32[]{:S(2)}) collective-permute-start(bf16[2,8,8,1024]{3,2,1,0:T(8,128)(2,1)S(1)} %copy-done.29), channel_id=1, source_target_pairs={{0,12},{1,13},{2,14},{3,15},{4,8},{5,9},{6,10},{7,11},{8,4},{9,5},... | collective-permute-start | bytes 786440 | tf_op jit(solution)/shard_map/ppermute | solution.py:390
  55.7 8.3 %collective-permute-done.15.refs_2_ = bf16[2,8,8,1024]{3,2,1,0:T(8,128)(2,1)S(1)} collective-permute-done((bf16[2,8,8,1024]{3,2,1,0:T(8,128)(2,1)}, bf16[2,8,8,1024]{3,2,1,0:T(8,128)(2,1)S(1)}, u32[]{:S(2)}, u32[]{:S(2)}) %collective-permute-start.15) | collective-permute-done | bytes 262176 | tf_op jit(solution)/shard_map/ppermute | solution.py:390
  64.0 3.4 %collective-permute-start.21 = (bf16[2,8,8,1024]{3,2,1,0:T(8,128)(2,1)S(1)}, bf16[2,8,8,1024]{3,2,1,0:T(8,128)(2,1)S(1)}, u32[]{:S(2)}, u32[]{:S(2)}) collective-permute-start(bf16[2,8,8,1024]{3,2,1,0:T(8,128)(2,1)S(1)} %copy-done.28), channel_id=1, source_target_pairs={{0,13},{1,12},{2,15},{3,14},{4,9},{5,8},{6,11},{7,10},{8,5},{9,4},... | collective-permute-start | bytes 786440 | tf_op jit(solution)/shard_map/ppermute | solution.py:390
  67.5 7.8 %collective-permute-done.16.refs_3_ = bf16[2,8,8,1024]{3,2,1,0:T(8,128)(2,1)S(1)} collective-permute-done((bf16[2,8,8,1024]{3,2,1,0:T(8,128)(2,1)}, bf16[2,8,8,1024]{3,2,1,0:T(8,128)(2,1)S(1)}, u32[]{:S(2)}, u32[]{:S(2)}) %collective-permute-start.16) | collective-permute-done | bytes 262176 | tf_op jit(solution)/shard_map/ppermute | solution.py:390
  75.3 5.6 %collective-permute-start.22 = (bf16[2,8,8,1024]{3,2,1,0:T(8,128)(2,1)S(1)}, bf16[2,8,8,1024]{3,2,1,0:T(8,128)(2,1)S(1)}, u32[]{:S(2)}, u32[]{:S(2)}) collective-permute-start(bf16[2,8,8,1024]{3,2,1,0:T(8,128)(2,1)S(1)} %copy-done.27), channel_id=1, source_target_pairs={{0,6},{1,7},{2,4},{3,5},{4,2},{5,3},{6,0},{7,1},{8,14},{9,15},{10,... | collective-permute-start | bytes 786440 | tf_op jit(solution)/shard_map/ppermute | solution.py:390
  80.9 0.2 collective-permute-done.17.refs_4_
  81.1 5.8 %collective-permute-start.23 = (bf16[2,8,8,1024]{3,2,1,0:T(8,128)(2,1)S(1)}, bf16[2,8,8,1024]{3,2,1,0:T(8,128)(2,1)S(1)}, u32[]{:S(2)}, u32[]{:S(2)}) collective-permute-start(bf16[2,8,8,1024]{3,2,1,0:T(8,128)(2,1)S(1)} %copy-done.26), channel_id=1, source_target_pairs={{0,7},{1,6},{2,5},{3,4},{4,3},{5,2},{6,1},{7,0},{8,15},{9,14},{10,... | collective-permute-start | bytes 786440 | tf_op jit(solution)/shard_map/ppermute | solution.py:390
  86.9 3.2 %collective-permute-done.20.refs_2_ = bf16[2,8,8,1024]{3,2,1,0:T(8,128)(2,1)S(1)} collective-permute-done((bf16[2,8,8,1024]{3,2,1,0:T(8,128)(2,1)S(1)}, bf16[2,8,8,1024]{3,2,1,0:T(8,128)(2,1)S(1)}, u32[]{:S(2)}, u32[]{:S(2)}) %collective-permute-start.20) | collective-permute-done | bytes 262176 | tf_op jit(solution)/shard_map/ppermute | solution.py:390
  90.1 0.7 collective-permute-start.24
  90.7 4.9 %collective-permute-done.21.refs_3_ = bf16[2,8,8,1024]{3,2,1,0:T(8,128)(2,1)S(1)} collective-permute-done((bf16[2,8,8,1024]{3,2,1,0:T(8,128)(2,1)S(1)}, bf16[2,8,8,1024]{3,2,1,0:T(8,128)(2,1)S(1)}, u32[]{:S(2)}, u32[]{:S(2)}) %collective-permute-start.21) | collective-permute-done | bytes 262176 | tf_op jit(solution)/shard_map/ppermute | solution.py:390
  95.7 1.2 collective-permute-start.25
  96.9 0.9 collective-permute-start.26
  97.8 0.0 collective-permute-done.23.refs_5_
  97.8 0.3 collective-permute-start.27
  98.1 0.0 collective-permute-done.6.got
  98.2 2.1 %collective-permute-start.28 = (bf16[2,8,8,1024]{3,2,1,0:T(8,128)(2,1)S(1)}, bf16[2,8,8,1024]{3,2,1,0:T(8,128)(2,1)S(1)}, u32[]{:S(2)}, u32[]{:S(2)}) collective-permute-start(bf16[2,8,8,1024]{3,2,1,0:T(8,128)(2,1)S(1)} %copy-done.21), channel_id=1, source_target_pairs={{0,15},{1,14},{2,13},{3,12},{4,11},{5,10},{6,9},{7,8},{8,7},{9,6},... | collective-permute-start | bytes 786440 | tf_op jit(solution)/shard_map/ppermute | solution.py:390
  100.3 2.5 %fold.1 = (bf16[27,8,128]{2,1,0:T(8,128)(2,1)S(1)}, bf16[27,8,128]{2,1,0:T(8,128)(2,1)S(1)}, bf16[27,8,128]{2,1,0:T(8,128)(2,1)S(1)}, bf16[27,8,128]{2,1,0:T(8,1...) custom-call(bf16[8,27,8,128]{3,2,1,0:T(8,128)(2,1)S(1)} %get-tuple-e, ...), custom_call_target="tpu_custom_call" | custom-call | flops 884736 | bytes 1327104 | tf_op jit(solution)/shard_map/fold/pallas_call | solution.py:257
  102.8 1.1 collective-permute-start.10
  103.9 0.0 collective-permute-done.25.refs_7_
  103.9 9.4 %collective-permute-start.11 = (bf16[27,8,128]{2,1,0:T(8,128)(2,1)S(1)}, bf16[27,8,128]{2,1,0:T(8,128)(2,1)S(1)}, u32[]{:S(2)}, u32[]{:S(2)}) collective-permute-start(bf16[27,8,128]{2,1,0:T(8,128)(2,1)S(1)} %get-tuple-element.47), channel_id=1, source_target_pairs={{0,10},{1,11},{2,8},{3,9},{4,14},{5,15},{6,12},{7,13},{8,2},{9,3},... | collective-permute-start | bytes 165896 | tf_op jit(solution)/shard_map/ppermute | solution.py:390
  113.4 0.0 collective-permute-done.26.refs_8_
  113.4 1.7 %collective-permute-start.12 = (bf16[27,8,128]{2,1,0:T(8,128)(2,1)S(1)}, bf16[27,8,128]{2,1,0:T(8,128)(2,1)S(1)}, u32[]{:S(2)}, u32[]{:S(2)}) collective-permute-start(bf16[27,8,128]{2,1,0:T(8,128)(2,1)S(1)} %get-tuple-element.48), channel_id=1, source_target_pairs={{0,12},{1,13},{2,14},{3,15},{4,8},{5,9},{6,10},{7,11},{8,4},{9,5},... | collective-permute-start | bytes 165896 | tf_op jit(solution)/shard_map/ppermute | solution.py:390
  115.1 5.3 %collective-permute-done.27.refs_2_ = bf16[2,8,8,1024]{3,2,1,0:T(8,128)(2,1)S(1)} collective-permute-done((bf16[2,8,8,1024]{3,2,1,0:T(8,128)(2,1)S(1)}, bf16[2,8,8,1024]{3,2,1,0:T(8,128)(2,1)S(1)}, u32[]{:S(2)}, u32[]{:S(2)}) %collective-permute-start.27) | collective-permute-done | bytes 262176 | tf_op jit(solution)/shard_map/ppermute | solution.py:390
  120.4 0.3 collective-permute-start.13
  120.7 8.1 %collective-permute-done.28.refs_3_ = bf16[2,8,8,1024]{3,2,1,0:T(8,128)(2,1)S(1)} collective-permute-done((bf16[2,8,8,1024]{3,2,1,0:T(8,128)(2,1)S(1)}, bf16[2,8,8,1024]{3,2,1,0:T(8,128)(2,1)S(1)}, u32[]{:S(2)}, u32[]{:S(2)}) %collective-permute-start.28) | collective-permute-done | bytes 262176 | tf_op jit(solution)/shard_map/ppermute | solution.py:390
  128.7 0.8 collective-permute-start.7
  129.5 1.2 collective-permute-start.8
  130.7 0.0 collective-permute-done.11.refs_5_
  130.7 2.1 %collective-permute-start.9 = (bf16[27,8,128]{2,1,0:T(8,128)(2,1)S(1)}, bf16[27,8,128]{2,1,0:T(8,128)(2,1)S(1)}, u32[]{:S(2)}, u32[]{:S(2)}) collective-permute-start(bf16[27,8,128]{2,1,0:T(8,128)(2,1)S(1)} %get-tuple-element.45), channel_id=1, source_target_pairs={{0,6},{1,7},{2,4},{3,5},{4,2},{5,3},{6,0},{7,1},{8,14},{9,15},{10,... | collective-permute-start | bytes 165896 | tf_op jit(solution)/shard_map/ppermute | solution.py:390
  132.8 2.3 %settle.3 = (bf16[16,8,8,1024]{3,2,1,0:T(8,128)(2,1)}, bf16[16,8,8,1024]{3,2,1,0:T(8,128)(2,1)}) custom-call(bf16[2,8,8,1024]{3,2,1,0:T(8,128)(2,1)} %get-tuple-element.52.refs_0_, bf16[2,8,8,1024]{3,2,1,0:T(8,128)(2,1)} %copy-done.8, bf16[2,8,8,1024]{3,2,1,0:T(8,128)(2,1)} %copy-done.9, bf16[2,8,8,1024]{3,2,1,0:T(8,128)(2,1)} %copy-done.10, ...), custom_call_target="tpu_custom_call" | custom-call | bytes 3670016 | tf_op jit(solution)/shard_map/settle/pallas_call | solution.py:297
  135.3 2.4 %settle.4 = (bf16[16,8,8,1024]{3,2,1,0:T(8,128)(2,1)}, bf16[16,8,8,1024]{3,2,1,0:T(8,128)(2,1)}) custom-call(bf16[16,8,8,1024]{3,2,1,0:T(8,128)(2,1)} %get-tuple-element.59.refs_0_, bf16[16,8,8,1024]{3,2,1,0:T(8,128)(2,1)} %get-tuple-element.60.refs_1_, bf16[2,8,8,1024]{3,2,1,0:T(8,128)(2,1)} %copy-done.12, ...), custom_call_target="tpu_custom_call", output_to_operand_aliasing={{0}: (0, {}), {1}: (1, {})} | custom-call | bytes 3670016 | tf_op jit(solution)/shard_map/settle/pallas_call | solution.py:297
  137.6 0.0 copy-start.3
  137.6 0.0 copy-start.4
  137.7 1.8 %settle.5 = (bf16[16,8,8,1024]{3,2,1,0:T(8,128)(2,1)}, bf16[16,8,8,1024]{3,2,1,0:T(8,128)(2,1)}) custom-call(bf16[16,8,8,1024]{3,2,1,0:T(8,128)(2,1)} %get-tuple-element.68.refs_0_, bf16[16,8,8,1024]{3,2,1,0:T(8,128)(2,1)} %get-tuple-element.69.refs_1_, bf16[2,8,8,1024]{3,2,1,0:T(8,128)(2,1)} %copy-done.19, ...), custom_call_target="tpu_custom_call", output_to_operand_aliasing={{0}: (0, {}), {1}: (1, {})} | custom-call | bytes 1048576 | tf_op jit(solution)/shard_map/settle/pallas_call | solution.py:297
  139.5 0.6 reshape.57
  140.1 0.0 collective-permute-done.8.refs_2_
  140.1 0.0 collective-permute-done.9.refs_3_
  140.1 1.4 %merge.1 = (bf16[1,8192]{1,0:T(2,128)(2,1)}, bf16[2,8192]{1,0:T(2,128)(2,1)}) custom-call(bf16[25,8,128]{2,1,0:T(8,128)(2,1)S(1)} %copy-done.2, bf16[2,1024]{1,0:T(2,128)(2,1)S(1)} %bitcast.18, bf16[2,1024]{1,0:T(2,128)(2,1)S(1)} %bitcast.19, bf16[27,8,128]{2,1,0:T(8,128)(2,1)S(1)} %get-tuple-element.42.refs_0_, ...), custom_call_target="tpu_custom_call" | custom-call | flops 884736 | bytes 442368 | tf_op jit(solution)/shard_map/merge/pallas_call | solution.py:369
  (65 shorter events, 0.1 us)
Async XLA Ops:
  2.8 3.2 %collective-permute-start = (bf16[25,8,128]{2,1,0:T(8,128)(2,1)}, bf16[25,8,128]{2,1,0:T(8,128)(2,1)S(1)}, u32[]{:S(2)}, u32[]{:S(2)}) collective-permute-start(bf16[25,8,128]{2,1,0:T(8,128)(2,1)} %message.1), channel_id=1, source_target_pairs={{0,4},{1,5},{2,6},{3,7},{4,0},{5,1},{6,2},{7,3},{8,12},{9,13},{10,... | collective-permute-start | bytes 153608 | tf_op jit(solution)/shard_map/ppermute | solution.py:390
  2.9 4.7 %collective-permute-start.1 = (bf16[25,8,128]{2,1,0:T(8,128)(2,1)}, bf16[25,8,128]{2,1,0:T(8,128)(2,1)S(1)}, u32[]{:S(2)}, u32[]{:S(2)}) collective-permute-start(bf16[25,8,128]{2,1,0:T(8,128)(2,1)} %message.1), channel_id=1, source_target_pairs={{0,8},{1,9},{2,10},{3,11},{4,12},{5,13},{6,14},{7,15},{8,0},{9,1},... | collective-permute-start | bytes 153608 | tf_op jit(solution)/shard_map/ppermute | solution.py:390
  5.2 4.1 %collective-permute-start.2 = (bf16[25,8,128]{2,1,0:T(8,128)(2,1)}, bf16[25,8,128]{2,1,0:T(8,128)(2,1)S(1)}, u32[]{:S(2)}, u32[]{:S(2)}) collective-permute-start(bf16[25,8,128]{2,1,0:T(8,128)(2,1)} %message.1), channel_id=1, source_target_pairs={{0,12},{1,13},{2,14},{3,15},{4,8},{5,9},{6,10},{7,11},{8,4},{9,5},... | collective-permute-start | bytes 153608 | tf_op jit(solution)/shard_map/ppermute | solution.py:390
  10.2 9.9 %collective-permute-start.4 = (bf16[100,8,128]{2,1,0:T(8,128)(2,1)S(1)}, bf16[100,8,128]{2,1,0:T(8,128)(2,1)S(1)}, u32[]{:S(2)}, u32[]{:S(2)}) collective-permute-start(bf16[100,8,128]{2,1,0:T(8,128)(2,1)S(1)} %pad_maximum_fusion.refs_0_), channel_id=1, source_target_pairs={{0,2},{1,3},{2,0},{3,1},{4,6},{5,7},{6,4},{7,5},{8,10},{9,11},{10,... | collective-permute-start | bytes 614408 | tf_op jit(solution)/shard_map/ppermute | solution.py:390
  10.5 20.1 %copy-start = (bf16[512,1024]{1,0:T(8,128)(2,1)S(1)}, bf16[512,1024]{1,0:T(8,128)(2,1)}, u32[]{:S(2)}) copy-start(bf16[512,1024]{1,0:T(8,128)(2,1)} %refs_4_.1) | copy-start | bytes 3145732
  10.5 20.1 %copy-start.1 = (bf16[512,1024]{1,0:T(8,128)(2,1)S(1)}, bf16[512,1024]{1,0:T(8,128)(2,1)}, u32[]{:S(2)}) copy-start(bf16[512,1024]{1,0:T(8,128)(2,1)} %refs_5_.1) | copy-start | bytes 3145732
  10.5 20.1 %copy-start.5 = (s32[16]{0:T(128)S(1)}, s32[16]{0:T(128)}, u32[]{:S(2)}) copy-start(s32[16]{0:T(128)} %counts.5) | copy-start | bytes 196
  15.4 11.8 %collective-permute-start.18 = (bf16[2,8,8,1024]{3,2,1,0:T(8,128)(2,1)}, bf16[2,8,8,1024]{3,2,1,0:T(8,128)(2,1)S(1)}, u32[]{:S(2)}, u32[]{:S(2)}) collective-permute-start(bf16[2,8,8,1024]{3,2,1,0:T(8,128)(2,1)} %get-tuple-element.57), channel_id=1, source_target_pairs={{0,4},{1,5},{2,6},{3,7},{4,0},{5,1},{6,2},{7,3},{8,12},{9,13},{10,... | collective-permute-start | bytes 786440 | tf_op jit(solution)/shard_map/ppermute | solution.py:390
  17.6 7.3 %collective-permute-start.3 = (bf16[100,8,128]{2,1,0:T(8,128)(2,1)S(1)}, bf16[100,8,128]{2,1,0:T(8,128)(2,1)S(1)}, u32[]{:S(2)}, u32[]{:S(2)}) collective-permute-start(bf16[100,8,128]{2,1,0:T(8,128)(2,1)S(1)} %pad_maximum_fusion.refs_0_), channel_id=1, source_target_pairs={{0,1},{1,0},{2,3},{3,2},{4,5},{5,4},{6,7},{7,6},{8,9},{9,8},{10,11... | collective-permute-start | bytes 614408 | tf_op jit(solution)/shard_map/ppermute | solution.py:390
  20.1 7.6 %collective-permute-start.5 = (bf16[100,8,128]{2,1,0:T(8,128)(2,1)S(1)}, bf16[100,8,128]{2,1,0:T(8,128)(2,1)S(1)}, u32[]{:S(2)}, u32[]{:S(2)}) collective-permute-start(bf16[100,8,128]{2,1,0:T(8,128)(2,1)S(1)} %collective-permute-done.4.refs_2_), channel_id=1, source_target_pairs={{0,1},{1,0},{2,3},{3,2},{4,5},{5,4},{6,7},{7,6},{8,9},{9,8},{10,11... | collective-permute-start | bytes 614408 | tf_op jit(solution)/shard_map/ppermute | solution.py:390
  20.1 18.0 %collective-permute-start.19 = (bf16[2,8,8,1024]{3,2,1,0:T(8,128)(2,1)}, bf16[2,8,8,1024]{3,2,1,0:T(8,128)(2,1)S(1)}, u32[]{:S(2)}, u32[]{:S(2)}) collective-permute-start(bf16[2,8,8,1024]{3,2,1,0:T(8,128)(2,1)} %get-tuple-element.58), channel_id=1, source_target_pairs={{0,5},{1,4},{2,7},{3,6},{4,1},{5,0},{6,3},{7,2},{8,13},{9,12},{10,... | collective-permute-start | bytes 786440 | tf_op jit(solution)/shard_map/ppermute | solution.py:390
  24.0 28.9 %copy-start.29 = (bf16[2,8,8,1024]{3,2,1,0:T(8,128)(2,1)S(1)}, bf16[2,8,8,1024]{3,2,1,0:T(8,128)(2,1)}, u32[]{:S(2)}) copy-start(bf16[2,8,8,1024]{3,2,1,0:T(8,128)(2,1)} %get-tuple-element.61) | copy-start | bytes 786436
  24.0 40.0 %copy-start.28 = (bf16[2,8,8,1024]{3,2,1,0:T(8,128)(2,1)S(1)}, bf16[2,8,8,1024]{3,2,1,0:T(8,128)(2,1)}, u32[]{:S(2)}) copy-start(bf16[2,8,8,1024]{3,2,1,0:T(8,128)(2,1)} %get-tuple-element.62) | copy-start | bytes 786436
  24.1 51.2 %copy-start.27 = (bf16[2,8,8,1024]{3,2,1,0:T(8,128)(2,1)S(1)}, bf16[2,8,8,1024]{3,2,1,0:T(8,128)(2,1)}, u32[]{:S(2)}) copy-start(bf16[2,8,8,1024]{3,2,1,0:T(8,128)(2,1)} %get-tuple-element.63) | copy-start | bytes 786436
  24.1 57.0 %copy-start.26 = (bf16[2,8,8,1024]{3,2,1,0:T(8,128)(2,1)S(1)}, bf16[2,8,8,1024]{3,2,1,0:T(8,128)(2,1)}, u32[]{:S(2)}) copy-start(bf16[2,8,8,1024]{3,2,1,0:T(8,128)(2,1)} %get-tuple-element.64) | copy-start | bytes 786436
  24.1 66.0 %copy-start.25 = (bf16[2,8,8,1024]{3,2,1,0:T(8,128)(2,1)S(1)}, bf16[2,8,8,1024]{3,2,1,0:T(8,128)(2,1)}, u32[]{:S(2)}) copy-start(bf16[2,8,8,1024]{3,2,1,0:T(8,128)(2,1)} %get-tuple-element.65) | copy-start | bytes 786436
  24.1 71.6 %copy-start.24 = (bf16[2,8,8,1024]{3,2,1,0:T(8,128)(2,1)S(1)}, bf16[2,8,8,1024]{3,2,1,0:T(8,128)(2,1)}, u32[]{:S(2)}) copy-start(bf16[2,8,8,1024]{3,2,1,0:T(8,128)(2,1)} %get-tuple-element.66) | copy-start | bytes 786436
  24.1 72.8 %copy-start.23 = (bf16[2,8,8,1024]{3,2,1,0:T(8,128)(2,1)S(1)}, bf16[2,8,8,1024]{3,2,1,0:T(8,128)(2,1)}, u32[]{:S(2)}) copy-start(bf16[2,8,8,1024]{3,2,1,0:T(8,128)(2,1)} %get-tuple-element.67) | copy-start | bytes 786436
  24.1 73.7 %copy-start.22 = (bf16[2,8,8,1024]{3,2,1,0:T(8,128)(2,1)S(1)}, bf16[2,8,8,1024]{3,2,1,0:T(8,128)(2,1)}, u32[]{:S(2)}) copy-start(bf16[2,8,8,1024]{3,2,1,0:T(8,128)(2,1)} %get-tuple-element.70) | copy-start | bytes 786436
  24.1 74.0 %copy-start.21 = (bf16[2,8,8,1024]{3,2,1,0:T(8,128)(2,1)S(1)}, bf16[2,8,8,1024]{3,2,1,0:T(8,128)(2,1)}, u32[]{:S(2)}) copy-start(bf16[2,8,8,1024]{3,2,1,0:T(8,128)(2,1)} %get-tuple-element.71) | copy-start | bytes 786436
  24.1 28.8 %collective-permute-start.14 = (bf16[2,8,8,1024]{3,2,1,0:T(8,128)(2,1)}, bf16[2,8,8,1024]{3,2,1,0:T(8,128)(2,1)S(1)}, u32[]{:S(2)}, u32[]{:S(2)}) collective-permute-start(bf16[2,8,8,1024]{3,2,1,0:T(8,128)(2,1)} %get-tuple-element.53), channel_id=1, source_target_pairs={{0,8},{1,9},{2,10},{3,11},{4,12},{5,13},{6,14},{7,15},{8,0},{9,1},... | collective-permute-start | bytes 786440 | tf_op jit(solution)/shard_map/ppermute | solution.py:390
  25.0 39.1 %collective-permute-start.15 = (bf16[2,8,8,1024]{3,2,1,0:T(8,128)(2,1)}, bf16[2,8,8,1024]{3,2,1,0:T(8,128)(2,1)S(1)}, u32[]{:S(2)}, u32[]{:S(2)}) collective-permute-start(bf16[2,8,8,1024]{3,2,1,0:T(8,128)(2,1)} %get-tuple-element.54), channel_id=1, source_target_pairs={{0,9},{1,8},{2,11},{3,10},{4,13},{5,12},{6,15},{7,14},{8,1},{9,0},... | collective-permute-start | bytes 786440 | tf_op jit(solution)/shard_map/ppermute | solution.py:390
  27.2 105.6 %copy-start.6 = (bf16[2,8,8,1024]{3,2,1,0:T(8,128)(2,1)}, bf16[2,8,8,1024]{3,2,1,0:T(8,128)(2,1)S(1)}, u32[]{:S(2)}) copy-start(bf16[2,8,8,1024]{3,2,1,0:T(8,128)(2,1)S(1)} %collective-permute-done.18.refs_5_) | copy-start | bytes 786436
  27.2 48.0 %collective-permute-start.16 = (bf16[2,8,8,1024]{3,2,1,0:T(8,128)(2,1)}, bf16[2,8,8,1024]{3,2,1,0:T(8,128)(2,1)S(1)}, u32[]{:S(2)}, u32[]{:S(2)}) collective-permute-start(bf16[2,8,8,1024]{3,2,1,0:T(8,128)(2,1)} %get-tuple-element.55), channel_id=1, source_target_pairs={{0,10},{1,11},{2,8},{3,9},{4,14},{5,15},{6,12},{7,13},{8,2},{9,3},... | collective-permute-start | bytes 786440 | tf_op jit(solution)/shard_map/ppermute | solution.py:390
  27.7 53.3 %collective-permute-start.17 = (bf16[2,8,8,1024]{3,2,1,0:T(8,128)(2,1)}, bf16[2,8,8,1024]{3,2,1,0:T(8,128)(2,1)S(1)}, u32[]{:S(2)}, u32[]{:S(2)}) collective-permute-start(bf16[2,8,8,1024]{3,2,1,0:T(8,128)(2,1)} %get-tuple-element.56), channel_id=1, source_target_pairs={{0,11},{1,10},{2,9},{3,8},{4,15},{5,14},{6,13},{7,12},{8,3},{9,2},... | collective-permute-start | bytes 786440 | tf_op jit(solution)/shard_map/ppermute | solution.py:390
  38.1 94.7 %copy-start.7 = (bf16[2,8,8,1024]{3,2,1,0:T(8,128)(2,1)}, bf16[2,8,8,1024]{3,2,1,0:T(8,128)(2,1)S(1)}, u32[]{:S(2)}) copy-start(bf16[2,8,8,1024]{3,2,1,0:T(8,128)(2,1)S(1)} %collective-permute-done.19.refs_6_) | copy-start | bytes 786436
  38.1 60.0 %collective-permute-start.6 = (bf16[8,27,8,128]{3,2,1,0:T(8,128)(2,1)S(1)}, bf16[8,27,8,128]{3,2,1,0:T(8,128)(2,1)S(1)}, u32[]{:S(2)}, u32[]{:S(2)}) collective-permute-start(bf16[8,27,8,128]{3,2,1,0:T(8,128)(2,1)S(1)} %get-tuple-element.41), channel_id=1, source_target_pairs={{0,1},{1,0},{2,3},{3,2},{4,5},{5,4},{6,7},{7,6},{8,9},{9,8},{10,11... | collective-permute-start | bytes 1327112 | tf_op jit(solution)/shard_map/ppermute | solution.py:390
  52.9 79.8 %copy-start.8 = (bf16[2,8,8,1024]{3,2,1,0:T(8,128)(2,1)}, bf16[2,8,8,1024]{3,2,1,0:T(8,128)(2,1)S(1)}, u32[]{:S(2)}) copy-start(bf16[2,8,8,1024]{3,2,1,0:T(8,128)(2,1)S(1)} %collective-permute-done.14.refs_1_) | copy-start | bytes 786436
  53.0 37.1 %collective-permute-start.20 = (bf16[2,8,8,1024]{3,2,1,0:T(8,128)(2,1)S(1)}, bf16[2,8,8,1024]{3,2,1,0:T(8,128)(2,1)S(1)}, u32[]{:S(2)}, u32[]{:S(2)}) collective-permute-start(bf16[2,8,8,1024]{3,2,1,0:T(8,128)(2,1)S(1)} %copy-done.29), channel_id=1, source_target_pairs={{0,12},{1,13},{2,14},{3,15},{4,8},{5,9},{6,10},{7,11},{8,4},{9,5},... | collective-permute-start | bytes 786440 | tf_op jit(solution)/shard_map/ppermute | solution.py:390
  64.0 68.7 %copy-start.9 = (bf16[2,8,8,1024]{3,2,1,0:T(8,128)(2,1)}, bf16[2,8,8,1024]{3,2,1,0:T(8,128)(2,1)S(1)}, u32[]{:S(2)}) copy-start(bf16[2,8,8,1024]{3,2,1,0:T(8,128)(2,1)S(1)} %collective-permute-done.15.refs_2_) | copy-start | bytes 786436
  64.0 31.6 %collective-permute-start.21 = (bf16[2,8,8,1024]{3,2,1,0:T(8,128)(2,1)S(1)}, bf16[2,8,8,1024]{3,2,1,0:T(8,128)(2,1)S(1)}, u32[]{:S(2)}, u32[]{:S(2)}) collective-permute-start(bf16[2,8,8,1024]{3,2,1,0:T(8,128)(2,1)S(1)} %copy-done.28), channel_id=1, source_target_pairs={{0,13},{1,12},{2,15},{3,14},{4,9},{5,8},{6,11},{7,10},{8,5},{9,4},... | collective-permute-start | bytes 786440 | tf_op jit(solution)/shard_map/ppermute | solution.py:390
  75.3 57.5 %copy-start.10 = (bf16[2,8,8,1024]{3,2,1,0:T(8,128)(2,1)}, bf16[2,8,8,1024]{3,2,1,0:T(8,128)(2,1)S(1)}, u32[]{:S(2)}) copy-start(bf16[2,8,8,1024]{3,2,1,0:T(8,128)(2,1)S(1)} %collective-permute-done.16.refs_3_) | copy-start | bytes 786436
  75.3 21.6 %collective-permute-start.22 = (bf16[2,8,8,1024]{3,2,1,0:T(8,128)(2,1)S(1)}, bf16[2,8,8,1024]{3,2,1,0:T(8,128)(2,1)S(1)}, u32[]{:S(2)}, u32[]{:S(2)}) collective-permute-start(bf16[2,8,8,1024]{3,2,1,0:T(8,128)(2,1)S(1)} %copy-done.27), channel_id=1, source_target_pairs={{0,6},{1,7},{2,4},{3,5},{4,2},{5,3},{6,0},{7,1},{8,14},{9,15},{10,... | collective-permute-start | bytes 786440 | tf_op jit(solution)/shard_map/ppermute | solution.py:390
  81.1 51.7 %copy-start.11 = (bf16[2,8,8,1024]{3,2,1,0:T(8,128)(2,1)}, bf16[2,8,8,1024]{3,2,1,0:T(8,128)(2,1)S(1)}, u32[]{:S(2)}) copy-start(bf16[2,8,8,1024]{3,2,1,0:T(8,128)(2,1)S(1)} %collective-permute-done.17.refs_4_) | copy-start | bytes 786436
  81.1 16.7 %collective-permute-start.23 = (bf16[2,8,8,1024]{3,2,1,0:T(8,128)(2,1)S(1)}, bf16[2,8,8,1024]{3,2,1,0:T(8,128)(2,1)S(1)}, u32[]{:S(2)}, u32[]{:S(2)}) collective-permute-start(bf16[2,8,8,1024]{3,2,1,0:T(8,128)(2,1)S(1)} %copy-done.26), channel_id=1, source_target_pairs={{0,7},{1,6},{2,5},{3,4},{4,3},{5,2},{6,1},{7,0},{8,15},{9,14},{10,... | collective-permute-start | bytes 786440 | tf_op jit(solution)/shard_map/ppermute | solution.py:390
  90.1 45.1 %copy-start.12 = (bf16[2,8,8,1024]{3,2,1,0:T(8,128)(2,1)}, bf16[2,8,8,1024]{3,2,1,0:T(8,128)(2,1)S(1)}, u32[]{:S(2)}) copy-start(bf16[2,8,8,1024]{3,2,1,0:T(8,128)(2,1)S(1)} %collective-permute-done.20.refs_2_) | copy-start | bytes 786436
  90.1 12.7 %collective-permute-start.24 = (bf16[2,8,8,1024]{3,2,1,0:T(8,128)(2,1)S(1)}, bf16[2,8,8,1024]{3,2,1,0:T(8,128)(2,1)S(1)}, u32[]{:S(2)}, u32[]{:S(2)}) collective-permute-start(bf16[2,8,8,1024]{3,2,1,0:T(8,128)(2,1)S(1)} %copy-done.25), channel_id=1, source_target_pairs={{0,1},{1,0},{2,3},{3,2},{4,5},{5,4},{6,7},{7,6},{8,9},{9,8},{10,11... | collective-permute-start | bytes 786440 | tf_op jit(solution)/shard_map/ppermute | solution.py:390
  95.7 39.5 %copy-start.13 = (bf16[2,8,8,1024]{3,2,1,0:T(8,128)(2,1)}, bf16[2,8,8,1024]{3,2,1,0:T(8,128)(2,1)S(1)}, u32[]{:S(2)}) copy-start(bf16[2,8,8,1024]{3,2,1,0:T(8,128)(2,1)S(1)} %collective-permute-done.21.refs_3_) | copy-start | bytes 786436
  95.7 8.2 %collective-permute-start.25 = (bf16[2,8,8,1024]{3,2,1,0:T(8,128)(2,1)S(1)}, bf16[2,8,8,1024]{3,2,1,0:T(8,128)(2,1)S(1)}, u32[]{:S(2)}, u32[]{:S(2)}) collective-permute-start(bf16[2,8,8,1024]{3,2,1,0:T(8,128)(2,1)S(1)} %copy-done.24), channel_id=1, source_target_pairs={{0,2},{1,3},{2,0},{3,1},{4,6},{5,7},{6,4},{7,5},{8,10},{9,11},{10,... | collective-permute-start | bytes 786440 | tf_op jit(solution)/shard_map/ppermute | solution.py:390
  96.9 38.3 %copy-start.14 = (bf16[2,8,8,1024]{3,2,1,0:T(8,128)(2,1)}, bf16[2,8,8,1024]{3,2,1,0:T(8,128)(2,1)S(1)}, u32[]{:S(2)}) copy-start(bf16[2,8,8,1024]{3,2,1,0:T(8,128)(2,1)S(1)} %collective-permute-done.22.refs_4_) | copy-start | bytes 786436
  96.9 16.5 %collective-permute-start.26 = (bf16[2,8,8,1024]{3,2,1,0:T(8,128)(2,1)S(1)}, bf16[2,8,8,1024]{3,2,1,0:T(8,128)(2,1)S(1)}, u32[]{:S(2)}, u32[]{:S(2)}) collective-permute-start(bf16[2,8,8,1024]{3,2,1,0:T(8,128)(2,1)S(1)} %copy-done.23), channel_id=1, source_target_pairs={{0,3},{1,2},{2,1},{3,0},{4,7},{5,6},{6,5},{7,4},{8,11},{9,10},{10,... | collective-permute-start | bytes 786440 | tf_op jit(solution)/shard_map/ppermute | solution.py:390
  97.8 37.4 %copy-start.15 = (bf16[2,8,8,1024]{3,2,1,0:T(8,128)(2,1)}, bf16[2,8,8,1024]{3,2,1,0:T(8,128)(2,1)S(1)}, u32[]{:S(2)}) copy-start(bf16[2,8,8,1024]{3,2,1,0:T(8,128)(2,1)S(1)} %collective-permute-done.23.refs_5_) | copy-start | bytes 786436
  97.8 22.6 %collective-permute-start.27 = (bf16[2,8,8,1024]{3,2,1,0:T(8,128)(2,1)S(1)}, bf16[2,8,8,1024]{3,2,1,0:T(8,128)(2,1)S(1)}, u32[]{:S(2)}, u32[]{:S(2)}) collective-permute-start(bf16[2,8,8,1024]{3,2,1,0:T(8,128)(2,1)S(1)} %copy-done.22), channel_id=1, source_target_pairs={{0,14},{1,15},{2,12},{3,13},{4,10},{5,11},{6,8},{7,9},{8,6},{9,7},... | collective-permute-start | bytes 786440 | tf_op jit(solution)/shard_map/ppermute | solution.py:390
  98.2 30.6 %collective-permute-start.28 = (bf16[2,8,8,1024]{3,2,1,0:T(8,128)(2,1)S(1)}, bf16[2,8,8,1024]{3,2,1,0:T(8,128)(2,1)S(1)}, u32[]{:S(2)}, u32[]{:S(2)}) collective-permute-start(bf16[2,8,8,1024]{3,2,1,0:T(8,128)(2,1)S(1)} %copy-done.21), channel_id=1, source_target_pairs={{0,15},{1,14},{2,13},{3,12},{4,11},{5,10},{6,9},{7,8},{8,7},{9,6},... | collective-permute-start | bytes 786440 | tf_op jit(solution)/shard_map/ppermute | solution.py:390
  102.8 32.4 %copy-start.16 = (bf16[2,8,8,1024]{3,2,1,0:T(8,128)(2,1)}, bf16[2,8,8,1024]{3,2,1,0:T(8,128)(2,1)S(1)}, u32[]{:S(2)}) copy-start(bf16[2,8,8,1024]{3,2,1,0:T(8,128)(2,1)S(1)} %collective-permute-done.24.refs_6_) | copy-start | bytes 786436
  102.8 26.7 %collective-permute-start.10 = (bf16[27,8,128]{2,1,0:T(8,128)(2,1)S(1)}, bf16[27,8,128]{2,1,0:T(8,128)(2,1)S(1)}, u32[]{:S(2)}, u32[]{:S(2)}) collective-permute-start(bf16[27,8,128]{2,1,0:T(8,128)(2,1)S(1)} %get-tuple-element.46), channel_id=1, source_target_pairs={{0,8},{1,9},{2,10},{3,11},{4,12},{5,13},{6,14},{7,15},{8,0},{9,1},... | collective-permute-start | bytes 165896 | tf_op jit(solution)/shard_map/ppermute | solution.py:390
  103.9 31.3 %copy-start.17 = (bf16[2,8,8,1024]{3,2,1,0:T(8,128)(2,1)}, bf16[2,8,8,1024]{3,2,1,0:T(8,128)(2,1)S(1)}, u32[]{:S(2)}) copy-start(bf16[2,8,8,1024]{3,2,1,0:T(8,128)(2,1)S(1)} %collective-permute-done.25.refs_7_) | copy-start | bytes 786436
  103.9 26.8 %collective-permute-start.11 = (bf16[27,8,128]{2,1,0:T(8,128)(2,1)S(1)}, bf16[27,8,128]{2,1,0:T(8,128)(2,1)S(1)}, u32[]{:S(2)}, u32[]{:S(2)}) collective-permute-start(bf16[27,8,128]{2,1,0:T(8,128)(2,1)S(1)} %get-tuple-element.47), channel_id=1, source_target_pairs={{0,10},{1,11},{2,8},{3,9},{4,14},{5,15},{6,12},{7,13},{8,2},{9,3},... | collective-permute-start | bytes 165896 | tf_op jit(solution)/shard_map/ppermute | solution.py:390
  113.4 21.9 %copy-start.18 = (bf16[2,8,8,1024]{3,2,1,0:T(8,128)(2,1)}, bf16[2,8,8,1024]{3,2,1,0:T(8,128)(2,1)S(1)}, u32[]{:S(2)}) copy-start(bf16[2,8,8,1024]{3,2,1,0:T(8,128)(2,1)S(1)} %collective-permute-done.26.refs_8_) | copy-start | bytes 786436
  113.4 26.7 %collective-permute-start.12 = (bf16[27,8,128]{2,1,0:T(8,128)(2,1)S(1)}, bf16[27,8,128]{2,1,0:T(8,128)(2,1)S(1)}, u32[]{:S(2)}, u32[]{:S(2)}) collective-permute-start(bf16[27,8,128]{2,1,0:T(8,128)(2,1)S(1)} %get-tuple-element.48), channel_id=1, source_target_pairs={{0,12},{1,13},{2,14},{3,15},{4,8},{5,9},{6,10},{7,11},{8,4},{9,5},... | collective-permute-start | bytes 165896 | tf_op jit(solution)/shard_map/ppermute | solution.py:390
  120.4 12.4 %copy-start.19 = (bf16[2,8,8,1024]{3,2,1,0:T(8,128)(2,1)}, bf16[2,8,8,1024]{3,2,1,0:T(8,128)(2,1)S(1)}, u32[]{:S(2)}) copy-start(bf16[2,8,8,1024]{3,2,1,0:T(8,128)(2,1)S(1)} %collective-permute-done.27.refs_2_) | copy-start | bytes 786436
  120.4 19.7 %collective-permute-start.13 = (bf16[27,8,128]{2,1,0:T(8,128)(2,1)S(1)}, bf16[27,8,128]{2,1,0:T(8,128)(2,1)S(1)}, u32[]{:S(2)}, u32[]{:S(2)}) collective-permute-start(bf16[27,8,128]{2,1,0:T(8,128)(2,1)S(1)} %get-tuple-element.49), channel_id=1, source_target_pairs={{0,14},{1,15},{2,12},{3,13},{4,10},{5,11},{6,8},{7,9},{8,6},{9,7},... | collective-permute-start | bytes 165896 | tf_op jit(solution)/shard_map/ppermute | solution.py:390
  128.7 4.1 %copy-start.20 = (bf16[2,8,8,1024]{3,2,1,0:T(8,128)(2,1)}, bf16[2,8,8,1024]{3,2,1,0:T(8,128)(2,1)S(1)}, u32[]{:S(2)}) copy-start(bf16[2,8,8,1024]{3,2,1,0:T(8,128)(2,1)S(1)} %collective-permute-done.28.refs_3_) | copy-start | bytes 786436
  128.7 11.4 %collective-permute-start.7 = (bf16[27,8,128]{2,1,0:T(8,128)(2,1)S(1)}, bf16[27,8,128]{2,1,0:T(8,128)(2,1)S(1)}, u32[]{:S(2)}, u32[]{:S(2)}) collective-permute-start(bf16[27,8,128]{2,1,0:T(8,128)(2,1)S(1)} %get-tuple-element.43), channel_id=1, source_target_pairs={{0,2},{1,3},{2,0},{3,1},{4,6},{5,7},{6,4},{7,5},{8,10},{9,11},{10,... | collective-permute-start | bytes 165896 | tf_op jit(solution)/shard_map/ppermute | solution.py:390
  129.5 10.6 %collective-permute-start.8 = (bf16[27,8,128]{2,1,0:T(8,128)(2,1)S(1)}, bf16[27,8,128]{2,1,0:T(8,128)(2,1)S(1)}, u32[]{:S(2)}, u32[]{:S(2)}) collective-permute-start(bf16[27,8,128]{2,1,0:T(8,128)(2,1)S(1)} %get-tuple-element.44), channel_id=1, source_target_pairs={{0,4},{1,5},{2,6},{3,7},{4,0},{5,1},{6,2},{7,3},{8,12},{9,13},{10,... | collective-permute-start | bytes 165896 | tf_op jit(solution)/shard_map/ppermute | solution.py:390
  130.7 9.4 %collective-permute-start.9 = (bf16[27,8,128]{2,1,0:T(8,128)(2,1)S(1)}, bf16[27,8,128]{2,1,0:T(8,128)(2,1)S(1)}, u32[]{:S(2)}, u32[]{:S(2)}) collective-permute-start(bf16[27,8,128]{2,1,0:T(8,128)(2,1)S(1)} %get-tuple-element.45), channel_id=1, source_target_pairs={{0,6},{1,7},{2,4},{3,5},{4,2},{5,3},{6,0},{7,1},{8,14},{9,15},{10,... | collective-permute-start | bytes 165896 | tf_op jit(solution)/shard_map/ppermute | solution.py:390
  137.6 2.5 %copy-start.2 = (bf16[25,8,128]{2,1,0:T(8,128)(2,1)S(1)}, bf16[25,8,128]{2,1,0:T(8,128)(2,1)}, u32[]{:S(2)}) copy-start(bf16[25,8,128]{2,1,0:T(8,128)(2,1)} %message.1) | copy-start | bytes 153604
  137.6 2.5 %copy-start.3 = (bf16[1,2,1024]{2,1,0:T(2,128)(2,1)S(1)}, bf16[1,2,1024]{2,1,0:T(2,128)(2,1)}, u32[]{:S(2)}) copy-start(bf16[1,2,1024]{2,1,0:T(2,128)(2,1)} %param.15) | copy-start | bytes 12292
  137.6 2.5 %copy-start.4 = (bf16[1,2,1024]{2,1,0:T(2,128)(2,1)S(1)}, bf16[1,2,1024]{2,1,0:T(2,128)(2,1)}, u32[]{:S(2)}) copy-start(bf16[1,2,1024]{2,1,0:T(2,128)(2,1)} %param.16) | copy-start | bytes 12292

commit v6 on v5

--- a/solution.py
+++ b/solution.py
@@ -17,6 +17,7 @@
 VMEM = pltpu.MemorySpace.VMEM
 SMEM = pltpu.MemorySpace.SMEM
 LIMIT = 32 * 1024 * 1024
+SMALL = 8 * 1024 * 1024
 
 
 def whole(space):
@@ -230,10 +231,18 @@
     )(counts, *messages, keys, values)
 
 
-def fold_kernel(rows, keep, got, *outs):
+def fold_kernel(rows, split, keep, got, *outs):
     lane = lax.broadcasted_iota(jnp.int32, (GRP, 128), 1)
     inside = lane < KVH
-    for j, out in enumerate(outs):
+
+    def put(j, at, value):
+        value = value.astype(jnp.bfloat16)
+        if split:
+            outs[j % 2][j // 2, at] = value
+        else:
+            outs[j][at] = value
+
+    for j in range(keep.shape[0]):
         for r in range(rows):
             raw = [ref[j, rows * KVH + r].astype(jnp.float32) for ref in (keep, got)]
             high = jnp.maximum(jnp.where(inside, raw[0], 0.0), jnp.where(inside, raw[1], 0.0))
@@ -244,21 +253,26 @@
             total = jnp.where(inside, factors[0] * sizes[0] + factors[1] * sizes[1], 0.0)
             coarse = total.astype(jnp.bfloat16).astype(jnp.float32)
             line = high + pltpu.roll(coarse, KVH, 1) + pltpu.roll(total - coarse, 2 * KVH, 1)
-            out[rows * KVH + r] = line.astype(jnp.bfloat16)
+            put(j, rows * KVH + r, line)
             for g in range(KVH):
                 at = r * KVH + g
                 mixed = factors[0][:, g : g + 1] * keep[j, at].astype(jnp.float32)
                 mixed = mixed + factors[1][:, g : g + 1] * got[j, at].astype(jnp.float32)
-                out[at] = mixed.astype(jnp.bfloat16)
-
-
-def fold(rows, keep, got):
-    piece = jax.ShapeDtypeStruct(keep.shape[1:], keep.dtype)
-    return pl.pallas_call(
-        functools.partial(fold_kernel, rows),
-        out_shape=(piece,) * keep.shape[0],
+                put(j, at, mixed)
+
+
+def fold(rows, split, keep, got):
+    number = keep.shape[0]
+    if split:
+        half = jax.ShapeDtypeStruct((number // 2,) + keep.shape[1:], keep.dtype)
+        outs = (half, half)
+    else:
+        outs = (jax.ShapeDtypeStruct(keep.shape[1:], keep.dtype),) * number
+    return pl.pallas_call(
+        functools.partial(fold_kernel, rows, split),
+        out_shape=outs,
         in_specs=[whole(VMEM)] * 2,
-        out_specs=(whole(VMEM),) * keep.shape[0],
+        out_specs=(whole(VMEM),) * len(outs),
         compiler_params=pltpu.CompilerParams(vmem_limit_bytes=LIMIT),
         cost_estimate=pl.CostEstimate(
             flops=keep.size * 4, transcendentals=0, bytes_accessed=keep.size * 6
@@ -269,42 +283,34 @@
 
 def settle_kernel(partners, old, *refs):
     refs = refs[old:]
-    pieces, refs = refs[: len(partners)], refs[len(partners) :]
-    store_k, store_v, held, sems_in, sems_out = refs
+    pieces, (store_k, store_v, sems) = refs[: len(partners)], refs[len(partners) :]
     me = lax.axis_index("seq")
-    fetches = [
-        pltpu.make_async_copy(piece, held.at[i], sems_in.at[i]) for i, piece in enumerate(pieces)
-    ]
-    for fetch in fetches:
-        fetch.start()
     puts = []
-    for i, (partner, fetch) in enumerate(zip(partners, fetches)):
-        fetch.wait()
+    for partner, piece in zip(partners, pieces):
         for part, store in enumerate((store_k, store_v)):
-            put = pltpu.make_async_copy(
-                held.at[i, part], store.at[me ^ partner], sems_out.at[2 * i + part]
+            puts.append(
+                pltpu.make_async_copy(
+                    piece.at[part], store.at[me ^ partner], sems.at[len(puts)]
+                )
             )
-            put.start()
-            puts.append(put)
+    for put in puts:
+        put.start()
     for put in puts:
         put.wait()
 
 
-def settle(shards, partners, pieces, stores=()):
+def settle(shards, partners, pieces, stores):
     number = len(partners)
     shape = (shards,) + pieces[0].shape[1:]
     store = jax.ShapeDtypeStruct(shape, pieces[0].dtype)
     return pl.pallas_call(
         functools.partial(settle_kernel, partners, len(stores)),
         out_shape=(store, store),
-        in_specs=[whole(pl.ANY)] * (len(stores) + number),
+        in_specs=[whole(pl.ANY)] * len(stores) + [whole(VMEM)] * number,
         out_specs=(whole(pl.ANY),) * 2,
         input_output_aliases={i: i for i in range(len(stores))},
-        scratch_shapes=[
-            pltpu.VMEM((number,) + pieces[0].shape, pieces[0].dtype),
-            pltpu.SemaphoreType.DMA((number,)),
-            pltpu.SemaphoreType.DMA((2 * number,)),
-        ],
+        scratch_shapes=[pltpu.SemaphoreType.DMA((2 * number,))],
+        compiler_params=pltpu.CompilerParams(vmem_limit_bytes=SMALL),
         cost_estimate=pl.CostEstimate(
             flops=0, transcendentals=0, bytes_accessed=4 * number * pieces[0].size
         ),
@@ -392,13 +398,13 @@
 
 def send_order(shards):
     upper = list(range(shards // 2, shards))
-    lower = [k for k in range(1, shards // 2)]
-    quarter = len(upper) // 2
-    early = upper[:quarter]
-    side = [k for k in lower if k >= 4] + [k for k in lower if k < 4]
-    before, after = side[: quarter // 2], side[quarter // 2 :]
-    late = upper[quarter:]
-    return early, before, late, after
+    side = [k for k in range(1, shards // 2) if k >= 4] + [1, 2, 3]
+    half = len(upper) // 2
+    first = upper[:1]
+    second = upper[1:half] + side[:2] + upper[half : half + 1] + side[2:3]
+    third = upper[half + 1 : half + 2] + side[3:]
+    fourth = upper[half + 2 :]
+    return first, second, third, fourth
 
 
 def per_device(
@@ -413,13 +419,13 @@
     pages_k = cache_k.reshape(page_slots, PAGE, KVD)
     pages_v = cache_v.reshape(page_slots, PAGE, KVD)
     rows = rows_p + rows_d
-    early, before, late, after = send_order(shards)
+    first, second, third, fourth = send_order(shards)
     pieces = {}
     message = make_message(prefill_q, decode_q, page_owner, context_len)
     far = [message]
     for k in range(4, shards, 4):
         far.append(swap(message, k))
-    for group in (early, [0] + before + late + after):
+    for group in (first, [0] + second + third + fourth):
         packed = pack(owners, page_counts, pages_k, pages_v, shards, capacity, group)
         for k, piece in zip(group, packed):
             pieces[k] = swap(piece, k) if k else piece
@@ -437,13 +443,15 @@
         cache_v,
     )
     got = swap(give, 1)
-    folded = fold(rows, keep, got)
+    keep, give = fold(rows, True, keep, got)
+    got = swap(give, 2)
+    folded = fold(rows, False, keep, got)
     parts = [folded[0]]
-    for j in range(1, shards // 2):
-        parts.append(swap(folded[j], 2 * j))
+    for j in range(1, shards // 4):
+        parts.append(swap(folded[j], 4 * j))
     prefill_out, decode_out = merge(rows_p, rows_d, parts, message, decode_k, decode_v)
     stores = ()
-    for group in ([0] + early + before, late[:-2] + after, late[-2:]):
+    for group in ([0] + first + second, third, fourth):
         stores = settle(shards, group, [pieces[k] for k in group], stores)
     store_page = table[:, :capacity].reshape(-1)
     return (

time: 144 us -> 131 us (0.910)
  the two profiles are of different devices: /device:TPU:13 before, /device:TPU:0 now
where the time goes in v6:
time: 131 us
  waiting for transfers between devices  72.9 us (56%)
  starting transfers between devices  26 us (20%)
  Pallas kernels  25.9 us (20%)
  local copies, waits for them, and re-layouts  3.86 us (3%)
  between operations  1.58 us (1%)
    ppermute x26, waiting for transfers between devices, swap(): lax.ppermute(array, 'seq', [(i, i ^ distance) for i in range(shards)])  72.9 us
    ppermute x26, starting transfers between devices, swap(): lax.ppermute(array, 'seq', [(i, i ^ distance) for i in range(shards)])  26 us
    pallas_call x1, Pallas kernels, attend(): pl.pallas_call(functools.partial(attend_kernel, rows_p, rows_d, capacity)...  8.27 us
    pallas_call x2, Pallas kernels, pack(): pl.pallas_call(functools.partial(pack_kernel, shards, capacity, partners)...  7.84 us
    pallas_call x2, Pallas kernels, fold(): pl.pallas_call(functools.partial(fold_kernel, rows, split), out_shape=out...  3.71 us
    pallas_call x3, Pallas kernels, settle(): pl.pallas_call(functools.partial(settle_kernel, partners, len(stores)), o...  3.51 us
    unnamed x24, local copies, waits for them, and re-layouts  3.26 us
  transfers between devices with their start and end apart: 26, of which 13 were waited for; matrix products, arithmetic and copies ran while one was open for 0% of the time, Pallas kernels for 18%

profile of v6, /device:TPU:0, one launch (start us, length us, event | category | flops | bytes accessed | tf_op | source)
XLA Modules:
  0.0 131.2 jit_solution(2504619045864589020)
XLA Ops:
  0.6 0.0 copy-start
  0.6 0.0 copy-start.1
  0.7 0.0 copy-start.6
  1.5 1.5 %message.1 = bf16[25,8,128]{2,1,0:T(8,128)(2,1)} custom-call(s32[1,1]{1,0:T(1,128)} %bitcast.12.length, bf16[1,8192]{1,0:T(2,128)(2,1)} %prefill_q.1, bf16[2,8192]{1,0:T(2,128)(2,1)} %bitcast.22, s32[1,64]{1,0:T(1,128)} %bitcast.23), custom_call_target="tpu_custom_call" | custom-call | tf_op jit(solution)/shard_map/message/pallas_call | solution.py:51
  2.9 3.1 %collective-permute-start = (bf16[25,8,128]{2,1,0:T(8,128)(2,1)}, bf16[25,8,128]{2,1,0:T(8,128)(2,1)S(1)}, u32[]{:S(2)}, u32[]{:S(2)}) collective-permute-start(bf16[25,8,128]{2,1,0:T(8,128)(2,1)} %message.1), channel_id=1, source_target_pairs={{0,4},{1,5},{2,6},{3,7},{4,0},{5,1},{6,2},{7,3},{8,12},{9,13},{10,... | collective-permute-start | bytes 153608 | tf_op jit(solution)/shard_map/ppermute | solution.py:396
  6.0 2.6 %collective-permute-start.1 = (bf16[25,8,128]{2,1,0:T(8,128)(2,1)}, bf16[25,8,128]{2,1,0:T(8,128)(2,1)S(1)}, u32[]{:S(2)}, u32[]{:S(2)}) collective-permute-start(bf16[25,8,128]{2,1,0:T(8,128)(2,1)} %message.1), channel_id=1, source_target_pairs={{0,8},{1,9},{2,10},{3,11},{4,12},{5,13},{6,14},{7,15},{8,0},{9,1},... | collective-permute-start | bytes 153608 | tf_op jit(solution)/shard_map/ppermute | solution.py:396
  8.6 0.0 collective-permute-start.2
  8.6 0.0 collective-permute-done
  8.6 3.6 %collective-permute-done.1 = bf16[25,8,128]{2,1,0:T(8,128)(2,1)S(1)} collective-permute-done((bf16[25,8,128]{2,1,0:T(8,128)(2,1)}, bf16[25,8,128]{2,1,0:T(8,128)(2,1)S(1)}, u32[]{:S(2)}, u32[]{:S(2)}) %collective-permute-start.1) | collective-permute-done | bytes 51232 | tf_op jit(solution)/shard_map/ppermute | solution.py:396
  12.2 2.5 %collective-permute-done.2 = bf16[25,8,128]{2,1,0:T(8,128)(2,1)S(1)} collective-permute-done((bf16[25,8,128]{2,1,0:T(8,128)(2,1)}, bf16[25,8,128]{2,1,0:T(8,128)(2,1)S(1)}, u32[]{:S(2)}, u32[]{:S(2)}) %collective-permute-start.2) | collective-permute-done | bytes 51232 | tf_op jit(solution)/shard_map/ppermute | solution.py:396
  14.7 0.8 pad_maximum_fusion.refs_0_
  15.5 1.6 %collective-permute-start.4 = (bf16[100,8,128]{2,1,0:T(8,128)(2,1)S(1)}, bf16[100,8,128]{2,1,0:T(8,128)(2,1)S(1)}, u32[]{:S(2)}, u32[]{:S(2)}) collective-permute-start(bf16[100,8,128]{2,1,0:T(8,128)(2,1)S(1)} %pad_maximum_fusion.refs_0_), channel_id=1, source_target_pairs={{0,2},{1,3},{2,0},{3,1},{4,6},{5,7},{6,4},{7,5},{8,10},{9,11},{10,... | collective-permute-start | bytes 614408 | tf_op jit(solution)/shard_map/ppermute | solution.py:396
  17.1 0.0 collective-permute-start.3
  17.1 4.2 %collective-permute-done.4.refs_2_ = bf16[100,8,128]{2,1,0:T(8,128)(2,1)S(1)} collective-permute-done((bf16[100,8,128]{2,1,0:T(8,128)(2,1)S(1)}, bf16[100,8,128]{2,1,0:T(8,128)(2,1)S(1)}, u32[]{:S(2)}, u32[]{:S(2)}) %collective-permute-start.4) | collective-permute-done | bytes 204832 | tf_op jit(solution)/shard_map/ppermute | solution.py:396
  21.4 0.0 collective-permute-start.5
  21.4 4.9 %pack.2 = (bf16[2,8,8,1024]{3,2,1,0:T(8,128)(2,1)}, bf16[2,8,8,1024]{3,2,1,0:T(8,128)(2,1)}, bf16[2,8,8,1024]{3,2,1,0:T(8,128)(2,1)}, bf16[2,8,8,1024]{3,2,1,0:T...) custom-call(s32[64]{0:T(128)} %bitcast.24, ...), custom_call_target="tpu_custom_call" | custom-call | bytes 9961472 | tf_op jit(solution)/shard_map/pack/pallas_call | solution.py:97
  26.3 0.8 collective-permute-start.12
  27.1 3.4 %collective-permute-start.13 = (bf16[2,8,8,1024]{3,2,1,0:T(8,128)(2,1)}, bf16[2,8,8,1024]{3,2,1,0:T(8,128)(2,1)S(1)}, u32[]{:S(2)}, u32[]{:S(2)}) collective-permute-start(bf16[2,8,8,1024]{3,2,1,0:T(8,128)(2,1)} %get-tuple-element.49), channel_id=1, source_target_pairs={{0,10},{1,11},{2,8},{3,9},{4,14},{5,15},{6,12},{7,13},{8,2},{9,3},... | collective-permute-start | bytes 786440 | tf_op jit(solution)/shard_map/ppermute | solution.py:396
  30.5 0.0 collective-permute-done.3.refs_1_
  30.5 0.7 copy-done.7
  31.2 0.0 collective-permute-done.5.refs_3_
  31.2 0.7 copy-done.9
  31.9 0.9 copy-done.8
  32.8 0.9 copy-done.10
  33.8 8.3 %attend.1 = (bf16[8,27,8,128]{3,2,1,0:T(8,128)(2,1)S(1)}, bf16[8,27,8,128]{3,2,1,0:T(8,128)(2,1)}, s32[16,128]{1,0:T(8,128)S(1)}) custom-call(s32[16]{0:T(128)S(1)} %copy-done.6, bf16[100,8,128]{2,1,0:T(8,128)(2,1)S(1)} %pad_maximum_fusion.refs_0_, bf16[100,8,128]{2,1,0:T(8,128)(2,1)S(1)} %copy-done.8, ...), custom_call_target="tpu_custom_call" | custom-call | flops 805306368 | bytes 3670016 | tf_op jit(solution)/shard_map/attend/pallas_call | solution.py:214
  42.0 0.0 collective-permute-start.6
  42.1 0.5 collective-permute-start.14
  42.6 0.5 collective-permute-start.15
  43.1 8.4 %collective-permute-done.12.refs_2_ = bf16[2,8,8,1024]{3,2,1,0:T(8,128)(2,1)S(1)} collective-permute-done((bf16[2,8,8,1024]{3,2,1,0:T(8,128)(2,1)}, bf16[2,8,8,1024]{3,2,1,0:T(8,128)(2,1)S(1)}, u32[]{:S(2)}, u32[]{:S(2)}) %collective-permute-start.12) | collective-permute-done | bytes 262176 | tf_op jit(solution)/shard_map/ppermute | solution.py:396
  51.4 7.1 %collective-permute-done.13.refs_3_ = bf16[2,8,8,1024]{3,2,1,0:T(8,128)(2,1)S(1)} collective-permute-done((bf16[2,8,8,1024]{3,2,1,0:T(8,128)(2,1)}, bf16[2,8,8,1024]{3,2,1,0:T(8,128)(2,1)S(1)}, u32[]{:S(2)}, u32[]{:S(2)}) %collective-permute-start.13) | collective-permute-done | bytes 262176 | tf_op jit(solution)/shard_map/ppermute | solution.py:396
  58.5 2.3 %collective-permute-start.17 = (bf16[2,8,8,1024]{3,2,1,0:T(8,128)(2,1)}, bf16[2,8,8,1024]{3,2,1,0:T(8,128)(2,1)S(1)}, u32[]{:S(2)}, u32[]{:S(2)}) collective-permute-start(bf16[2,8,8,1024]{3,2,1,0:T(8,128)(2,1)} %get-tuple-element.53), channel_id=1, source_target_pairs={{0,12},{1,13},{2,14},{3,15},{4,8},{5,9},{6,10},{7,11},{8,4},{9,5},... | collective-permute-start | bytes 786440 | tf_op jit(solution)/shard_map/ppermute | solution.py:396
  60.8 8.7 %collective-permute-done.14.refs_4_ = bf16[2,8,8,1024]{3,2,1,0:T(8,128)(2,1)S(1)} collective-permute-done((bf16[2,8,8,1024]{3,2,1,0:T(8,128)(2,1)S(1)}, bf16[2,8,8,1024]{3,2,1,0:T(8,128)(2,1)S(1)}, u32[]{:S(2)}, u32[]{:S(2)}) %collective-permute-start.14) | collective-permute-done | bytes 262176 | tf_op jit(solution)/shard_map/ppermute | solution.py:396
  69.6 2.9 %pack.3 = bf16[2,8,8,1024]{3,2,1,0:T(8,128)(2,1)} custom-call(s32[64]{0:T(128)} %bitcast.25, s32[16]{0:T(128)} %counts.5, bf16[64,8,1024]{2,1,0:T(8,128)(2,1)} %bitcast.14, bf16[64,8,1024]{2,1,0:T(8,128)(2,1)} %bitcast.16), custom_call_target="tpu_custom_call" | custom-call | bytes 2621440 | tf_op jit(solution)/shard_map/pack/pallas_call | solution.py:97
  72.5 0.0 collective-permute-done.15.refs_5_
  72.5 0.0 collective-permute-start.11
  72.5 1.6 %collective-permute-done.16.refs_6_ = bf16[2,8,8,1024]{3,2,1,0:T(8,128)(2,1)S(1)} collective-permute-done((bf16[2,8,8,1024]{3,2,1,0:T(8,128)(2,1)}, bf16[2,8,8,1024]{3,2,1,0:T(8,128)(2,1)S(1)}, u32[]{:S(2)}, u32[]{:S(2)}) %collective-permute-start.16) | collective-permute-done | bytes 262176 | tf_op jit(solution)/shard_map/ppermute | solution.py:396
  74.0 1.7 %collective-permute-start.19 = (bf16[2,8,8,1024]{3,2,1,0:T(8,128)(2,1)}, bf16[2,8,8,1024]{3,2,1,0:T(8,128)(2,1)S(1)}, u32[]{:S(2)}, u32[]{:S(2)}) collective-permute-start(bf16[2,8,8,1024]{3,2,1,0:T(8,128)(2,1)} %get-tuple-element.57), channel_id=1, source_target_pairs={{0,13},{1,12},{2,15},{3,14},{4,9},{5,8},{6,11},{7,10},{8,5},{9,4},... | collective-permute-start | bytes 786440 | tf_op jit(solution)/shard_map/ppermute | solution.py:396
  75.7 0.0 collective-permute-done.6.got
  75.7 0.4 collective-permute-start.20
  76.1 2.5 %fold.2 = (bf16[4,27,8,128]{3,2,1,0:T(8,128)(2,1)S(1)}, bf16[4,27,8,128]{3,2,1,0:T(8,128)(2,1)S(1)}) custom-call(bf16[8,27,8,128]{3,2,1,0:T(8,128)(2,1)S(1)} %get-tuple-element.37.keep, bf16[8,27,8,128]{3,2,1,0:T(8,128)(2,1)S(1)} %collective-permute-done.6.got), custom_call_target="tpu_custom_call" | custom-call | flops 884736 | bytes 1327104 | tf_op jit(solution)/shard_map/fold/pallas_call | solution.py:271
  78.6 1.9 %collective-permute-start.7 = (bf16[4,27,8,128]{3,2,1,0:T(8,128)(2,1)S(1)}, bf16[4,27,8,128]{3,2,1,0:T(8,128)(2,1)S(1)}, u32[]{:S(2)}, u32[]{:S(2)}) collective-permute-start(bf16[4,27,8,128]{3,2,1,0:T(8,128)(2,1)S(1)} %get-tuple-element.40), channel_id=1, source_target_pairs={{0,2},{1,3},{2,0},{3,1},{4,6},{5,7},{6,4},{7,5},{8,10},{9,11},{10,... | collective-permute-start | bytes 663560 | tf_op jit(solution)/shard_map/ppermute | solution.py:396
  80.5 3.8 %collective-permute-done.18.refs_8_ = bf16[2,8,8,1024]{3,2,1,0:T(8,128)(2,1)S(1)} collective-permute-done((bf16[2,8,8,1024]{3,2,1,0:T(8,128)(2,1)}, bf16[2,8,8,1024]{3,2,1,0:T(8,128)(2,1)S(1)}, u32[]{:S(2)}, u32[]{:S(2)}) %collective-permute-start.18) | collective-permute-done | bytes 262176 | tf_op jit(solution)/shard_map/ppermute | solution.py:396
  84.4 0.0 collective-permute-start.21
  84.4 9.7 %collective-permute-done.11.refs_1_ = bf16[2,8,8,1024]{3,2,1,0:T(8,128)(2,1)S(1)} collective-permute-done((bf16[2,8,8,1024]{3,2,1,0:T(8,128)(2,1)}, bf16[2,8,8,1024]{3,2,1,0:T(8,128)(2,1)S(1)}, u32[]{:S(2)}, u32[]{:S(2)}) %collective-permute-start.11) | collective-permute-done | bytes 262176 | tf_op jit(solution)/shard_map/ppermute | solution.py:396
  94.1 0.8 collective-permute-start.22
  94.9 2.9 %collective-permute-done.20.refs_3_ = bf16[2,8,8,1024]{3,2,1,0:T(8,128)(2,1)S(1)} collective-permute-done((bf16[2,8,8,1024]{3,2,1,0:T(8,128)(2,1)}, bf16[2,8,8,1024]{3,2,1,0:T(8,128)(2,1)S(1)}, u32[]{:S(2)}, u32[]{:S(2)}) %collective-permute-start.20) | collective-permute-done | bytes 262176 | tf_op jit(solution)/shard_map/ppermute | solution.py:396
  97.8 1.4 %collective-permute-start.24 = (bf16[2,8,8,1024]{3,2,1,0:T(8,128)(2,1)}, bf16[2,8,8,1024]{3,2,1,0:T(8,128)(2,1)S(1)}, u32[]{:S(2)}, u32[]{:S(2)}) collective-permute-start(bf16[2,8,8,1024]{3,2,1,0:T(8,128)(2,1)} %get-tuple-element.64), channel_id=1, source_target_pairs={{0,14},{1,15},{2,12},{3,13},{4,10},{5,11},{6,8},{7,9},{8,6},{9,7},... | collective-permute-start | bytes 786440 | tf_op jit(solution)/shard_map/ppermute | solution.py:396
  99.2 3.2 %collective-permute-start.25 = (bf16[2,8,8,1024]{3,2,1,0:T(8,128)(2,1)}, bf16[2,8,8,1024]{3,2,1,0:T(8,128)(2,1)S(1)}, u32[]{:S(2)}, u32[]{:S(2)}) collective-permute-start(bf16[2,8,8,1024]{3,2,1,0:T(8,128)(2,1)} %get-tuple-element.65), channel_id=1, source_target_pairs={{0,15},{1,14},{2,13},{3,12},{4,11},{5,10},{6,9},{7,8},{8,7},{9,6},... | collective-permute-start | bytes 786440 | tf_op jit(solution)/shard_map/ppermute | solution.py:396
  102.4 1.2 fold.3
  103.6 0.0 collective-permute-done.21.refs_4_
  103.6 1.9 %collective-permute-start.10 = (bf16[27,8,128]{2,1,0:T(8,128)(2,1)S(1)}, bf16[27,8,128]{2,1,0:T(8,128)(2,1)S(1)}, u32[]{:S(2)}, u32[]{:S(2)}) collective-permute-start(bf16[27,8,128]{2,1,0:T(8,128)(2,1)S(1)} %get-tuple-element.44), channel_id=1, source_target_pairs={{0,12},{1,13},{2,14},{3,15},{4,8},{5,9},{6,10},{7,11},{8,4},{9,5},... | collective-permute-start | bytes 165896 | tf_op jit(solution)/shard_map/ppermute | solution.py:396
  105.5 9.6 %collective-permute-done.22.refs_5_ = bf16[2,8,8,1024]{3,2,1,0:T(8,128)(2,1)S(1)} collective-permute-done((bf16[2,8,8,1024]{3,2,1,0:T(8,128)(2,1)}, bf16[2,8,8,1024]{3,2,1,0:T(8,128)(2,1)S(1)}, u32[]{:S(2)}, u32[]{:S(2)}) %collective-permute-start.22) | collective-permute-done | bytes 262176 | tf_op jit(solution)/shard_map/ppermute | solution.py:396
  115.1 5.8 %collective-permute-done.23.refs_6_ = bf16[2,8,8,1024]{3,2,1,0:T(8,128)(2,1)S(1)} collective-permute-done((bf16[2,8,8,1024]{3,2,1,0:T(8,128)(2,1)}, bf16[2,8,8,1024]{3,2,1,0:T(8,128)(2,1)S(1)}, u32[]{:S(2)}, u32[]{:S(2)}) %collective-permute-start.23) | collective-permute-done | bytes 262176 | tf_op jit(solution)/shard_map/ppermute | solution.py:396
  120.8 1.5 %settle.3 = (bf16[16,8,8,1024]{3,2,1,0:T(8,128)(2,1)}, bf16[16,8,8,1024]{3,2,1,0:T(8,128)(2,1)}) custom-call(bf16[2,8,8,1024]{3,2,1,0:T(8,128)(2,1)S(1)} %copy-done.3, bf16[2,8,8,1024]{3,2,1,0:T(8,128)(2,1)S(1)} %collective-permute-done.11.refs_1_, bf16[2,8,8,1024]{3,2,1,0:T(8,128)(2,1)S(1)} %collective-permute-done.12.refs_2_, ...), custom_call_target="tpu_custom_call" | custom-call | bytes 4718592 | tf_op jit(solution)/shard_map/settle/pallas_call | solution.py:306
  122.4 1.1 settle.4
  123.5 0.0 collective-permute-done.24.refs_2_
  123.6 0.0 copy-start.4
  123.6 0.0 copy-start.5
  123.6 0.8 settle.5
  124.4 0.6 reshape.57
  125.0 0.0 collective-permute-done.10.refs_3_
  125.0 0.0 collective-permute-done.8.refs_1_
  125.0 5.0 %collective-permute-done.9.refs_2_ = bf16[27,8,128]{2,1,0:T(8,128)(2,1)S(1)} collective-permute-done((bf16[27,8,128]{2,1,0:T(8,128)(2,1)S(1)}, bf16[27,8,128]{2,1,0:T(8,128)(2,1)S(1)}, u32[]{:S(2)}, u32[]{:S(2)}) %collective-permute-start.9) | collective-permute-done | bytes 55328 | tf_op jit(solution)/shard_map/ppermute | solution.py:396
  130.0 1.1 merge.1
  (24 shorter events, 0.1 us)
Async XLA Ops:
  0.6 31.3 %copy-start = (bf16[512,1024]{1,0:T(8,128)(2,1)S(1)}, bf16[512,1024]{1,0:T(8,128)(2,1)}, u32[]{:S(2)}) copy-start(bf16[512,1024]{1,0:T(8,128)(2,1)} %refs_4_.1) | copy-start | bytes 3145732
  0.6 31.3 %copy-start.1 = (bf16[512,1024]{1,0:T(8,128)(2,1)S(1)}, bf16[512,1024]{1,0:T(8,128)(2,1)}, u32[]{:S(2)}) copy-start(bf16[512,1024]{1,0:T(8,128)(2,1)} %refs_5_.1) | copy-start | bytes 3145732
  0.7 31.3 %copy-start.6 = (s32[16]{0:T(128)S(1)}, s32[16]{0:T(128)}, u32[]{:S(2)}) copy-start(s32[16]{0:T(128)} %counts.5) | copy-start | bytes 196
  2.9 5.6 %collective-permute-start = (bf16[25,8,128]{2,1,0:T(8,128)(2,1)}, bf16[25,8,128]{2,1,0:T(8,128)(2,1)S(1)}, u32[]{:S(2)}, u32[]{:S(2)}) collective-permute-start(bf16[25,8,128]{2,1,0:T(8,128)(2,1)} %message.1), channel_id=1, source_target_pairs={{0,4},{1,5},{2,6},{3,7},{4,0},{5,1},{6,2},{7,3},{8,12},{9,13},{10,... | collective-permute-start | bytes 153608 | tf_op jit(solution)/shard_map/ppermute | solution.py:396
  6.0 6.2 %collective-permute-start.1 = (bf16[25,8,128]{2,1,0:T(8,128)(2,1)}, bf16[25,8,128]{2,1,0:T(8,128)(2,1)S(1)}, u32[]{:S(2)}, u32[]{:S(2)}) collective-permute-start(bf16[25,8,128]{2,1,0:T(8,128)(2,1)} %message.1), channel_id=1, source_target_pairs={{0,8},{1,9},{2,10},{3,11},{4,12},{5,13},{6,14},{7,15},{8,0},{9,1},... | collective-permute-start | bytes 153608 | tf_op jit(solution)/shard_map/ppermute | solution.py:396
  8.6 6.1 %collective-permute-start.2 = (bf16[25,8,128]{2,1,0:T(8,128)(2,1)}, bf16[25,8,128]{2,1,0:T(8,128)(2,1)S(1)}, u32[]{:S(2)}, u32[]{:S(2)}) collective-permute-start(bf16[25,8,128]{2,1,0:T(8,128)(2,1)} %message.1), channel_id=1, source_target_pairs={{0,12},{1,13},{2,14},{3,15},{4,8},{5,9},{6,10},{7,11},{8,4},{9,5},... | collective-permute-start | bytes 153608 | tf_op jit(solution)/shard_map/ppermute | solution.py:396
  15.5 5.8 %collective-permute-start.4 = (bf16[100,8,128]{2,1,0:T(8,128)(2,1)S(1)}, bf16[100,8,128]{2,1,0:T(8,128)(2,1)S(1)}, u32[]{:S(2)}, u32[]{:S(2)}) collective-permute-start(bf16[100,8,128]{2,1,0:T(8,128)(2,1)S(1)} %pad_maximum_fusion.refs_0_), channel_id=1, source_target_pairs={{0,2},{1,3},{2,0},{3,1},{4,6},{5,7},{6,4},{7,5},{8,10},{9,11},{10,... | collective-permute-start | bytes 614408 | tf_op jit(solution)/shard_map/ppermute | solution.py:396
  17.1 13.4 %collective-permute-start.3 = (bf16[100,8,128]{2,1,0:T(8,128)(2,1)S(1)}, bf16[100,8,128]{2,1,0:T(8,128)(2,1)S(1)}, u32[]{:S(2)}, u32[]{:S(2)}) collective-permute-start(bf16[100,8,128]{2,1,0:T(8,128)(2,1)S(1)} %pad_maximum_fusion.refs_0_), channel_id=1, source_target_pairs={{0,1},{1,0},{2,3},{3,2},{4,5},{5,4},{6,7},{7,6},{8,9},{9,8},{10,11... | collective-permute-start | bytes 614408 | tf_op jit(solution)/shard_map/ppermute | solution.py:396
  21.4 9.9 %collective-permute-start.5 = (bf16[100,8,128]{2,1,0:T(8,128)(2,1)S(1)}, bf16[100,8,128]{2,1,0:T(8,128)(2,1)S(1)}, u32[]{:S(2)}, u32[]{:S(2)}) collective-permute-start(bf16[100,8,128]{2,1,0:T(8,128)(2,1)S(1)} %collective-permute-done.4.refs_2_), channel_id=1, source_target_pairs={{0,1},{1,0},{2,3},{3,2},{4,5},{5,4},{6,7},{7,6},{8,9},{9,8},{10,11... | collective-permute-start | bytes 614408 | tf_op jit(solution)/shard_map/ppermute | solution.py:396
  26.3 25.1 %collective-permute-start.12 = (bf16[2,8,8,1024]{3,2,1,0:T(8,128)(2,1)}, bf16[2,8,8,1024]{3,2,1,0:T(8,128)(2,1)S(1)}, u32[]{:S(2)}, u32[]{:S(2)}) collective-permute-start(bf16[2,8,8,1024]{3,2,1,0:T(8,128)(2,1)} %get-tuple-element.48), channel_id=1, source_target_pairs={{0,9},{1,8},{2,11},{3,10},{4,13},{5,12},{6,15},{7,14},{8,1},{9,0},... | collective-permute-start | bytes 786440 | tf_op jit(solution)/shard_map/ppermute | solution.py:396
  27.1 31.4 %collective-permute-start.13 = (bf16[2,8,8,1024]{3,2,1,0:T(8,128)(2,1)}, bf16[2,8,8,1024]{3,2,1,0:T(8,128)(2,1)S(1)}, u32[]{:S(2)}, u32[]{:S(2)}) collective-permute-start(bf16[2,8,8,1024]{3,2,1,0:T(8,128)(2,1)} %get-tuple-element.49), channel_id=1, source_target_pairs={{0,10},{1,11},{2,8},{3,9},{4,14},{5,15},{6,12},{7,13},{8,2},{9,3},... | collective-permute-start | bytes 786440 | tf_op jit(solution)/shard_map/ppermute | solution.py:396
  30.5 0.7 copy-start.7
  31.2 0.7 copy-start.9
  31.9 0.9 copy-start.8
  32.8 0.9 copy-start.10
  33.8 8.3 %copy-start.11 = (bf16[2,8,8,1024]{3,2,1,0:T(8,128)(2,1)S(1)}, bf16[2,8,8,1024]{3,2,1,0:T(8,128)(2,1)}, u32[]{:S(2)}) copy-start(bf16[2,8,8,1024]{3,2,1,0:T(8,128)(2,1)} %get-tuple-element.50) | copy-start | bytes 786436
  42.0 78.8 %copy-start.3 = (bf16[2,8,8,1024]{3,2,1,0:T(8,128)(2,1)S(1)}, bf16[2,8,8,1024]{3,2,1,0:T(8,128)(2,1)}, u32[]{:S(2)}) copy-start(bf16[2,8,8,1024]{3,2,1,0:T(8,128)(2,1)} %get-tuple-element.47.refs_0_) | copy-start | bytes 786436
  42.0 33.7 %collective-permute-start.6 = (bf16[8,27,8,128]{3,2,1,0:T(8,128)(2,1)}, bf16[8,27,8,128]{3,2,1,0:T(8,128)(2,1)S(1)}, u32[]{:S(2)}, u32[]{:S(2)}) collective-permute-start(bf16[8,27,8,128]{3,2,1,0:T(8,128)(2,1)} %get-tuple-element.38), channel_id=1, source_target_pairs={{0,1},{1,0},{2,3},{3,2},{4,5},{5,4},{6,7},{7,6},{8,9},{9,8},{10,11... | collective-permute-start | bytes 1327112 | tf_op jit(solution)/shard_map/ppermute | solution.py:396
  42.1 27.5 %collective-permute-start.14 = (bf16[2,8,8,1024]{3,2,1,0:T(8,128)(2,1)S(1)}, bf16[2,8,8,1024]{3,2,1,0:T(8,128)(2,1)S(1)}, u32[]{:S(2)}, u32[]{:S(2)}) collective-permute-start(bf16[2,8,8,1024]{3,2,1,0:T(8,128)(2,1)S(1)} %copy-done.11), channel_id=1, source_target_pairs={{0,11},{1,10},{2,9},{3,8},{4,15},{5,14},{6,13},{7,12},{8,3},{9,2},... | collective-permute-start | bytes 786440 | tf_op jit(solution)/shard_map/ppermute | solution.py:396
  42.6 29.9 %collective-permute-start.15 = (bf16[2,8,8,1024]{3,2,1,0:T(8,128)(2,1)}, bf16[2,8,8,1024]{3,2,1,0:T(8,128)(2,1)S(1)}, u32[]{:S(2)}, u32[]{:S(2)}) collective-permute-start(bf16[2,8,8,1024]{3,2,1,0:T(8,128)(2,1)} %get-tuple-element.51), channel_id=1, source_target_pairs={{0,4},{1,5},{2,6},{3,7},{4,0},{5,1},{6,2},{7,3},{8,12},{9,13},{10,... | collective-permute-start | bytes 786440 | tf_op jit(solution)/shard_map/ppermute | solution.py:396
  51.4 22.6 %collective-permute-start.16 = (bf16[2,8,8,1024]{3,2,1,0:T(8,128)(2,1)}, bf16[2,8,8,1024]{3,2,1,0:T(8,128)(2,1)S(1)}, u32[]{:S(2)}, u32[]{:S(2)}) collective-permute-start(bf16[2,8,8,1024]{3,2,1,0:T(8,128)(2,1)} %get-tuple-element.52), channel_id=1, source_target_pairs={{0,5},{1,4},{2,7},{3,6},{4,1},{5,0},{6,3},{7,2},{8,13},{9,12},{10,... | collective-permute-start | bytes 786440 | tf_op jit(solution)/shard_map/ppermute | solution.py:396
  58.5 20.1 %collective-permute-start.17 = (bf16[2,8,8,1024]{3,2,1,0:T(8,128)(2,1)}, bf16[2,8,8,1024]{3,2,1,0:T(8,128)(2,1)S(1)}, u32[]{:S(2)}, u32[]{:S(2)}) collective-permute-start(bf16[2,8,8,1024]{3,2,1,0:T(8,128)(2,1)} %get-tuple-element.53), channel_id=1, source_target_pairs={{0,12},{1,13},{2,14},{3,15},{4,8},{5,9},{6,10},{7,11},{8,4},{9,5},... | collective-permute-start | bytes 786440 | tf_op jit(solution)/shard_map/ppermute | solution.py:396
  69.6 14.8 %collective-permute-start.18 = (bf16[2,8,8,1024]{3,2,1,0:T(8,128)(2,1)}, bf16[2,8,8,1024]{3,2,1,0:T(8,128)(2,1)S(1)}, u32[]{:S(2)}, u32[]{:S(2)}) collective-permute-start(bf16[2,8,8,1024]{3,2,1,0:T(8,128)(2,1)} %get-tuple-element.54), channel_id=1, source_target_pairs={{0,6},{1,7},{2,4},{3,5},{4,2},{5,3},{6,0},{7,1},{8,14},{9,15},{10,... | collective-permute-start | bytes 786440 | tf_op jit(solution)/shard_map/ppermute | solution.py:396
  72.5 21.6 %collective-permute-start.11 = (bf16[2,8,8,1024]{3,2,1,0:T(8,128)(2,1)}, bf16[2,8,8,1024]{3,2,1,0:T(8,128)(2,1)S(1)}, u32[]{:S(2)}, u32[]{:S(2)}) collective-permute-start(bf16[2,8,8,1024]{3,2,1,0:T(8,128)(2,1)} %pack.3), channel_id=1, source_target_pairs={{0,8},{1,9},{2,10},{3,11},{4,12},{5,13},{6,14},{7,15},{8,0},{9,1},... | collective-permute-start | bytes 786440 | tf_op jit(solution)/shard_map/ppermute | solution.py:396
  74.0 20.9 %collective-permute-start.19 = (bf16[2,8,8,1024]{3,2,1,0:T(8,128)(2,1)}, bf16[2,8,8,1024]{3,2,1,0:T(8,128)(2,1)S(1)}, u32[]{:S(2)}, u32[]{:S(2)}) collective-permute-start(bf16[2,8,8,1024]{3,2,1,0:T(8,128)(2,1)} %get-tuple-element.57), channel_id=1, source_target_pairs={{0,13},{1,12},{2,15},{3,14},{4,9},{5,8},{6,11},{7,10},{8,5},{9,4},... | collective-permute-start | bytes 786440 | tf_op jit(solution)/shard_map/ppermute | solution.py:396
  75.7 22.1 %collective-permute-start.20 = (bf16[2,8,8,1024]{3,2,1,0:T(8,128)(2,1)}, bf16[2,8,8,1024]{3,2,1,0:T(8,128)(2,1)S(1)}, u32[]{:S(2)}, u32[]{:S(2)}) collective-permute-start(bf16[2,8,8,1024]{3,2,1,0:T(8,128)(2,1)} %get-tuple-element.58), channel_id=1, source_target_pairs={{0,7},{1,6},{2,5},{3,4},{4,3},{5,2},{6,1},{7,0},{8,15},{9,14},{10,... | collective-permute-start | bytes 786440 | tf_op jit(solution)/shard_map/ppermute | solution.py:396
  78.6 20.6 %collective-permute-start.7 = (bf16[4,27,8,128]{3,2,1,0:T(8,128)(2,1)S(1)}, bf16[4,27,8,128]{3,2,1,0:T(8,128)(2,1)S(1)}, u32[]{:S(2)}, u32[]{:S(2)}) collective-permute-start(bf16[4,27,8,128]{3,2,1,0:T(8,128)(2,1)S(1)} %get-tuple-element.40), channel_id=1, source_target_pairs={{0,2},{1,3},{2,0},{3,1},{4,6},{5,7},{6,4},{7,5},{8,10},{9,11},{10,... | collective-permute-start | bytes 663560 | tf_op jit(solution)/shard_map/ppermute | solution.py:396
  84.4 19.2 %collective-permute-start.21 = (bf16[2,8,8,1024]{3,2,1,0:T(8,128)(2,1)}, bf16[2,8,8,1024]{3,2,1,0:T(8,128)(2,1)S(1)}, u32[]{:S(2)}, u32[]{:S(2)}) collective-permute-start(bf16[2,8,8,1024]{3,2,1,0:T(8,128)(2,1)} %get-tuple-element.59), channel_id=1, source_target_pairs={{0,1},{1,0},{2,3},{3,2},{4,5},{5,4},{6,7},{7,6},{8,9},{9,8},{10,11... | collective-permute-start | bytes 786440 | tf_op jit(solution)/shard_map/ppermute | solution.py:396
  94.1 21.0 %collective-permute-start.22 = (bf16[2,8,8,1024]{3,2,1,0:T(8,128)(2,1)}, bf16[2,8,8,1024]{3,2,1,0:T(8,128)(2,1)S(1)}, u32[]{:S(2)}, u32[]{:S(2)}) collective-permute-start(bf16[2,8,8,1024]{3,2,1,0:T(8,128)(2,1)} %get-tuple-element.60), channel_id=1, source_target_pairs={{0,2},{1,3},{2,0},{3,1},{4,6},{5,7},{6,4},{7,5},{8,10},{9,11},{10,... | collective-permute-start | bytes 786440 | tf_op jit(solution)/shard_map/ppermute | solution.py:396
  94.9 25.9 %collective-permute-start.23 = (bf16[2,8,8,1024]{3,2,1,0:T(8,128)(2,1)}, bf16[2,8,8,1024]{3,2,1,0:T(8,128)(2,1)S(1)}, u32[]{:S(2)}, u32[]{:S(2)}) collective-permute-start(bf16[2,8,8,1024]{3,2,1,0:T(8,128)(2,1)} %get-tuple-element.61), channel_id=1, source_target_pairs={{0,3},{1,2},{2,1},{3,0},{4,7},{5,6},{6,5},{7,4},{8,11},{9,10},{10,... | collective-permute-start | bytes 786440 | tf_op jit(solution)/shard_map/ppermute | solution.py:396
  97.8 25.7 %collective-permute-start.24 = (bf16[2,8,8,1024]{3,2,1,0:T(8,128)(2,1)}, bf16[2,8,8,1024]{3,2,1,0:T(8,128)(2,1)S(1)}, u32[]{:S(2)}, u32[]{:S(2)}) collective-permute-start(bf16[2,8,8,1024]{3,2,1,0:T(8,128)(2,1)} %get-tuple-element.64), channel_id=1, source_target_pairs={{0,14},{1,15},{2,12},{3,13},{4,10},{5,11},{6,8},{7,9},{8,6},{9,7},... | collective-permute-start | bytes 786440 | tf_op jit(solution)/shard_map/ppermute | solution.py:396
  99.2 24.3 %collective-permute-start.25 = (bf16[2,8,8,1024]{3,2,1,0:T(8,128)(2,1)}, bf16[2,8,8,1024]{3,2,1,0:T(8,128)(2,1)S(1)}, u32[]{:S(2)}, u32[]{:S(2)}) collective-permute-start(bf16[2,8,8,1024]{3,2,1,0:T(8,128)(2,1)} %get-tuple-element.65), channel_id=1, source_target_pairs={{0,15},{1,14},{2,13},{3,12},{4,11},{5,10},{6,9},{7,8},{8,7},{9,6},... | collective-permute-start | bytes 786440 | tf_op jit(solution)/shard_map/ppermute | solution.py:396
  103.6 21.4 %collective-permute-start.10 = (bf16[27,8,128]{2,1,0:T(8,128)(2,1)S(1)}, bf16[27,8,128]{2,1,0:T(8,128)(2,1)S(1)}, u32[]{:S(2)}, u32[]{:S(2)}) collective-permute-start(bf16[27,8,128]{2,1,0:T(8,128)(2,1)S(1)} %get-tuple-element.44), channel_id=1, source_target_pairs={{0,12},{1,13},{2,14},{3,15},{4,8},{5,9},{6,10},{7,11},{8,4},{9,5},... | collective-permute-start | bytes 165896 | tf_op jit(solution)/shard_map/ppermute | solution.py:396
  115.0 10.0 %collective-permute-start.8 = (bf16[27,8,128]{2,1,0:T(8,128)(2,1)S(1)}, bf16[27,8,128]{2,1,0:T(8,128)(2,1)S(1)}, u32[]{:S(2)}, u32[]{:S(2)}) collective-permute-start(bf16[27,8,128]{2,1,0:T(8,128)(2,1)S(1)} %get-tuple-element.42), channel_id=1, source_target_pairs={{0,4},{1,5},{2,6},{3,7},{4,0},{5,1},{6,2},{7,3},{8,12},{9,13},{10,... | collective-permute-start | bytes 165896 | tf_op jit(solution)/shard_map/ppermute | solution.py:396
  120.8 9.2 %collective-permute-start.9 = (bf16[27,8,128]{2,1,0:T(8,128)(2,1)S(1)}, bf16[27,8,128]{2,1,0:T(8,128)(2,1)S(1)}, u32[]{:S(2)}, u32[]{:S(2)}) collective-permute-start(bf16[27,8,128]{2,1,0:T(8,128)(2,1)S(1)} %get-tuple-element.43), channel_id=1, source_target_pairs={{0,8},{1,9},{2,10},{3,11},{4,12},{5,13},{6,14},{7,15},{8,0},{9,1},... | collective-permute-start | bytes 165896 | tf_op jit(solution)/shard_map/ppermute | solution.py:396
  123.5 6.5 %copy-start.2 = (bf16[25,8,128]{2,1,0:T(8,128)(2,1)S(1)}, bf16[25,8,128]{2,1,0:T(8,128)(2,1)}, u32[]{:S(2)}) copy-start(bf16[25,8,128]{2,1,0:T(8,128)(2,1)} %message.1) | copy-start | bytes 153604
  123.6 6.5 %copy-start.4 = (bf16[1,2,1024]{2,1,0:T(2,128)(2,1)S(1)}, bf16[1,2,1024]{2,1,0:T(2,128)(2,1)}, u32[]{:S(2)}) copy-start(bf16[1,2,1024]{2,1,0:T(2,128)(2,1)} %param.15) | copy-start | bytes 12292
  123.6 6.5 %copy-start.5 = (bf16[1,2,1024]{2,1,0:T(2,128)(2,1)S(1)}, bf16[1,2,1024]{2,1,0:T(2,128)(2,1)}, u32[]{:S(2)}) copy-start(bf16[1,2,1024]{2,1,0:T(2,128)(2,1)} %param.16) | copy-start | bytes 12292
